TPU v7x, 1024 devices: a whole 4x8x16 slice. The times are simulated.
1024 devices in a mesh: gx: 8 (over y), gy: 4 (over x), gz: 32 (over z, core).
Axes of the slice: x: 4, y: 8, z: 16, core: 2. Of those that a mesh axis runs over, the one named last changes fastest.
Arguments:
- adjoint_state: float32 [3, 64, 64, 4096], P(None, 'gx', 'gy', 'gz'), may hold values from -20 to 20
- base_flow: bfloat16 [3, 64, 64, 4096], P(None, 'gx', 'gy', 'gz'), may hold values from -4 to 4
- base_grads: bfloat16 [9, 64, 64, 4096], P(None, 'gx', 'gy', 'gz'), may hold values from -3 to 3
- sponge: float32 [64, 64, 4096], P('gx', 'gy', 'gz'), may hold values from 0.5 to 8
Outputs:
- solution: float32 [3, 64, 64, 4096], P(None, 'gx', 'gy', 'gz')
All inputs are finite; a program needn't handle non-finite values.
Results may differ from a plain program's by a relative error of at most 0.0004.
Values sent between devices are 32-bit elements; how exact they have to be, the bound alone decides.
No kernel may reach another device: no remote copies, remote signals or barrier semaphores. Data moves between devices by JAX's collectives and lax.ppermute only.
A program may use at most 32 MiB of HBM per device.

v0:
```python
import jax
import jax.numpy as jnp
import numpy as np
from jax import lax
from jax.sharding import PartitionSpec as P

ITERS = 2


inverse_step = 2.0
viscosity = 0.05


def with_halo(cells, sides, width):
    for axis, dim in sides:
        count = lax.axis_size(axis)
        ends = count - 1
        head = lax.slice_in_dim(cells, 0, width, axis=dim)
        tail = lax.slice_in_dim(cells, cells.shape[dim] - width, cells.shape[dim], axis=dim)
        cells = jnp.concatenate(
            [
                lax.ppermute(tail, axis, [(i, (i + 1) % count) for i in range(ends)]),
                cells,
                lax.ppermute(head, axis, [((i + 1) % count, i) for i in range(ends)]),
            ],
            axis=dim,
        )
    return cells


def gll_tables():
    degree = 7
    interior = np.array(
        [
            -0.8717401485096066,
            -0.5917001814331423,
            -0.2092992179024789,
            0.2092992179024789,
            0.5917001814331423,
            0.8717401485096066,
        ]
    )
    points = np.concatenate([[-1.0], interior, [1.0]])
    previous = np.ones(8)
    current = points * 1.0
    for degree_now in range(1, degree):
        following = ((2 * degree_now + 1) * points * current - degree_now * previous) / (
            degree_now + 1
        )
        previous = current
        current = following
    weights = 2.0 / (degree * (degree + 1) * current**2)
    matrix = np.zeros((8, 8))
    for row_idx in range(8):
        for col_idx in range(8):
            if row_idx != col_idx:
                matrix[row_idx, col_idx] = current[row_idx] / (
                    current[col_idx] * (points[row_idx] - points[col_idx])
                )
    matrix[0, 0] = -degree * (degree + 1) / 4.0
    matrix[7, 7] = degree * (degree + 1) / 4.0
    return (weights, matrix)


def grad_x(field, matrix):
    dims_all = field.shape
    lead = dims_all[:-3]
    blocks = field.reshape(lead + (dims_all[-3] // 8, 8, dims_all[-2], dims_all[-1]))
    return jnp.einsum(
        "ab,...ebyz->...eayz", matrix, blocks, precision=lax.Precision.HIGHEST
    ).reshape(dims_all)


def grad_y(field, matrix):
    dims_all = field.shape
    lead = dims_all[:-3]
    blocks = field.reshape(lead + (dims_all[-3], dims_all[-2] // 8, 8, dims_all[-1]))
    return jnp.einsum(
        "ab,...xebz->...xeaz", matrix, blocks, precision=lax.Precision.HIGHEST
    ).reshape(dims_all)


def grad_z(field, matrix):
    dims_all = field.shape
    lead = dims_all[:-3]
    blocks = field.reshape(lead + (dims_all[-3], dims_all[-2], dims_all[-1] // 8, 8))
    return jnp.einsum(
        "ab,...xyeb->...xyea", matrix, blocks, precision=lax.Precision.HIGHEST
    ).reshape(dims_all)


def twin_pass(extended, axis):
    count = extended.shape[axis] - 2
    middle = lax.slice_in_dim(extended, 1, count + 1, axis=axis)
    after = lax.slice_in_dim(extended, 2, count + 2, axis=axis)
    before = lax.slice_in_dim(extended, 0, count, axis=axis)
    position = jnp.arange(count) % 8
    bshape = (count,) + (1,) * (-axis - 1)
    upper = (position == 7).reshape(bshape)
    lower = (position == 0).reshape(bshape)
    return middle + jnp.where(upper, after, 0.0) + jnp.where(lower, before, 0.0)


def dim_factors(count, start, total):
    global_pos = start + jnp.arange(count)
    position = jnp.arange(count) % 8
    border = (global_pos == 0) | (global_pos == total - 1)
    keep_dim = jnp.where(border, 0.0, 1.0).astype(jnp.float32)
    twin = ((position == 0) | (position == 7)) & jnp.logical_not(border)
    share = jnp.where(twin, 0.5, 1.0).astype(jnp.float32)
    return (keep_dim, share)


def node_masks(sizes_xyz, starts, totals):
    keep_x, share_x = dim_factors(sizes_xyz[0], starts[0], totals[0])
    keep_y, share_y = dim_factors(sizes_xyz[1], starts[1], totals[1])
    keep_z, share_z = dim_factors(sizes_xyz[2], starts[2], totals[2])
    keep = keep_x[:, None, None] * keep_y[None, :, None] * keep_z[None, None, :]
    weight = keep * (share_x[:, None, None] * share_y[None, :, None] * share_z[None, None, :])
    return (keep, weight)


def mass_nodes(sizes_xyz, weights):
    mass_x = jnp.tile(weights, sizes_xyz[0] // 8)
    mass_y = jnp.tile(weights, sizes_xyz[1] // 8)
    mass_z = jnp.tile(weights, sizes_xyz[2] // 8)
    return mass_x[:, None, None] * mass_y[None, :, None] * mass_z[None, None, :]


def assemble(field):
    extended = with_halo(field, (("gx", 1), ("gy", 2), ("gz", 3)), 1)
    summed = twin_pass(extended, -3)
    summed = twin_pass(summed, -2)
    return twin_pass(summed, -1)


def body(adjoint_state, base_flow, base_grads, sponge):
    weights_np, matrix_np = gll_tables()
    weights = jnp.asarray(weights_np, jnp.float32)
    deriv = jnp.asarray(matrix_np, jnp.float32)
    deriv_t = jnp.asarray(matrix_np.T, jnp.float32)
    sizes_xyz = adjoint_state.shape[1:]
    starts = (
        lax.axis_index("gx") * sizes_xyz[0],
        lax.axis_index("gy") * sizes_xyz[1],
        lax.axis_index("gz") * sizes_xyz[2],
    )
    totals = (
        lax.axis_size("gx") * sizes_xyz[0],
        lax.axis_size("gy") * sizes_xyz[1],
        lax.axis_size("gz") * sizes_xyz[2],
    )
    mass3 = mass_nodes(sizes_xyz, weights)
    keep, weight = node_masks(sizes_xyz, starts, totals)
    flow = base_flow.astype(jnp.float32)
    grads = base_grads.astype(jnp.float32).reshape((3, 3) + tuple(sizes_xyz))
    sponge_term = mass3 * (inverse_step + sponge)
    transport = (
        flow[0] * grad_x(adjoint_state, deriv)
        + flow[1] * grad_y(adjoint_state, deriv)
        + flow[2] * grad_z(adjoint_state, deriv)
    )
    coupling = (
        grads[:, 0] * adjoint_state[0]
        + grads[:, 1] * adjoint_state[1]
        + grads[:, 2] * adjoint_state[2]
    )
    forcing = keep * assemble(mass3 * (inverse_step * adjoint_state + transport - coupling))

    def inner(left, right):
        return jnp.sum(weight * left * right)

    def squares(residual):
        return lax.psum(inner(residual, residual), ("gx", "gy", "gz"))

    solution = jnp.zeros_like(forcing)
    residual = forcing
    direction = forcing
    norm_now = squares(residual)
    for step in range(ITERS):
        stiff = grad_x(mass3 * grad_x(direction, deriv), deriv_t) + grad_y(
            mass3 * grad_y(direction, deriv), deriv_t
        )
        stiff = stiff + grad_z(mass3 * grad_z(direction, deriv), deriv_t)
        image = keep * assemble(sponge_term * direction + viscosity * stiff)
        alpha = norm_now / lax.psum(inner(direction, image), ("gx", "gy", "gz"))
        solution = solution + alpha * direction
        if step + 1 < ITERS:
            residual = residual - alpha * image
            norm_next = squares(residual)
            direction = residual + norm_next / norm_now * direction
            norm_now = norm_next
    return solution


def solution(mesh):
    placed = (
        P(None, "gx", "gy", "gz"),
        P(None, "gx", "gy", "gz"),
        P(None, "gx", "gy", "gz"),
        P("gx", "gy", "gz"),
    )
    return jax.shard_map(
        body, mesh=mesh, in_specs=placed, out_specs=P(None, "gx", "gy", "gz"), check_vma=False
    )
```

profile of v0, /device:TPU:1, one launch (start us, length us, event | category | flops | bytes accessed | tf_op | source)
XLA Modules:
  0.0 508.2 jit_solution(15876089883354336077)
XLA Ops:
  12.9 4.0 collective-permute-start
  21.5 3.1 collective-permute-start.2
  26.0 3.2 collective-permute-done.3
  29.5 7.4 %collective-permute-start.4 = (f32[3,10,18,1]{3,1,2,0:T(8,128)S(1)}, f32[3,10,18,1]{3,1,2,0:T(8,128)S(1)}, u32[]{:S(2)}, u32[]{:S(2)}) collective-permute-start(f32[3,10,18,1]{3,1,2,0:T(8,128)S(1)} %get-tuple-element.14), channel_id=1, source_target_pairs={{0,1},{1,2},{2,3},{3,4},{4,5},{5,6},{6,7},{7,8},{8,9},{9,10},{10,1... | collective-permute-start | bytes 6488 | tf_op jit(solution)/shard_map/ppermute | solution.py:22
  36.9 7.9 %collective-permute-start.5 = (f32[3,10,18,1]{3,1,2,0:T(8,128)S(1)}, f32[3,10,18,1]{3,1,2,0:T(8,128)S(1)}, u32[]{:S(2)}, u32[]{:S(2)}) collective-permute-start(f32[3,10,18,1]{3,1,2,0:T(8,128)S(1)} %get-tuple-element.15), channel_id=1, source_target_pairs={{1,0},{2,1},{3,2},{4,3},{5,4},{6,5},{7,6},{8,7},{9,8},{10,9},{11,1... | collective-permute-start | bytes 6488 | tf_op jit(solution)/shard_map/ppermute | solution.py:24
  56.4 3.2 collective-permute-start.6
  60.9 3.9 collective-permute-done.7
  64.8 3.1 collective-permute-start.8
  69.3 3.3 collective-permute-done.9
  72.8 4.3 collective-permute-start.10
  79.1 3.3 collective-permute-done.10
  82.4 4.4 collective-permute-done.11
  89.2 131.4 %all-reduce = (f32[]{:T(128)}, f32[]{:T(128)}) all-reduce(f32[]{:T(128)} %get-tuple-element.6, f32[]{:T(128)} %get-tuple-element.5), channel_id=1, replica_groups=mesh['gx'=8,'gy'=4,'gz'=32] {'gx','gy','gz'}, use_global_device_ids=true, to_apply=%region_1.2 | all-reduce | flops 2 | bytes 16 | tf_op jit(solution)/shard_map/psum | solution.py:174
  222.7 117.5 %psum.30 = f32[]{:T(128)} all-reduce(f32[]{:T(128)} %fusion.34), channel_id=1, replica_groups=mesh['gx'=8,'gy'=4,'gz'=32] {'gx','gy','gz'}, use_global_device_ids=true, to_apply=%region_5.6 | all-reduce | flops 1 | bytes 8 | tf_op jit(solution)/shard_map/psum | solution.py:174
  344.2 2.8 convolution_multiply_fusion
  348.8 2.8 convolution_bitcast_fusion
  353.1 2.8 collective-permute-start.12
  357.2 5.0 collective-permute-done.13
  362.2 2.8 collective-permute-start.14
  366.4 3.3 collective-permute-done.15
  369.9 6.0 %collective-permute-start.16 = (f32[3,10,18,1]{3,1,2,0:T(8,128)S(1)}, f32[3,10,18,1]{3,1,2,0:T(8,128)S(1)}, u32[]{:S(2)}, u32[]{:S(2)}) collective-permute-start(f32[3,10,18,1]{3,1,2,0:T(8,128)S(1)} %get-tuple-element.10), channel_id=1, source_target_pairs={{0,1},{1,2},{2,3},{3,4},{4,5},{5,6},{6,7},{7,8},{8,9},{9,10},{10,1... | collective-permute-start | bytes 6488 | tf_op jit(solution)/shard_map/ppermute | solution.py:22
  377.9 3.3 collective-permute-done.16
  381.2 4.4 collective-permute-done.17
  387.2 118.8 %psum.31 = f32[]{:T(128)} all-reduce(f32[]{:T(128)} %fusion.38), channel_id=1, replica_groups=mesh['gx'=8,'gy'=4,'gz'=32] {'gx','gy','gz'}, use_global_device_ids=true, to_apply=%region_7.8 | all-reduce | flops 1 | bytes 8 | tf_op jit(solution)/shard_map/psum | solution.py:186
  (185 shorter events, 51.3 us)
Async XLA Ops:
  2.8 45.3 %copy-start.8 = (f32[8,16,128]{2,0,1:T(8,128)}, f32[8,16,128]{2,0,1:T(8,128)S(1)}, u32[]{:S(2)}) copy-start(f32[8,16,128]{2,0,1:T(8,128)S(1)} %copy.27) | copy-start | bytes 196612
  12.9 8.1 %collective-permute-start = (f32[3,1,16,128]{3,1,2,0:T(1,128)S(1)}, f32[3,1,16,128]{3,1,2,0:T(1,128)S(1)}, u32[]{:S(2)}, u32[]{:S(2)}) collective-permute-start(f32[3,1,16,128]{3,1,2,0:T(1,128)S(1)} %get-tuple-element.29), channel_id=1, source_target_pairs={{0,128},{128,256},{256,384},{384,512},{512,640},{640,768},{768,896... | collective-permute-start | bytes 73736 | tf_op jit(solution)/shard_map/ppermute | solution.py:22
  16.9 4.6 collective-permute-start.1
  20.9 26.5 %copy-start.3 = (f32[8,16,128]{2,0,1:T(8,128)}, f32[8,16,128]{2,0,1:T(8,128)S(1)}, u32[]{:S(2)}) copy-start(f32[8,16,128]{2,0,1:T(8,128)S(1)} %get-tuple-element.38) | copy-start | bytes 196612
  20.9 26.2 %copy-start.31 = (pred[8]{0:T(512)(128)(4,1)}, pred[8]{0:T(512)(128)(4,1)S(1)}, u32[]{:S(2)}) copy-start(pred[8]{0:T(512)(128)(4,1)S(1)} %get-tuple-element.41) | copy-start | bytes 28
  21.0 26.2 %copy-start.33 = (pred[8]{0:T(512)(128)(4,1)}, pred[8]{0:T(512)(128)(4,1)S(1)}, u32[]{:S(2)}) copy-start(pred[8]{0:T(512)(128)(4,1)S(1)} %get-tuple-element.42) | copy-start | bytes 28
  21.5 4.5 collective-permute-start.2
  24.6 4.6 collective-permute-start.3
  25.9 21.4 %copy-start.35 = (pred[16]{0:T(512)(128)(4,1)}, pred[16]{0:T(512)(128)(4,1)S(1)}, u32[]{:S(2)}) copy-start(pred[16]{0:T(512)(128)(4,1)S(1)} %get-tuple-element.43) | copy-start | bytes 52
  29.5 16.0 %collective-permute-start.4 = (f32[3,10,18,1]{3,1,2,0:T(8,128)S(1)}, f32[3,10,18,1]{3,1,2,0:T(8,128)S(1)}, u32[]{:S(2)}, u32[]{:S(2)}) collective-permute-start(f32[3,10,18,1]{3,1,2,0:T(8,128)S(1)} %get-tuple-element.14), channel_id=1, source_target_pairs={{0,1},{1,2},{2,3},{3,4},{4,5},{5,6},{6,7},{7,8},{8,9},{9,10},{10,1... | collective-permute-start | bytes 6488 | tf_op jit(solution)/shard_map/ppermute | solution.py:22
  36.9 9.6 %collective-permute-start.5 = (f32[3,10,18,1]{3,1,2,0:T(8,128)S(1)}, f32[3,10,18,1]{3,1,2,0:T(8,128)S(1)}, u32[]{:S(2)}, u32[]{:S(2)}) collective-permute-start(f32[3,10,18,1]{3,1,2,0:T(8,128)S(1)} %get-tuple-element.15), channel_id=1, source_target_pairs={{1,0},{2,1},{3,2},{4,3},{5,4},{6,5},{7,6},{8,7},{9,8},{10,9},{11,1... | collective-permute-start | bytes 6488 | tf_op jit(solution)/shard_map/ppermute | solution.py:24
  56.4 4.5 collective-permute-start.6
  59.6 5.2 %collective-permute-start.7 = (f32[3,1,16,128]{3,1,2,0:T(1,128)S(1)}, f32[3,1,16,128]{3,1,2,0:T(1,128)S(1)}, u32[]{:S(2)}, u32[]{:S(2)}) collective-permute-start(f32[3,1,16,128]{3,1,2,0:T(1,128)S(1)} %get-tuple-element.28), channel_id=1, source_target_pairs={{128,0},{256,128},{384,256},{512,384},{640,512},{768,640},{896,768... | collective-permute-start | bytes 73736 | tf_op jit(solution)/shard_map/ppermute | solution.py:24
  64.8 4.4 collective-permute-start.8
  68.0 4.6 collective-permute-start.9
  72.8 9.6 %collective-permute-start.10 = (f32[3,10,18,1]{3,1,2,0:T(8,128)S(1)}, f32[3,10,18,1]{3,1,2,0:T(8,128)S(1)}, u32[]{:S(2)}, u32[]{:S(2)}) collective-permute-start(f32[3,10,18,1]{3,1,2,0:T(8,128)S(1)} %get-tuple-element.12), channel_id=1, source_target_pairs={{0,1},{1,2},{2,3},{3,4},{4,5},{5,6},{6,7},{7,8},{8,9},{9,10},{10,1... | collective-permute-start | bytes 6488 | tf_op jit(solution)/shard_map/ppermute | solution.py:22
  77.2 9.6 %collective-permute-start.11 = (f32[3,10,18,1]{3,1,2,0:T(8,128)S(1)}, f32[3,10,18,1]{3,1,2,0:T(8,128)S(1)}, u32[]{:S(2)}, u32[]{:S(2)}) collective-permute-start(f32[3,10,18,1]{3,1,2,0:T(8,128)S(1)} %get-tuple-element.13), channel_id=1, source_target_pairs={{1,0},{2,1},{3,2},{4,3},{5,4},{6,5},{7,6},{8,7},{9,8},{10,9},{11,1... | collective-permute-start | bytes 6488 | tf_op jit(solution)/shard_map/ppermute | solution.py:24
  222.7 119.4 %copy-start.9 = (f32[8,16,128]{2,0,1:T(8,128)S(1)}, f32[8,16,128]{2,0,1:T(8,128)}, u32[]{:S(2)}) copy-start(f32[8,16,128]{2,0,1:T(8,128)} %copy-done.8) | copy-start | bytes 196612
  353.1 4.1 collective-permute-start.12
  355.9 6.3 %collective-permute-start.13 = (f32[3,1,16,128]{3,1,2,0:T(1,128)S(1)}, f32[3,1,16,128]{3,1,2,0:T(1,128)S(1)}, u32[]{:S(2)}, u32[]{:S(2)}) collective-permute-start(f32[3,1,16,128]{3,1,2,0:T(1,128)S(1)} %get-tuple-element.26), channel_id=1, source_target_pairs={{128,0},{256,128},{384,256},{512,384},{640,512},{768,640},{896,768... | collective-permute-start | bytes 73736 | tf_op jit(solution)/shard_map/ppermute | solution.py:24
  362.2 4.1 collective-permute-start.14
  365.1 4.6 collective-permute-start.15
  369.9 11.3 %collective-permute-start.16 = (f32[3,10,18,1]{3,1,2,0:T(8,128)S(1)}, f32[3,10,18,1]{3,1,2,0:T(8,128)S(1)}, u32[]{:S(2)}, u32[]{:S(2)}) collective-permute-start(f32[3,10,18,1]{3,1,2,0:T(8,128)S(1)} %get-tuple-element.10), channel_id=1, source_target_pairs={{0,1},{1,2},{2,3},{3,4},{4,5},{5,6},{6,7},{7,8},{8,9},{9,10},{10,1... | collective-permute-start | bytes 6488 | tf_op jit(solution)/shard_map/ppermute | solution.py:22
  375.9 9.6 %collective-permute-start.17 = (f32[3,10,18,1]{3,1,2,0:T(8,128)S(1)}, f32[3,10,18,1]{3,1,2,0:T(8,128)S(1)}, u32[]{:S(2)}, u32[]{:S(2)}) collective-permute-start(f32[3,10,18,1]{3,1,2,0:T(8,128)S(1)} %get-tuple-element.11), channel_id=1, source_target_pairs={{1,0},{2,1},{3,2},{4,3},{5,4},{6,5},{7,6},{8,7},{9,8},{10,9},{11,1... | collective-permute-start | bytes 6488 | tf_op jit(solution)/shard_map/ppermute | solution.py:24
  (35 other events, 124.3 us)
where the time goes:
time: 515 us; the launch traced here: 508 us
  blocking collectives  368 us (71%)
  starting transfers between devices  56.3 us (11%)
  waiting for transfers between devices  35.6 us (7%)
  local copies, waits for them, and re-layouts  19.4 us (4%)
  matrix products  15.6 us (3%)
  other arithmetic  8.77 us (2%)
    psum x2, blocking collectives, squares(): return lax.psum(inner(residual, residual), ('gx', 'gy', 'gz'))  249 us
    psum x1, blocking collectives, body(): alpha = norm_now / lax.psum(inner(direction, image), ('gx', 'gy', 'gz'))  119 us
    ppermute x9, starting transfers between devices, with_halo(): lax.ppermute(tail, axis, [(i, (i + 1) % count) for i in range(ends)])  36.9 us
    ppermute x9, waiting for transfers between devices, with_halo(): lax.ppermute(head, axis, [((i + 1) % count, i) for i in range(ends)])  29 us
    ppermute x9, starting transfers between devices, with_halo(): lax.ppermute(head, axis, [((i + 1) % count, i) for i in range(ends)])  19.5 us
    dot_general x5, matrix products, grad_z(): jnp.einsum('ab,...xyeb->...xyea', matrix, blocks, precision=lax.Precision...  10.9 us
  transfers between devices with their start and end apart: 18, of which 11 were waited for; matrix products, arithmetic and copies ran while one was open for 1% of the time, Pallas kernels for 0%

commit v1 on v0

v1 whole, which is shorter than its diff:
```python
import functools

import jax
import jax.numpy as jnp
import numpy as np
from jax import lax
from jax.experimental import pallas as pl
from jax.experimental.pallas import tpu as pltpu
from jax.sharding import PartitionSpec as P

inverse_step = 2.0
viscosity = 0.05
F32 = jnp.float32
BF16 = jnp.bfloat16
NODES = 8


def gll_tables():
    degree = 7
    interior = np.array(
        [
            -0.8717401485096066,
            -0.5917001814331423,
            -0.2092992179024789,
            0.2092992179024789,
            0.5917001814331423,
            0.8717401485096066,
        ]
    )
    points = np.concatenate([[-1.0], interior, [1.0]])
    previous = np.ones(8)
    current = points * 1.0
    for degree_now in range(1, degree):
        following = ((2 * degree_now + 1) * points * current - degree_now * previous) / (
            degree_now + 1
        )
        previous = current
        current = following
    weights = 2.0 / (degree * (degree + 1) * current**2)
    matrix = np.zeros((8, 8))
    for row_idx in range(8):
        for col_idx in range(8):
            if row_idx != col_idx:
                matrix[row_idx, col_idx] = current[row_idx] / (
                    current[col_idx] * (points[row_idx] - points[col_idx])
                )
    matrix[0, 0] = -degree * (degree + 1) / 4.0
    matrix[7, 7] = degree * (degree + 1) / 4.0
    return (weights, matrix)


W1, D1 = gll_tables()
W1 = W1.astype(np.float32).astype(np.float64)
D1 = D1.astype(np.float32).astype(np.float64)
K1 = D1.T @ (W1[:, None] * D1)


def block_diag(small, count):
    return np.kron(np.eye(count), small)


def twin_matrix(length):
    out = np.eye(length)
    for i in range(NODES - 1, length - 1, NODES):
        out[i, i + 1] = 1.0
        out[i + 1, i] = 1.0
    return out


def assembled_stiffness(length):
    out = twin_matrix(length) @ block_diag(K1, length // NODES)
    out[0, 0] += K1[7, 7]
    out[-1, -1] += K1[0, 0]
    return out


def assembled_weights(length):
    out = np.tile(W1, length // NODES)
    out[0::NODES] *= 2.0
    out[NODES - 1 :: NODES] *= 2.0
    return out


def halves(matrix):
    high = matrix.astype(np.float32).astype(BF16)
    low = (matrix - high.astype(np.float64)).astype(np.float32).astype(BF16)
    return np.asarray(high), np.asarray(low)


def left_operand(matrix):
    high, low = halves(matrix)
    zero = np.zeros_like(low)
    return np.concatenate(
        [np.concatenate([high, high], 1), np.concatenate([low, zero], 1)], 0
    )


def right_operand(matrix):
    high, low = halves(matrix)
    zero = np.zeros_like(low)
    return np.concatenate(
        [np.concatenate([high, low], 1), np.concatenate([high, zero], 1)], 0
    )


def split(x):
    high = x.astype(BF16)
    low = (x - high.astype(F32)).astype(BF16)
    return high, low


def mul_left(operand, x):
    rows = operand.shape[0] // 2
    high, low = split(x)
    out = jnp.dot(operand, jnp.concatenate([high, low], 0), preferred_element_type=F32)
    return out[:rows] + out[rows:]


def mul_right(x, operand):
    cols = operand.shape[1] // 2
    high, low = split(x)
    out = jnp.dot(jnp.concatenate([high, low], 1), operand, preferred_element_type=F32)
    return out[:, :cols] + out[:, cols:]


def twin_z(x):
    length = x.shape[-1]
    lane = lax.broadcasted_iota(jnp.int32, x.shape, 1)
    after = pltpu.roll(x, length - 1, 1)
    before = pltpu.roll(x, 1, 1)
    spot = lane & (NODES - 1)
    upper = (spot == NODES - 1) & (lane != length - 1)
    lower = (spot == 0) & (lane != 0)
    return x + jnp.where(upper, after, 0.0) + jnp.where(lower, before, 0.0)


def twin_y(x):
    first, second = x[:, :8], x[:, 8:]
    row = lax.broadcasted_iota(jnp.int32, first.shape, 1)
    one = first + jnp.where(row == 7, second[:, 0:1], 0.0)
    two = second + jnp.where(row == 0, first[:, 7:8], 0.0)
    return jnp.concatenate([one, two], 1)


def forcing_kernel(
    nx, adj, flow, grads, sponge, mass, dy, dz, field, drag, right, left, right2, left2
):
    ix = lax.axis_index("gx")
    a = adj[...]
    _, sx, sy, sz = a.shape
    rows = sx * sy
    m = mass[...]
    grad_z = mul_right(a.reshape(3 * rows, sz), dz[...]).reshape(3, rows, sz)
    s_local = m * (inverse_step + sponge[...].reshape(rows, sz))
    s_asm = twin_z(twin_y(s_local.reshape(sx, sy, sz)).reshape(rows, sz))
    drag[...] = s_asm
    right[6] = s_asm[(sx - 1) * sy :]
    left[6] = s_asm[:sy]
    fl = [flow[j].astype(F32).reshape(rows, sz) for j in range(3)]
    flat = a.reshape(3, rows, sz)
    low_edge = jnp.where(ix == 0, 0.0, float(K1[7, 0])).astype(F32)
    high_edge = jnp.where(ix == nx - 1, 0.0, float(K1[0, 7])).astype(F32)
    for c in range(3):
        grad_y = mul_left(dy[...], flat[c])
        planes = [a[c, i] for i in range(sx)]
        grad_x = []
        for i in range(sx):
            total = float(D1[i, 0]) * planes[0]
            for k in range(1, sx):
                total = total + float(D1[i, k]) * planes[k]
            grad_x.append(total)
        grad_x = jnp.concatenate(grad_x, 0)
        local = inverse_step * flat[c]
        local = local + fl[0] * grad_x + fl[1] * grad_y + fl[2] * grad_z[c]
        for j in range(3):
            local = local - grads[3 * c + j].astype(F32).reshape(rows, sz) * flat[j]
        local = m * local
        out = twin_z(twin_y(local.reshape(sx, sy, sz)).reshape(rows, sz))
        field[c] = out
        plane = [out[i * sy : (i + 1) * sy] for i in range(sx)]
        up = low_edge * plane[0]
        for i in range(1, sx - 1):
            up = up + float(K1[7, i]) * plane[i]
        down = high_edge * plane[sx - 1]
        for i in range(1, sx - 1):
            down = down + float(K1[0, i]) * plane[i]
        right[c] = plane[sx - 1]
        right[3 + c] = up
        left[c] = plane[0]
        left[3 + c] = down
        right2[c] = plane[sx - 1]
        left2[c] = plane[0]


def x_stage_kernel(
    field, drag, from_low, from_high, from_low2, from_high2, ext, drag_out, up, down
):
    sy, sz = from_low.shape[1:]
    rows = field.shape[1]
    sx = rows // sy
    drag_out[...] = drag[...]
    drag_out[:sy] = drag[:sy] + from_low[6]
    drag_out[rows - sy :] = drag[rows - sy :] + from_high[6]
    count = 2 * sx
    for c in range(3):
        ext[c, :rows] = field[c]
        ext[c, :sy] = field[c, :sy] + from_low[c]
        ext[c, rows - sy : rows] = field[c, rows - sy :] + from_high[c]
        ext[c, rows : rows + sy] = from_low[3 + c] + float(K1[7, 0]) * from_low2[c]
        ext[c, rows + sy : rows + 2 * sy] = (
            from_high[3 + c] + float(K1[0, 7]) * from_high2[c]
        )

        def row(y):
            return ext[c, pl.ds(y, sx, stride=sy), :]

        up[c * count : c * count + sx] = row(sy - 1)
        total = float(K1[7, 0]) * row(sy - 8)
        for k in range(1, 7):
            total = total + float(K1[7, k]) * row(sy - 8 + k)
        up[c * count + sx : (c + 1) * count] = total
        down[c * count : c * count + sx] = row(0)
        total = float(K1[0, 7]) * row(7)
        for k in range(1, 7):
            total = total + float(K1[0, k]) * row(k)
        down[c * count + sx : (c + 1) * count] = total
    base = 3 * count
    up[base : base + sx] = drag_out[pl.ds(sy - 1, sx, stride=sy), :]
    down[base : base + sx] = drag_out[pl.ds(0, sx, stride=sy), :]
    base += sx
    up[base : base + 8] = jnp.zeros((8, sz), F32)
    down[base : base + 8] = jnp.zeros((8, sz), F32)
    for c in range(3):
        for side in range(2):
            spot = rows + side * sy
            at = base + 2 * c + side
            up[at : at + 1] = ext[c, spot + sy - 1 : spot + sy]
            down[at : at + 1] = ext[c, spot : spot + 1]


def y_stage_kernel(ext, drag, from_low, from_high, pick, ext_out, drag_out, message):
    rows, sz = drag.shape
    sy = (ext.shape[1] - rows) // 2
    sx = rows // sy
    count = 2 * sx
    base = 3 * count
    drag_out[...] = drag[...]
    drag_out[pl.ds(0, sx, stride=sy), :] = (
        drag[pl.ds(0, sx, stride=sy), :] + from_low[base : base + sx]
    )
    drag_out[pl.ds(sy - 1, sx, stride=sy), :] = (
        drag[pl.ds(sy - 1, sx, stride=sy), :] + from_high[base : base + sx]
    )
    base += sx
    used = rows + 2 * sy
    size = ext_out.shape[1]
    for c in range(3):
        ext_out[c, :used] = ext[c]
        ext_out[c, pl.ds(0, sx, stride=sy), :] = (
            ext[c, pl.ds(0, sx, stride=sy), :] + from_low[c * count : c * count + sx]
        )
        ext_out[c, pl.ds(sy - 1, sx, stride=sy), :] = (
            ext[c, pl.ds(sy - 1, sx, stride=sy), :]
            + from_high[c * count : c * count + sx]
        )
        for side in range(2):
            spot = rows + side * sy
            at = base + 2 * c + side
            ext_out[c, spot : spot + 1] = ext[c, spot : spot + 1] + from_low[at : at + 1]
            ext_out[c, spot + sy - 1 : spot + sy] = (
                ext[c, spot + sy - 1 : spot + sy] + from_high[at : at + 1]
            )
        ext_out[c, used : used + sx] = from_low[c * count + sx : (c + 1) * count]
        ext_out[c, used + sx : used + 2 * sx] = from_high[c * count + sx : (c + 1) * count]
        ext_out[c, used + 2 * sx :] = jnp.zeros((size - used - 2 * sx, sz), F32)
    for c in range(3):
        message[:, c * size : (c + 1) * size] = lax.dot_general(
            pick[...],
            ext_out[c],
            (((1,), (1,)), ((), ())),
            precision=lax.Precision.HIGHEST,
            preferred_element_type=F32,
        )
    message[:, 3 * size :] = lax.dot_general(
        pick[...],
        drag_out[...],
        (((1,), (1,)), ((), ())),
        precision=lax.Precision.HIGHEST,
        preferred_element_type=F32,
    )


def keep_mask(shape, sy, counts):
    row = lax.broadcasted_iota(jnp.int32, shape, 0)
    z = lax.broadcasted_iota(jnp.int32, shape, 1)
    shift = sy.bit_length() - 1
    x = lax.shift_right_logical(row, shift)
    y = row & (sy - 1)
    sx = shape[0] // sy
    mask = None
    for axis, spot, size in (("gx", x, sx), ("gy", y, sy), ("gz", z, shape[1])):
        here = spot + lax.axis_index(axis) * size
        inside = (here != 0) & (here != counts[axis] * size - 1)
        mask = inside if mask is None else mask & inside
    return mask


def moments_kernel(
    counts,
    sy,
    ext,
    drag,
    sponge,
    from_low,
    from_high,
    place,
    plane_asm,
    line_asm,
    plane_own,
    line_own,
    mass,
    share,
    plane_weight_asm,
    line_weight_asm,
    plane_weight,
    line_weight,
    base,
    image,
    sums,
):
    rows, sz = drag.shape
    size = ext.shape[1]
    keep = keep_mask((rows, sz), sy, counts)
    lane = lax.broadcasted_iota(jnp.int32, from_low.shape, 0)
    both = jnp.where(lane < 2, from_low[...], from_high[...])
    high = both.astype(BF16)
    rest = both - high.astype(F32)
    mid = rest.astype(BF16)
    low = (rest - mid.astype(F32)).astype(BF16)
    parts = jnp.concatenate([high, mid, low], 0)
    add = lax.dot_general(
        parts, place[...], (((0,), (0,)), ((), ())), preferred_element_type=F32
    )
    s_asm = drag[...] + add[3 * size :, :sz]
    s_own = mass[...] * (inverse_step + sponge[...].reshape(rows, sz))
    halves_of = mass.shape[1]
    total = [jnp.zeros((1, sz), F32) for _ in range(4)]
    for c in range(3):
        whole = ext[c] + add[c * size : (c + 1) * size, :sz]
        v = jnp.where(keep, whole[:rows], 0.0)
        plane = mul_left(plane_asm[...], jnp.concatenate([v, whole[rows:]], 0))
        line = mul_right(v, line_asm[...]) + add[c * size : c * size + rows, sz:]
        stiff = plane * line_weight_asm[...] + line * plane_weight_asm[...]
        u = jnp.where(keep, s_asm * v + viscosity * stiff, 0.0)
        stiff = (
            mul_left(plane_own[...], u) * line_weight[...]
            + mul_right(u, line_own[...]) * plane_weight[...]
        )
        own = s_own * u + viscosity * stiff
        base[c] = v
        image[c] = u
        sv = share[...] * v
        su = share[...] * u
        for k, term in enumerate((sv * v, sv * u, su * u, u * own)):
            total[k] = total[k] + jnp.sum(term, axis=0, keepdims=True)
    spot = lax.broadcasted_iota(jnp.int32, (1, sz), 1)
    out = jnp.zeros((1, sz), F32)
    for k in range(4):
        out = jnp.where(spot == k, jnp.sum(total[k], axis=1, keepdims=True), out)
    sums[...] = jnp.broadcast_to(out, sums.shape)


def combine_kernel(base, image, sums, out):
    total = jnp.sum(sums[...], axis=0, keepdims=True)
    m0, m1, m2, m3 = (total[:, k : k + 1] for k in range(4))
    alpha = m0 / m1
    norm = m0 - 2.0 * alpha * m1 + alpha * alpha * m2
    grow = 1.0 + norm / m0
    bend = grow * grow * m1 - 2.0 * grow * alpha * m2 + alpha * alpha * m3
    alpha2 = norm / bend
    one = alpha + alpha2 * grow
    two = alpha * alpha2
    for c in range(3):
        out[c] = one * base[c] - two * image[c]


VMEM = pl.BlockSpec(memory_space=pltpu.VMEM)


def call(kernel, operands, outs, flops=1_000_000):
    shapes = [jax.ShapeDtypeStruct(s, F32) for s in outs]
    size = sum(4 * int(np.prod(s)) for s in outs) + sum(
        o.dtype.itemsize * o.size for o in operands
    )
    return pl.pallas_call(
        kernel,
        out_shape=shapes,
        in_specs=[VMEM] * len(operands),
        out_specs=[VMEM] * len(outs),
        compiler_params=pltpu.CompilerParams(vmem_limit_bytes=16 * 1024 * 1024),
        cost_estimate=pl.CostEstimate(
            flops=flops, bytes_accessed=size, transcendentals=0
        ),
    )(*operands)


def shift(x, axis, step):
    count = lax.axis_size(axis)
    pairs = [(i, i + step) for i in range(count) if 0 <= i + step < count]
    return lax.ppermute(x, axis, pairs)


def body(adjoint_state, base_flow, base_grads, sponge):
    _, sx, sy, sz = adjoint_state.shape
    rows = sx * sy
    size = 2 * rows
    used = rows + 2 * sy
    counts = {axis: lax.axis_size(axis) for axis in ("gx", "gy", "gz")}
    wx, wy, wz = W1, np.tile(W1, sy // NODES), np.tile(W1, sz // NODES)
    ax, ay, az = (assembled_weights(n) for n in (sx, sy, sz))

    def f32(x):
        return jnp.asarray(x.astype(np.float32))

    def over_plane(x, y):
        return f32(np.broadcast_to(np.kron(x, y)[:, None], (rows, sz)))

    mass = f32(np.kron(wx, wy)[:, None] * wz[None, :])
    ends = np.ones(NODES)
    ends[0] = ends[-1] = 0.5
    share = f32(
        np.kron(ends, np.tile(ends, sy // NODES))[:, None]
        * np.tile(ends, sz // NODES)[None, :]
    )
    dy = jnp.asarray(left_operand(block_diag(D1, rows // NODES)))
    dz = jnp.asarray(right_operand(block_diag(D1, sz // NODES).T))
    field, drag, right, left, right2, left2 = call(
        functools.partial(forcing_kernel, counts["gx"]),
        (adjoint_state, base_flow, base_grads, sponge, mass, dy, dz),
        [(3, rows, sz), (rows, sz)] + [(7, sy, sz)] * 2 + [(3, sy, sz)] * 2,
    )
    x_low2 = shift(right2, "gx", 2)
    x_high2 = shift(left2, "gx", -2)
    x_low = shift(right, "gx", 1)
    x_high = shift(left, "gx", -1)
    message_rows = 7 * sx + 8
    ext, drag, up, down = call(
        x_stage_kernel,
        (field, drag, x_low, x_high, x_low2, x_high2),
        [(3, used, sz), (rows, sz), (message_rows, sz), (message_rows, sz)],
    )
    y_low = shift(up, "gy", 1)
    y_high = shift(down, "gy", -1)
    pick = np.zeros((8, sz))
    pick[0, sz - 1] = 1.0
    pick[1, sz - 8 : sz - 1] = K1[7, :7]
    pick[2, 0] = 1.0
    pick[3, 1:8] = K1[0, 1:]
    ext, drag, message = call(
        y_stage_kernel,
        (ext, drag, y_low, y_high, f32(pick)),
        [(3, size, sz), (rows, sz), (8, 3 * size + rows)],
    )
    z_low = shift(message, "gz", 1)
    z_high = shift(message, "gz", -1)

    place = np.zeros((8, 2 * sz))
    place[0, 0] = place[1, sz] = place[2, sz - 1] = place[3, 2 * sz - 1] = 1.0
    place = jnp.asarray(np.tile(place, (3, 1)).astype(np.float32).astype(BF16))
    plane_asm = np.zeros((rows, size))
    plane_asm[:, :rows] = np.kron(assembled_stiffness(sx), np.diag(ay)) + np.kron(
        np.diag(ax), assembled_stiffness(sy)
    )
    for y in range(sy):
        plane_asm[y, rows + y] = ay[y]
        plane_asm[rows - sy + y, rows + sy + y] = ay[y]
    for x in range(sx):
        plane_asm[x * sy, used + x] = ax[x]
        plane_asm[x * sy + sy - 1, used + sx + x] = ax[x]
    plane_own = np.kron(K1, np.diag(wy)) + np.kron(
        np.diag(wx), block_diag(K1, sy // NODES)
    )
    slots = counts["gz"]
    base, image, sums = call(
        functools.partial(moments_kernel, counts, sy),
        (
            ext,
            drag,
            sponge,
            z_low,
            z_high,
            place,
            jnp.asarray(left_operand(plane_asm)),
            jnp.asarray(right_operand(assembled_stiffness(sz).T)),
            jnp.asarray(left_operand(plane_own)),
            jnp.asarray(right_operand(block_diag(K1, sz // NODES).T)),
            mass,
            share,
            over_plane(ax, ay),
            f32(az[None, :]),
            over_plane(wx, wy),
            f32(wz[None, :]),
        ),
        [(3, rows, sz), (3, rows, sz), (slots, sz)],
    )
    sums = lax.all_to_all(sums, "gz", 0, 0, tiled=True)
    sums = jnp.sum(sums, axis=0, keepdims=True)
    slots = counts["gx"] * counts["gy"]
    sums = jnp.broadcast_to(sums, (slots, sz))
    sums = lax.all_to_all(sums, ("gx", "gy"), 0, 0, tiled=True)
    (out,) = call(combine_kernel, (base, image, sums), [(3, rows, sz)])
    return out.reshape(3, sx, sy, sz)


def solution(mesh):
    placed = (
        P(None, "gx", "gy", "gz"),
        P(None, "gx", "gy", "gz"),
        P(None, "gx", "gy", "gz"),
        P("gx", "gy", "gz"),
    )
    return jax.shard_map(
        body, mesh=mesh, in_specs=placed, out_specs=P(None, "gx", "gy", "gz"), check_vma=False
    )
```

time: 515 us -> 95.9 us (0.19); the launches traced: 508 us -> 95.3 us
  blocking collectives: 368 us -> 47.9 us
  starting transfers between devices: 56.3 us -> 25.8 us
  waiting for transfers between devices: 35.6 us -> 11.1 us
  matrix products: 15.6 us -> 0 us
  local copies, waits for them, and re-layouts: 19.4 us -> 6.92 us
  other arithmetic: 8.77 us -> 0.05 us
    psum x3 -> x0, blocking collectives: 368 us -> none  [the longest x2 249 us: squares(): return lax.psum(inner(residual, residual), ('gx', 'gy', 'gz'))]
    all_to_all x0 -> x2, blocking collectives: none -> 47.9 us  [the longest x1 31.8 us: body(): sums = lax.all_to_all(sums, 'gz', 0, 0, tiled=True)]
    ppermute x18 -> x8, starting transfers between devices: 56.3 us -> 25.8 us  [shift(): return lax.ppermute(x, axis, pairs)]
    ppermute x18 -> x8, waiting for transfers between devices: 35.6 us -> 11.1 us  [shift(): return lax.ppermute(x, axis, pairs)]
    dot_general x15 -> x0, matrix products: 15.6 us -> none  [the longest x5 10.9 us: grad_z(): jnp.einsum('ab,...xyeb->...xyea', matrix, blocks, precision=lax.Precision...]
    mul x15 -> x0, local copies, waits for them, and re-layouts: 7.94 us -> none  [the longest x2 2.41 us: body(): stiff = stiff + grad_z(mass3 * grad_z(direction, deriv), deriv_t)]
  transfers between devices with their start and end apart: 18 -> 8, of which waited for: 11 -> 3; matrix products, arithmetic and copies ran while one was open for 1% -> 0% of each run, Pallas kernels for 0% -> 0%
where the time goes in v1:
time: 95.9 us; the launch traced here: 95.3 us
  blocking collectives  47.9 us (50%)
  starting transfers between devices  25.8 us (27%)
  waiting for transfers between devices  11.1 us (12%)
  local copies, waits for them, and re-layouts  6.92 us (7%)
  Pallas kernels  3.36 us (4%)
    all_to_all x1, blocking collectives, body(): sums = lax.all_to_all(sums, 'gz', 0, 0, tiled=True)  31.8 us
    ppermute x8, starting transfers between devices, shift(): return lax.ppermute(x, axis, pairs)  25.8 us
    all_to_all x1, blocking collectives, body(): sums = lax.all_to_all(sums, ('gx', 'gy'), 0, 0, tiled=True)  16.1 us
    ppermute x8, waiting for transfers between devices, shift(): return lax.ppermute(x, axis, pairs)  11.1 us
    unnamed x40, local copies, waits for them, and re-layouts  6.9 us
    pallas_call x5, Pallas kernels, call(): pl.pallas_call(kernel, out_shape=shapes, in_specs=[VMEM] * len(operands),...  3.36 us
  transfers between devices with their start and end apart: 8, of which 3 were waited for; matrix products, arithmetic and copies ran while one was open for 0% of the time, Pallas kernels for 0%

profile of v1, /device:TPU:1, one launch (start us, length us, event | category | flops | bytes accessed | tf_op | source)
XLA Modules:
  0.0 95.3 jit_solution(3598557063953124069)
XLA Ops:
  0.0 1.0 %copy-done = bf16[9,8,16,128]{3,2,1,0:T(8,128)(2,1)S(1)} copy-done((bf16[9,8,16,128]{3,2,1,0:T(8,128)(2,1)S(1)}, bf16[9,8,16,128]{3,2,1,0:T(8,128)(2,1)}, u32[]{:S(2)}) %copy-start) | copy-done | bytes 294936
  1.0 0.8 copy-done.2
  1.8 0.8 copy-done.4
  2.6 0.9 copy-done.6
  3.6 0.9 copy-done.10
  4.5 0.9 copy-done.11
  5.4 0.9 copy-done.12
  6.8 4.0 %collective-permute-start = (f32[7,16,128]{2,1,0:T(8,128)S(1)}, f32[7,16,128]{2,1,0:T(8,128)S(1)}, u32[]{:S(2)}, u32[]{:S(2)}) collective-permute-start(f32[7,16,128]{2,1,0:T(8,128)S(1)} %get-tuple-element.23), channel_id=1, source_target_pairs={{0,128},{128,256},{256,384},{384,512},{512,640},{640,768},{768,896... | collective-permute-start | bytes 172040 | tf_op jit(solution)/shard_map/ppermute | solution.py:410
  10.8 1.3 %collective-permute-start.1 = (f32[7,16,128]{2,1,0:T(8,128)S(1)}, f32[7,16,128]{2,1,0:T(8,128)S(1)}, u32[]{:S(2)}, u32[]{:S(2)}) collective-permute-start(f32[7,16,128]{2,1,0:T(8,128)S(1)} %get-tuple-element.24), channel_id=1, source_target_pairs={{128,0},{256,128},{384,256},{512,384},{640,512},{768,640},{896,768... | collective-permute-start | bytes 172040 | tf_op jit(solution)/shard_map/ppermute | solution.py:410
  12.1 5.0 %collective-permute-start.2 = (f32[3,16,128]{2,1,0:T(8,128)S(1)}, f32[3,16,128]{2,1,0:T(8,128)S(1)}, u32[]{:S(2)}, u32[]{:S(2)}) collective-permute-start(f32[3,16,128]{2,1,0:T(8,128)S(1)} %get-tuple-element.25), channel_id=1, source_target_pairs={{0,256},{128,384},{256,512},{384,640},{512,768},{640,896},{1,257},... | collective-permute-start | bytes 73736 | tf_op jit(solution)/shard_map/ppermute | solution.py:410
  17.1 1.3 %collective-permute-start.3 = (f32[3,16,128]{2,1,0:T(8,128)S(1)}, f32[3,16,128]{2,1,0:T(8,128)S(1)}, u32[]{:S(2)}, u32[]{:S(2)}) collective-permute-start(f32[3,16,128]{2,1,0:T(8,128)S(1)} %get-tuple-element.26), channel_id=1, source_target_pairs={{256,0},{384,128},{512,256},{640,384},{768,512},{896,640},{257,1},... | collective-permute-start | bytes 73736 | tf_op jit(solution)/shard_map/ppermute | solution.py:410
  18.4 6.5 %collective-permute-done.3.from_high2 = f32[3,16,128]{2,1,0:T(8,128)S(1)} collective-permute-done((f32[3,16,128]{2,1,0:T(8,128)S(1)}, f32[3,16,128]{2,1,0:T(8,128)S(1)}, u32[]{:S(2)}, u32[]{:S(2)}) %collective-permute-start.3) | collective-permute-done | bytes 24608 | tf_op jit(solution)/shard_map/ppermute | solution.py:410
  25.1 3.3 %collective-permute-start.4 = (f32[64,128]{1,0:T(8,128)S(1)}, f32[64,128]{1,0:T(8,128)S(1)}, u32[]{:S(2)}, u32[]{:S(2)}) collective-permute-start(f32[64,128]{1,0:T(8,128)S(1)} %get-tuple-element.29), channel_id=1, source_target_pairs={{0,32},{32,64},{64,96},{1,33},{33,65},{65,97},{2,34},{34,66},{66,9... | collective-permute-start | bytes 98312 | tf_op jit(solution)/shard_map/ppermute | solution.py:410
  28.4 1.3 %collective-permute-start.5 = (f32[64,128]{1,0:T(8,128)S(1)}, f32[64,128]{1,0:T(8,128)S(1)}, u32[]{:S(2)}, u32[]{:S(2)}) collective-permute-start(f32[64,128]{1,0:T(8,128)S(1)} %get-tuple-element.30), channel_id=1, source_target_pairs={{32,0},{64,32},{96,64},{33,1},{65,33},{97,65},{34,2},{66,34},{98,6... | collective-permute-start | bytes 98312 | tf_op jit(solution)/shard_map/ppermute | solution.py:410
  29.7 3.3 %collective-permute-done.5.from_high = f32[64,128]{1,0:T(8,128)S(1)} collective-permute-done((f32[64,128]{1,0:T(8,128)S(1)}, f32[64,128]{1,0:T(8,128)S(1)}, u32[]{:S(2)}, u32[]{:S(2)}) %collective-permute-start.5) | collective-permute-done | bytes 32800 | tf_op jit(solution)/shard_map/ppermute | solution.py:410
  33.1 0.5 shard_map.174
  33.6 7.7 %collective-permute-start.7 = (f32[8,896]{1,0:T(8,128)S(1)}, f32[8,896]{1,0:T(8,128)S(1)}, u32[]{:S(2)}, u32[]{:S(2)}) collective-permute-start(f32[8,896]{1,0:T(8,128)S(1)} %get-tuple-element.33), channel_id=1, source_target_pairs={{1,0},{2,1},{3,2},{4,3},{5,4},{6,5},{7,6},{8,7},{9,8},{10,9},{11,1... | collective-permute-start | bytes 86024 | tf_op jit(solution)/shard_map/ppermute | solution.py:410
  41.3 1.9 %collective-permute-start.6 = (f32[8,896]{1,0:T(8,128)S(1)}, f32[8,896]{1,0:T(8,128)S(1)}, u32[]{:S(2)}, u32[]{:S(2)}) collective-permute-start(f32[8,896]{1,0:T(8,128)S(1)} %get-tuple-element.33), channel_id=1, source_target_pairs={{0,1},{1,2},{2,3},{3,4},{4,5},{5,6},{6,7},{7,8},{8,9},{9,10},{10,1... | collective-permute-start | bytes 86024 | tf_op jit(solution)/shard_map/ppermute | solution.py:410
  43.3 1.2 %collective-permute-done.6.from_low = f32[8,896]{1,0:T(8,128)S(1)} collective-permute-done((f32[8,896]{1,0:T(8,128)S(1)}, f32[8,896]{1,0:T(8,128)S(1)}, u32[]{:S(2)}, u32[]{:S(2)}) %collective-permute-start.6) | collective-permute-done | bytes 28704 | tf_op jit(solution)/shard_map/ppermute | solution.py:410
  44.5 0.6 copy-done.18
  45.1 1.4 %shard_map.175 = (f32[3,128,128]{2,1,0:T(8,128)S(1)}, f32[3,128,128]{2,1,0:T(8,128)S(1)}, f32[32,128]{1,0:T(8,128)S(1)}) custom-call(f32[3,256,128]{2,1,0:T(8,128)S(1)} %get-tuple-element.31.ext, f32[128,128]{1,0:T(8,128)S(1)} %get-tuple-element.32.drag, f32[8,16,128]{2,1,0:T(8,128)S(1)} %copy-done.3, f32[8,896]{1,0:T(8,128)S(1)} %collective-permute-done.6.from_low, ...), custom_call_target="tpu_custom_call" | custom-call | flops 1000000 | bytes 1922048 | tf_op jit(solution)/shard_map/pallas_call | solution.py:395
  46.5 31.8 %all_to_all.17 = f32[32,1,128]{2,1,0:T(1,128)S(1)} all-to-all(f32[32,1,128]{2,1,0:T(1,128)S(1)} %bitcast.6), channel_id=1, replica_groups=mesh['gx'=8,'gy'=4,'gz'=32] {'gz'}, dimensions={0} | all-to-all | bytes 32768 | tf_op jit(solution)/shard_map/all_to_all | solution.py:506
  78.4 16.1 %all_to_all.18 = f32[32,1,128]{2,1,0:T(1,128)S(1)} all-to-all(f32[32,1,128]{2,1,0:T(1,128)S(1)} %broadcast_in_dim.2), channel_id=1, replica_groups=mesh['gx'=8,'gy'=4,'gz'=32] {'gx','gy'}, dimensions={0} | all-to-all | bytes 32768 | tf_op jit(solution)/shard_map/all_to_all | solution.py:510
  94.4 0.8 shard_map.176
  (41 shorter events, 0.7 us)
Async XLA Ops:
  0.0 1.0 %copy-start = (bf16[9,8,16,128]{3,2,1,0:T(8,128)(2,1)S(1)}, bf16[9,8,16,128]{3,2,1,0:T(8,128)(2,1)}, u32[]{:S(2)}) copy-start(bf16[9,8,16,128]{3,2,1,0:T(8,128)(2,1)} %grads.1) | copy-start | bytes 884740
  2.6 0.9 copy-start.6
  3.6 0.9 copy-start.10
  4.5 0.9 copy-start.11
  5.4 0.9 copy-start.12
  6.3 38.2 %copy-start.13 = (f32[128,128]{1,0:T(8,128)S(1)}, f32[128,128]{1,0:T(8,128)}, u32[]{:S(2)}) copy-start(f32[128,128]{1,0:T(8,128)} %constant.42.clone.plane_weight) | copy-start | bytes 196612
  6.3 38.2 %copy-start.14 = (f32[128,128]{1,0:T(8,128)S(1)}, f32[128,128]{1,0:T(8,128)}, u32[]{:S(2)}) copy-start(f32[128,128]{1,0:T(8,128)} %constant.40.clone.plane_weight_asm) | copy-start | bytes 196612
  6.3 38.2 %copy-start.15 = (f32[128,128]{1,0:T(8,128)S(1)}, f32[128,128]{1,0:T(8,128)}, u32[]{:S(2)}) copy-start(f32[128,128]{1,0:T(8,128)} %constant.31.clone.share) | copy-start | bytes 196612
  6.8 18.2 %collective-permute-start = (f32[7,16,128]{2,1,0:T(8,128)S(1)}, f32[7,16,128]{2,1,0:T(8,128)S(1)}, u32[]{:S(2)}, u32[]{:S(2)}) collective-permute-start(f32[7,16,128]{2,1,0:T(8,128)S(1)} %get-tuple-element.23), channel_id=1, source_target_pairs={{0,128},{128,256},{256,384},{384,512},{512,640},{640,768},{768,896... | collective-permute-start | bytes 172040 | tf_op jit(solution)/shard_map/ppermute | solution.py:410
  10.8 14.2 %collective-permute-start.1 = (f32[7,16,128]{2,1,0:T(8,128)S(1)}, f32[7,16,128]{2,1,0:T(8,128)S(1)}, u32[]{:S(2)}, u32[]{:S(2)}) collective-permute-start(f32[7,16,128]{2,1,0:T(8,128)S(1)} %get-tuple-element.24), channel_id=1, source_target_pairs={{128,0},{256,128},{384,256},{512,384},{640,512},{768,640},{896,768... | collective-permute-start | bytes 172040 | tf_op jit(solution)/shard_map/ppermute | solution.py:410
  12.1 6.3 %collective-permute-start.2 = (f32[3,16,128]{2,1,0:T(8,128)S(1)}, f32[3,16,128]{2,1,0:T(8,128)S(1)}, u32[]{:S(2)}, u32[]{:S(2)}) collective-permute-start(f32[3,16,128]{2,1,0:T(8,128)S(1)} %get-tuple-element.25), channel_id=1, source_target_pairs={{0,256},{128,384},{256,512},{384,640},{512,768},{640,896},{1,257},... | collective-permute-start | bytes 73736 | tf_op jit(solution)/shard_map/ppermute | solution.py:410
  17.1 7.8 %collective-permute-start.3 = (f32[3,16,128]{2,1,0:T(8,128)S(1)}, f32[3,16,128]{2,1,0:T(8,128)S(1)}, u32[]{:S(2)}, u32[]{:S(2)}) collective-permute-start(f32[3,16,128]{2,1,0:T(8,128)S(1)} %get-tuple-element.26), channel_id=1, source_target_pairs={{256,0},{384,128},{512,256},{640,384},{768,512},{896,640},{257,1},... | collective-permute-start | bytes 73736 | tf_op jit(solution)/shard_map/ppermute | solution.py:410
  25.0 8.1 %copy-start.17 = (f32[8,128]{1,0:T(8,128)S(1)}, f32[8,128]{1,0:T(8,128)}, u32[]{:S(2)}) copy-start(f32[8,128]{1,0:T(8,128)} %constant.34.clone.pick) | copy-start | bytes 12292
  25.0 19.5 %copy-start.7 = (bf16[256,256]{1,0:T(8,128)(2,1)S(1)}, bf16[256,256]{1,0:T(8,128)(2,1)}, u32[]{:S(2)}) copy-start(bf16[256,256]{1,0:T(8,128)(2,1)} %constant.39.clone.line_own) | copy-start | bytes 393220
  25.0 19.5 %copy-start.8 = (bf16[256,256]{1,0:T(8,128)(2,1)S(1)}, bf16[256,256]{1,0:T(8,128)(2,1)}, u32[]{:S(2)}) copy-start(bf16[256,256]{1,0:T(8,128)(2,1)} %constant.38.clone.plane_own) | copy-start | bytes 393220
  25.0 19.5 %copy-start.9 = (bf16[256,256]{1,0:T(8,128)(2,1)S(1)}, bf16[256,256]{1,0:T(8,128)(2,1)}, u32[]{:S(2)}) copy-start(bf16[256,256]{1,0:T(8,128)(2,1)} %constant.37.clone.line_asm) | copy-start | bytes 393220
  25.0 19.5 %copy-start.16 = (bf16[24,256]{1,0:T(8,128)(2,1)S(1)}, bf16[24,256]{1,0:T(8,128)(2,1)}, u32[]{:S(2)}) copy-start(bf16[24,256]{1,0:T(8,128)(2,1)} %constant.35.clone.place) | copy-start | bytes 36868
  25.1 19.4 %copy-start.1 = (bf16[256,512]{1,0:T(8,128)(2,1)S(1)}, bf16[256,512]{1,0:T(8,128)(2,1)}, u32[]{:S(2)}) copy-start(bf16[256,512]{1,0:T(8,128)(2,1)} %constant.36.clone.plane_asm) | copy-start | bytes 786436
  25.1 4.6 %collective-permute-start.4 = (f32[64,128]{1,0:T(8,128)S(1)}, f32[64,128]{1,0:T(8,128)S(1)}, u32[]{:S(2)}, u32[]{:S(2)}) collective-permute-start(f32[64,128]{1,0:T(8,128)S(1)} %get-tuple-element.29), channel_id=1, source_target_pairs={{0,32},{32,64},{64,96},{1,33},{33,65},{65,97},{2,34},{34,66},{66,9... | collective-permute-start | bytes 98312 | tf_op jit(solution)/shard_map/ppermute | solution.py:410
  28.4 4.7 %collective-permute-start.5 = (f32[64,128]{1,0:T(8,128)S(1)}, f32[64,128]{1,0:T(8,128)S(1)}, u32[]{:S(2)}, u32[]{:S(2)}) collective-permute-start(f32[64,128]{1,0:T(8,128)S(1)} %get-tuple-element.30), channel_id=1, source_target_pairs={{32,0},{64,32},{96,64},{33,1},{65,33},{97,65},{34,2},{66,34},{98,6... | collective-permute-start | bytes 98312 | tf_op jit(solution)/shard_map/ppermute | solution.py:410
  33.1 11.4 %copy-start.3 = (f32[8,16,128]{2,1,0:T(8,128)S(1)}, f32[8,16,128]{2,1,0:T(8,128)}, u32[]{:S(2)}) copy-start(f32[8,16,128]{2,1,0:T(8,128)} %sponge.3) | copy-start | bytes 196612
  33.1 11.4 %copy-start.5 = (f32[128,128]{1,0:T(8,128)S(1)}, f32[128,128]{1,0:T(8,128)}, u32[]{:S(2)}) copy-start(f32[128,128]{1,0:T(8,128)} %constant.30.clone.mass) | copy-start | bytes 196612
  33.6 9.7 %collective-permute-start.7 = (f32[8,896]{1,0:T(8,128)S(1)}, f32[8,896]{1,0:T(8,128)S(1)}, u32[]{:S(2)}, u32[]{:S(2)}) collective-permute-start(f32[8,896]{1,0:T(8,128)S(1)} %get-tuple-element.33), channel_id=1, source_target_pairs={{1,0},{2,1},{3,2},{4,3},{5,4},{6,5},{7,6},{8,7},{9,8},{10,9},{11,1... | collective-permute-start | bytes 86024 | tf_op jit(solution)/shard_map/ppermute | solution.py:410
  41.3 3.1 %collective-permute-start.6 = (f32[8,896]{1,0:T(8,128)S(1)}, f32[8,896]{1,0:T(8,128)S(1)}, u32[]{:S(2)}, u32[]{:S(2)}) collective-permute-start(f32[8,896]{1,0:T(8,128)S(1)} %get-tuple-element.33), channel_id=1, source_target_pairs={{0,1},{1,2},{2,3},{3,4},{4,5},{5,6},{6,7},{7,8},{8,9},{9,10},{10,1... | collective-permute-start | bytes 86024 | tf_op jit(solution)/shard_map/ppermute | solution.py:410
  (4 other events, 3.0 us)

commit v2 on v1

--- a/solution.py
+++ b/solution.py
@@ -143,9 +143,48 @@
 
 
 def forcing_kernel(
-    nx, adj, flow, grads, sponge, mass, dy, dz, field, drag, right, left, right2, left2
+    nx,
+    adj_hbm,
+    flow_hbm,
+    grads_hbm,
+    sponge_hbm,
+    mass_hbm,
+    dy_hbm,
+    dz_hbm,
+    field,
+    drag,
+    right,
+    left,
+    right2,
+    left2,
+    adj,
+    flow,
+    grads,
+    sponge,
+    mass,
+    dy,
+    dz,
+    sems,
 ):
+    copies = [
+        pltpu.make_async_copy(src, dst, sems.at[k])
+        for k, (src, dst) in enumerate(
+            (
+                (adj_hbm, adj),
+                (dz_hbm, dz),
+                (mass_hbm, mass),
+                (sponge_hbm, sponge),
+                (dy_hbm, dy),
+                (flow_hbm, flow),
+                (grads_hbm, grads),
+            )
+        )
+    ]
+    for copy in copies:
+        copy.start()
     ix = lax.axis_index("gx")
+    for copy in copies:
+        copy.wait()
     a = adj[...]
     _, sx, sy, sz = a.shape
     rows = sx * sy
@@ -305,6 +344,14 @@
     return mask
 
 
+def line_pattern(values, shape):
+    spot = lax.broadcasted_iota(jnp.int32, shape, 1) & (NODES - 1)
+    out = jnp.full(shape, float(values[0]), F32)
+    for k in range(1, NODES):
+        out = jnp.where(spot == k, float(values[k]), out)
+    return out
+
+
 def moments_kernel(
     counts,
     sy,
@@ -321,9 +368,7 @@
     mass,
     share,
     plane_weight_asm,
-    line_weight_asm,
     plane_weight,
-    line_weight,
     base,
     image,
     sums,
@@ -343,17 +388,18 @@
     )
     s_asm = drag[...] + add[3 * size :, :sz]
     s_own = mass[...] * (inverse_step + sponge[...].reshape(rows, sz))
-    halves_of = mass.shape[1]
+    line_weight = line_pattern(W1, (1, sz))
+    line_weight_asm = line_pattern(assembled_weights(NODES), (1, sz))
     total = [jnp.zeros((1, sz), F32) for _ in range(4)]
     for c in range(3):
         whole = ext[c] + add[c * size : (c + 1) * size, :sz]
         v = jnp.where(keep, whole[:rows], 0.0)
         plane = mul_left(plane_asm[...], jnp.concatenate([v, whole[rows:]], 0))
         line = mul_right(v, line_asm[...]) + add[c * size : c * size + rows, sz:]
-        stiff = plane * line_weight_asm[...] + line * plane_weight_asm[...]
+        stiff = plane * line_weight_asm + line * plane_weight_asm[...]
         u = jnp.where(keep, s_asm * v + viscosity * stiff, 0.0)
         stiff = (
-            mul_left(plane_own[...], u) * line_weight[...]
+            mul_left(plane_own[...], u) * line_weight
             + mul_right(u, line_own[...]) * plane_weight[...]
         )
         own = s_own * u + viscosity * stiff
@@ -385,9 +431,10 @@
 
 
 VMEM = pl.BlockSpec(memory_space=pltpu.VMEM)
-
-
-def call(kernel, operands, outs, flops=1_000_000):
+HBM = pl.BlockSpec(memory_space=pltpu.HBM)
+
+
+def call(kernel, operands, outs, fetch=False):
     shapes = [jax.ShapeDtypeStruct(s, F32) for s in outs]
     size = sum(4 * int(np.prod(s)) for s in outs) + sum(
         o.dtype.itemsize * o.size for o in operands
@@ -395,11 +442,15 @@
     return pl.pallas_call(
         kernel,
         out_shape=shapes,
-        in_specs=[VMEM] * len(operands),
+        in_specs=[HBM if fetch else VMEM] * len(operands),
         out_specs=[VMEM] * len(outs),
+        scratch_shapes=[pltpu.VMEM(o.shape, o.dtype) for o in operands]
+        + [pltpu.SemaphoreType.DMA((len(operands),))]
+        if fetch
+        else [],
         compiler_params=pltpu.CompilerParams(vmem_limit_bytes=16 * 1024 * 1024),
         cost_estimate=pl.CostEstimate(
-            flops=flops, bytes_accessed=size, transcendentals=0
+            flops=1_000_000, bytes_accessed=size, transcendentals=0
         ),
     )(*operands)
 
@@ -417,7 +468,7 @@
     used = rows + 2 * sy
     counts = {axis: lax.axis_size(axis) for axis in ("gx", "gy", "gz")}
     wx, wy, wz = W1, np.tile(W1, sy // NODES), np.tile(W1, sz // NODES)
-    ax, ay, az = (assembled_weights(n) for n in (sx, sy, sz))
+    ax, ay = assembled_weights(sx), assembled_weights(sy)
 
     def f32(x):
         return jnp.asarray(x.astype(np.float32))
@@ -438,6 +489,7 @@
         functools.partial(forcing_kernel, counts["gx"]),
         (adjoint_state, base_flow, base_grads, sponge, mass, dy, dz),
         [(3, rows, sz), (rows, sz)] + [(7, sy, sz)] * 2 + [(3, sy, sz)] * 2,
+        fetch=True,
     )
     x_low2 = shift(right2, "gx", 2)
     x_high2 = shift(left2, "gx", -2)
@@ -497,9 +549,7 @@
             mass,
             share,
             over_plane(ax, ay),
-            f32(az[None, :]),
             over_plane(wx, wy),
-            f32(wz[None, :]),
         ),
         [(3, rows, sz), (3, rows, sz), (slots, sz)],
     )

time: 95.9 us -> 96.3 us (level)
  Pallas kernels: 3.36 us -> 4.39 us
    pallas_call x5, Pallas kernels: 3.36 us -> 4.39 us  [call(): pl.pallas_call(kernel, out_shape=shapes, in_specs=[HBM if fetch else VMEM...]
    unnamed x40 -> x36, local copies, waits for them, and re-layouts: 6.9 us -> 6.32 us
where the time goes in v2:
time: 96.3 us; the launch traced here: 95.7 us
  blocking collectives  47.9 us (50%)
  starting transfers between devices  25.8 us (27%)
  waiting for transfers between devices  11.1 us (12%)
  local copies, waits for them, and re-layouts  6.33 us (7%)
  Pallas kernels  4.39 us (5%)
    all_to_all x1, blocking collectives, body(): sums = lax.all_to_all(sums, 'gz', 0, 0, tiled=True)  31.8 us
    ppermute x8, starting transfers between devices, shift(): return lax.ppermute(x, axis, pairs)  25.8 us
    all_to_all x1, blocking collectives, body(): sums = lax.all_to_all(sums, ('gx', 'gy'), 0, 0, tiled=True)  16.1 us
    ppermute x8, waiting for transfers between devices, shift(): return lax.ppermute(x, axis, pairs)  11.1 us
    unnamed x36, local copies, waits for them, and re-layouts  6.32 us
    pallas_call x5, Pallas kernels, call(): pl.pallas_call(kernel, out_shape=shapes, in_specs=[HBM if fetch else VMEM...  4.39 us
  transfers between devices with their start and end apart: 8, of which 3 were waited for; matrix products, arithmetic and copies ran while one was open for 0% of the time, Pallas kernels for 0%

profile of v2, /device:TPU:1, one launch (start us, length us, event | category | flops | bytes accessed | tf_op | source)
XLA Modules:
  0.0 95.7 jit_solution(17510112647158557758)
XLA Ops:
  0.0 1.0 %copy-done = bf16[9,8,16,128]{3,2,1,0:T(8,128)(2,1)S(1)} copy-done((bf16[9,8,16,128]{3,2,1,0:T(8,128)(2,1)S(1)}, bf16[9,8,16,128]{3,2,1,0:T(8,128)(2,1)}, u32[]{:S(2)}) %copy-start) | copy-done | bytes 294936
  1.0 0.8 copy-done.2
  1.8 0.8 copy-done.4
  2.6 0.9 copy-done.6
  3.6 0.9 copy-done.10
  4.5 0.9 copy-done.11
  5.4 0.9 copy-done.12
  6.3 1.5 %shard_map.154 = (f32[3,128,128]{2,1,0:T(8,128)S(1)}, f32[128,128]{1,0:T(8,128)S(1)}, f32[7,16,128]{2,1,0:T(8,128)S(1)}, f32[7,16,128]{2,1,0:T(8,128)S(1)}, f32[...) custom-call(f32[3,8,16,128]{3,2,1,0:T(8,128)S(1)} %copy-done.6, bf16[3,8,16,128]{3,2,1,0:T(8,128)(2,1)S(1)} %copy-done.12, ...), custom_call_target="tpu_custom_call" | custom-call | flops 1000000 | bytes 1409024 | tf_op jit(solution)/shard_map/pallas_call | solution.py:442
  7.8 4.0 %collective-permute-start = (f32[7,16,128]{2,1,0:T(8,128)S(1)}, f32[7,16,128]{2,1,0:T(8,128)S(1)}, u32[]{:S(2)}, u32[]{:S(2)}) collective-permute-start(f32[7,16,128]{2,1,0:T(8,128)S(1)} %get-tuple-element.23), channel_id=1, source_target_pairs={{0,128},{128,256},{256,384},{384,512},{512,640},{640,768},{768,896... | collective-permute-start | bytes 172040 | tf_op jit(solution)/shard_map/ppermute | solution.py:461
  11.8 1.3 %collective-permute-start.1 = (f32[7,16,128]{2,1,0:T(8,128)S(1)}, f32[7,16,128]{2,1,0:T(8,128)S(1)}, u32[]{:S(2)}, u32[]{:S(2)}) collective-permute-start(f32[7,16,128]{2,1,0:T(8,128)S(1)} %get-tuple-element.24), channel_id=1, source_target_pairs={{128,0},{256,128},{384,256},{512,384},{640,512},{768,640},{896,768... | collective-permute-start | bytes 172040 | tf_op jit(solution)/shard_map/ppermute | solution.py:461
  13.1 5.0 %collective-permute-start.2 = (f32[3,16,128]{2,1,0:T(8,128)S(1)}, f32[3,16,128]{2,1,0:T(8,128)S(1)}, u32[]{:S(2)}, u32[]{:S(2)}) collective-permute-start(f32[3,16,128]{2,1,0:T(8,128)S(1)} %get-tuple-element.25), channel_id=1, source_target_pairs={{0,256},{128,384},{256,512},{384,640},{512,768},{640,896},{1,257},... | collective-permute-start | bytes 73736 | tf_op jit(solution)/shard_map/ppermute | solution.py:461
  18.1 1.3 %collective-permute-start.3 = (f32[3,16,128]{2,1,0:T(8,128)S(1)}, f32[3,16,128]{2,1,0:T(8,128)S(1)}, u32[]{:S(2)}, u32[]{:S(2)}) collective-permute-start(f32[3,16,128]{2,1,0:T(8,128)S(1)} %get-tuple-element.26), channel_id=1, source_target_pairs={{256,0},{384,128},{512,256},{640,384},{768,512},{896,640},{257,1},... | collective-permute-start | bytes 73736 | tf_op jit(solution)/shard_map/ppermute | solution.py:461
  19.5 6.5 %collective-permute-done.3.from_high2 = f32[3,16,128]{2,1,0:T(8,128)S(1)} collective-permute-done((f32[3,16,128]{2,1,0:T(8,128)S(1)}, f32[3,16,128]{2,1,0:T(8,128)S(1)}, u32[]{:S(2)}, u32[]{:S(2)}) %collective-permute-start.3) | collective-permute-done | bytes 24608 | tf_op jit(solution)/shard_map/ppermute | solution.py:461
  26.2 3.2 %collective-permute-start.4 = (f32[64,128]{1,0:T(8,128)S(1)}, f32[64,128]{1,0:T(8,128)S(1)}, u32[]{:S(2)}, u32[]{:S(2)}) collective-permute-start(f32[64,128]{1,0:T(8,128)S(1)} %get-tuple-element.29), channel_id=1, source_target_pairs={{0,32},{32,64},{64,96},{1,33},{33,65},{65,97},{2,34},{34,66},{66,9... | collective-permute-start | bytes 98312 | tf_op jit(solution)/shard_map/ppermute | solution.py:461
  29.4 1.3 %collective-permute-start.5 = (f32[64,128]{1,0:T(8,128)S(1)}, f32[64,128]{1,0:T(8,128)S(1)}, u32[]{:S(2)}, u32[]{:S(2)}) collective-permute-start(f32[64,128]{1,0:T(8,128)S(1)} %get-tuple-element.30), channel_id=1, source_target_pairs={{32,0},{64,32},{96,64},{33,1},{65,33},{97,65},{34,2},{66,34},{98,6... | collective-permute-start | bytes 98312 | tf_op jit(solution)/shard_map/ppermute | solution.py:461
  30.7 3.3 %collective-permute-done.5.from_high = f32[64,128]{1,0:T(8,128)S(1)} collective-permute-done((f32[64,128]{1,0:T(8,128)S(1)}, f32[64,128]{1,0:T(8,128)S(1)}, u32[]{:S(2)}, u32[]{:S(2)}) %collective-permute-start.5) | collective-permute-done | bytes 32800 | tf_op jit(solution)/shard_map/ppermute | solution.py:461
  34.1 0.5 shard_map.156
  34.6 7.7 %collective-permute-start.7 = (f32[8,896]{1,0:T(8,128)S(1)}, f32[8,896]{1,0:T(8,128)S(1)}, u32[]{:S(2)}, u32[]{:S(2)}) collective-permute-start(f32[8,896]{1,0:T(8,128)S(1)} %get-tuple-element.33), channel_id=1, source_target_pairs={{1,0},{2,1},{3,2},{4,3},{5,4},{6,5},{7,6},{8,7},{9,8},{10,9},{11,1... | collective-permute-start | bytes 86024 | tf_op jit(solution)/shard_map/ppermute | solution.py:461
  42.4 1.9 %collective-permute-start.6 = (f32[8,896]{1,0:T(8,128)S(1)}, f32[8,896]{1,0:T(8,128)S(1)}, u32[]{:S(2)}, u32[]{:S(2)}) collective-permute-start(f32[8,896]{1,0:T(8,128)S(1)} %get-tuple-element.33), channel_id=1, source_target_pairs={{0,1},{1,2},{2,3},{3,4},{4,5},{5,6},{6,7},{7,8},{8,9},{9,10},{10,1... | collective-permute-start | bytes 86024 | tf_op jit(solution)/shard_map/ppermute | solution.py:461
  44.3 1.2 %collective-permute-done.6.from_low = f32[8,896]{1,0:T(8,128)S(1)} collective-permute-done((f32[8,896]{1,0:T(8,128)S(1)}, f32[8,896]{1,0:T(8,128)S(1)}, u32[]{:S(2)}, u32[]{:S(2)}) %collective-permute-start.6) | collective-permute-done | bytes 28704 | tf_op jit(solution)/shard_map/ppermute | solution.py:461
  45.5 1.4 %shard_map.157 = (f32[3,128,128]{2,1,0:T(8,128)S(1)}, f32[3,128,128]{2,1,0:T(8,128)S(1)}, f32[32,128]{1,0:T(8,128)S(1)}) custom-call(f32[3,256,128]{2,1,0:T(8,128)S(1)} %get-tuple-element.31.ext, f32[128,128]{1,0:T(8,128)S(1)} %get-tuple-element.32.drag, f32[8,16,128]{2,1,0:T(8,128)S(1)} %copy-done.3, f32[8,896]{1,0:T(8,128)S(1)} %collective-permute-done.6.from_low, ...), custom_call_target="tpu_custom_call" | custom-call | flops 1000000 | bytes 1921024 | tf_op jit(solution)/shard_map/pallas_call | solution.py:442
  46.9 31.8 %all_to_all.17 = f32[32,1,128]{2,1,0:T(1,128)S(1)} all-to-all(f32[32,1,128]{2,1,0:T(1,128)S(1)} %bitcast.6), channel_id=1, replica_groups=mesh['gx'=8,'gy'=4,'gz'=32] {'gz'}, dimensions={0} | all-to-all | bytes 32768 | tf_op jit(solution)/shard_map/all_to_all | solution.py:556
  78.8 16.1 %all_to_all.18 = f32[32,1,128]{2,1,0:T(1,128)S(1)} all-to-all(f32[32,1,128]{2,1,0:T(1,128)S(1)} %broadcast_in_dim.2), channel_id=1, replica_groups=mesh['gx'=8,'gy'=4,'gz'=32] {'gx','gy'}, dimensions={0} | all-to-all | bytes 32768 | tf_op jit(solution)/shard_map/all_to_all | solution.py:560
  94.9 0.8 shard_map.158
  (37 shorter events, 0.2 us)
Async XLA Ops:
  0.0 1.0 %copy-start = (bf16[9,8,16,128]{3,2,1,0:T(8,128)(2,1)S(1)}, bf16[9,8,16,128]{3,2,1,0:T(8,128)(2,1)}, u32[]{:S(2)}) copy-start(bf16[9,8,16,128]{3,2,1,0:T(8,128)(2,1)} %grads_hbm.1) | copy-start | bytes 884740
  2.6 0.9 copy-start.6
  3.6 0.9 copy-start.10
  4.5 0.9 copy-start.11
  5.4 0.9 copy-start.12
  6.3 39.2 %copy-start.13 = (f32[128,128]{1,0:T(8,128)S(1)}, f32[128,128]{1,0:T(8,128)}, u32[]{:S(2)}) copy-start(f32[128,128]{1,0:T(8,128)} %constant.37.clone.plane_weight) | copy-start | bytes 196612
  6.3 39.2 %copy-start.14 = (f32[128,128]{1,0:T(8,128)S(1)}, f32[128,128]{1,0:T(8,128)}, u32[]{:S(2)}) copy-start(f32[128,128]{1,0:T(8,128)} %constant.36.clone.plane_weight_asm) | copy-start | bytes 196612
  6.3 39.2 %copy-start.15 = (f32[128,128]{1,0:T(8,128)S(1)}, f32[128,128]{1,0:T(8,128)}, u32[]{:S(2)}) copy-start(f32[128,128]{1,0:T(8,128)} %constant.27.clone.share) | copy-start | bytes 196612
  7.8 18.2 %collective-permute-start = (f32[7,16,128]{2,1,0:T(8,128)S(1)}, f32[7,16,128]{2,1,0:T(8,128)S(1)}, u32[]{:S(2)}, u32[]{:S(2)}) collective-permute-start(f32[7,16,128]{2,1,0:T(8,128)S(1)} %get-tuple-element.23), channel_id=1, source_target_pairs={{0,128},{128,256},{256,384},{384,512},{512,640},{640,768},{768,896... | collective-permute-start | bytes 172040 | tf_op jit(solution)/shard_map/ppermute | solution.py:461
  11.8 14.2 %collective-permute-start.1 = (f32[7,16,128]{2,1,0:T(8,128)S(1)}, f32[7,16,128]{2,1,0:T(8,128)S(1)}, u32[]{:S(2)}, u32[]{:S(2)}) collective-permute-start(f32[7,16,128]{2,1,0:T(8,128)S(1)} %get-tuple-element.24), channel_id=1, source_target_pairs={{128,0},{256,128},{384,256},{512,384},{640,512},{768,640},{896,768... | collective-permute-start | bytes 172040 | tf_op jit(solution)/shard_map/ppermute | solution.py:461
  13.1 6.3 %collective-permute-start.2 = (f32[3,16,128]{2,1,0:T(8,128)S(1)}, f32[3,16,128]{2,1,0:T(8,128)S(1)}, u32[]{:S(2)}, u32[]{:S(2)}) collective-permute-start(f32[3,16,128]{2,1,0:T(8,128)S(1)} %get-tuple-element.25), channel_id=1, source_target_pairs={{0,256},{128,384},{256,512},{384,640},{512,768},{640,896},{1,257},... | collective-permute-start | bytes 73736 | tf_op jit(solution)/shard_map/ppermute | solution.py:461
  18.1 7.8 %collective-permute-start.3 = (f32[3,16,128]{2,1,0:T(8,128)S(1)}, f32[3,16,128]{2,1,0:T(8,128)S(1)}, u32[]{:S(2)}, u32[]{:S(2)}) collective-permute-start(f32[3,16,128]{2,1,0:T(8,128)S(1)} %get-tuple-element.26), channel_id=1, source_target_pairs={{256,0},{384,128},{512,256},{640,384},{768,512},{896,640},{257,1},... | collective-permute-start | bytes 73736 | tf_op jit(solution)/shard_map/ppermute | solution.py:461
  26.0 8.1 %copy-start.17 = (f32[8,128]{1,0:T(8,128)S(1)}, f32[8,128]{1,0:T(8,128)}, u32[]{:S(2)}) copy-start(f32[8,128]{1,0:T(8,128)} %constant.30.clone.pick) | copy-start | bytes 12292
  26.0 19.5 %copy-start.7 = (bf16[256,256]{1,0:T(8,128)(2,1)S(1)}, bf16[256,256]{1,0:T(8,128)(2,1)}, u32[]{:S(2)}) copy-start(bf16[256,256]{1,0:T(8,128)(2,1)} %constant.35.clone.line_own) | copy-start | bytes 393220
  26.0 19.5 %copy-start.8 = (bf16[256,256]{1,0:T(8,128)(2,1)S(1)}, bf16[256,256]{1,0:T(8,128)(2,1)}, u32[]{:S(2)}) copy-start(bf16[256,256]{1,0:T(8,128)(2,1)} %constant.34.clone.plane_own) | copy-start | bytes 393220
  26.0 19.5 %copy-start.9 = (bf16[256,256]{1,0:T(8,128)(2,1)S(1)}, bf16[256,256]{1,0:T(8,128)(2,1)}, u32[]{:S(2)}) copy-start(bf16[256,256]{1,0:T(8,128)(2,1)} %constant.33.clone.line_asm) | copy-start | bytes 393220
  26.0 19.4 %copy-start.16 = (bf16[24,256]{1,0:T(8,128)(2,1)S(1)}, bf16[24,256]{1,0:T(8,128)(2,1)}, u32[]{:S(2)}) copy-start(bf16[24,256]{1,0:T(8,128)(2,1)} %constant.31.clone.place) | copy-start | bytes 36868
  26.2 19.3 %copy-start.1 = (bf16[256,512]{1,0:T(8,128)(2,1)S(1)}, bf16[256,512]{1,0:T(8,128)(2,1)}, u32[]{:S(2)}) copy-start(bf16[256,512]{1,0:T(8,128)(2,1)} %constant.32.clone.plane_asm) | copy-start | bytes 786436
  26.2 4.6 %collective-permute-start.4 = (f32[64,128]{1,0:T(8,128)S(1)}, f32[64,128]{1,0:T(8,128)S(1)}, u32[]{:S(2)}, u32[]{:S(2)}) collective-permute-start(f32[64,128]{1,0:T(8,128)S(1)} %get-tuple-element.29), channel_id=1, source_target_pairs={{0,32},{32,64},{64,96},{1,33},{33,65},{65,97},{2,34},{34,66},{66,9... | collective-permute-start | bytes 98312 | tf_op jit(solution)/shard_map/ppermute | solution.py:461
  29.4 4.7 %collective-permute-start.5 = (f32[64,128]{1,0:T(8,128)S(1)}, f32[64,128]{1,0:T(8,128)S(1)}, u32[]{:S(2)}, u32[]{:S(2)}) collective-permute-start(f32[64,128]{1,0:T(8,128)S(1)} %get-tuple-element.30), channel_id=1, source_target_pairs={{32,0},{64,32},{96,64},{33,1},{65,33},{97,65},{34,2},{66,34},{98,6... | collective-permute-start | bytes 98312 | tf_op jit(solution)/shard_map/ppermute | solution.py:461
  34.1 11.4 %copy-start.3 = (f32[8,16,128]{2,1,0:T(8,128)S(1)}, f32[8,16,128]{2,1,0:T(8,128)}, u32[]{:S(2)}) copy-start(f32[8,16,128]{2,1,0:T(8,128)} %sponge.1) | copy-start | bytes 196612
  34.1 11.4 %copy-start.5 = (f32[128,128]{1,0:T(8,128)S(1)}, f32[128,128]{1,0:T(8,128)}, u32[]{:S(2)}) copy-start(f32[128,128]{1,0:T(8,128)} %constant.26.clone.mass_hbm.mass) | copy-start | bytes 196612
  34.6 9.7 %collective-permute-start.7 = (f32[8,896]{1,0:T(8,128)S(1)}, f32[8,896]{1,0:T(8,128)S(1)}, u32[]{:S(2)}, u32[]{:S(2)}) collective-permute-start(f32[8,896]{1,0:T(8,128)S(1)} %get-tuple-element.33), channel_id=1, source_target_pairs={{1,0},{2,1},{3,2},{4,3},{5,4},{6,5},{7,6},{8,7},{9,8},{10,9},{11,1... | collective-permute-start | bytes 86024 | tf_op jit(solution)/shard_map/ppermute | solution.py:461
  42.4 3.1 %collective-permute-start.6 = (f32[8,896]{1,0:T(8,128)S(1)}, f32[8,896]{1,0:T(8,128)S(1)}, u32[]{:S(2)}, u32[]{:S(2)}) collective-permute-start(f32[8,896]{1,0:T(8,128)S(1)} %get-tuple-element.33), channel_id=1, source_target_pairs={{0,1},{1,2},{2,3},{3,4},{4,5},{5,6},{6,7},{7,8},{8,9},{9,10},{10,1... | collective-permute-start | bytes 86024 | tf_op jit(solution)/shard_map/ppermute | solution.py:461
  (2 other events, 1.7 us)

commit v3 on v2

--- a/solution.py
+++ b/solution.py
@@ -439,6 +439,8 @@
     size = sum(4 * int(np.prod(s)) for s in outs) + sum(
         o.dtype.itemsize * o.size for o in operands
     )
+    if fetch:
+        operands = [pltpu.with_memory_space_constraint(o, pltpu.HBM) for o in operands]
     return pl.pallas_call(
         kernel,
         out_shape=shapes,

time: 96.3 us -> 90.2 us (0.937)
  local copies, waits for them, and re-layouts: 6.33 us -> 0.07 us
    unnamed x36 -> x22, local copies, waits for them, and re-layouts: 6.32 us -> 0.06 us
where the time goes in v3:
time: 90.2 us; the launch traced here: 89.8 us
  blocking collectives  47.9 us (53%)
  starting transfers between devices  25.8 us (29%)
  waiting for transfers between devices  11.1 us (12%)
  Pallas kernels  4.76 us (5%)
    all_to_all x1, blocking collectives, body(): sums = lax.all_to_all(sums, 'gz', 0, 0, tiled=True)  31.8 us
    ppermute x8, starting transfers between devices, shift(): return lax.ppermute(x, axis, pairs)  25.8 us
    all_to_all x1, blocking collectives, body(): sums = lax.all_to_all(sums, ('gx', 'gy'), 0, 0, tiled=True)  16.1 us
    ppermute x8, waiting for transfers between devices, shift(): return lax.ppermute(x, axis, pairs)  11.1 us
    pallas_call x5, Pallas kernels, call(): pl.pallas_call(kernel, out_shape=shapes, in_specs=[HBM if fetch else VMEM...  4.76 us
  transfers between devices with their start and end apart: 8, of which 3 were waited for; matrix products, arithmetic and copies ran while one was open for 0% of the time, Pallas kernels for 0%

profile of v3, /device:TPU:1, one launch (start us, length us, event | category | flops | bytes accessed | tf_op | source)
XLA Modules:
  0.0 89.8 jit_solution(9552049533344672512)
XLA Ops:
  0.0 1.9 %shard_map.154 = (f32[3,128,128]{2,1,0:T(8,128)S(1)}, f32[128,128]{1,0:T(8,128)S(1)}, f32[7,16,128]{2,1,0:T(8,128)S(1)}, f32[7,16,128]{2,1,0:T(8,128)S(1)}, f32[...) custom-call(f32[3,8,16,128]{3,2,1,0:T(8,128)} %adj_hbm.1, bf16[3,8,16,128]{3,2,1,0:T(8,128)(2,1)} %flow_hbm.1, ...), custom_call_target="tpu_custom_call" | custom-call | flops 1000000 | bytes 1409024 | tf_op jit(solution)/shard_map/pallas_call | solution.py:444
  1.9 4.0 %collective-permute-start = (f32[7,16,128]{2,1,0:T(8,128)S(1)}, f32[7,16,128]{2,1,0:T(8,128)S(1)}, u32[]{:S(2)}, u32[]{:S(2)}) collective-permute-start(f32[7,16,128]{2,1,0:T(8,128)S(1)} %get-tuple-element.23), channel_id=1, source_target_pairs={{0,128},{128,256},{256,384},{384,512},{512,640},{640,768},{768,896... | collective-permute-start | bytes 172040 | tf_op jit(solution)/shard_map/ppermute | solution.py:463
  5.9 1.3 %collective-permute-start.1 = (f32[7,16,128]{2,1,0:T(8,128)S(1)}, f32[7,16,128]{2,1,0:T(8,128)S(1)}, u32[]{:S(2)}, u32[]{:S(2)}) collective-permute-start(f32[7,16,128]{2,1,0:T(8,128)S(1)} %get-tuple-element.24), channel_id=1, source_target_pairs={{128,0},{256,128},{384,256},{512,384},{640,512},{768,640},{896,768... | collective-permute-start | bytes 172040 | tf_op jit(solution)/shard_map/ppermute | solution.py:463
  7.2 5.0 %collective-permute-start.2 = (f32[3,16,128]{2,1,0:T(8,128)S(1)}, f32[3,16,128]{2,1,0:T(8,128)S(1)}, u32[]{:S(2)}, u32[]{:S(2)}) collective-permute-start(f32[3,16,128]{2,1,0:T(8,128)S(1)} %get-tuple-element.25), channel_id=1, source_target_pairs={{0,256},{128,384},{256,512},{384,640},{512,768},{640,896},{1,257},... | collective-permute-start | bytes 73736 | tf_op jit(solution)/shard_map/ppermute | solution.py:463
  12.2 1.3 %collective-permute-start.3 = (f32[3,16,128]{2,1,0:T(8,128)S(1)}, f32[3,16,128]{2,1,0:T(8,128)S(1)}, u32[]{:S(2)}, u32[]{:S(2)}) collective-permute-start(f32[3,16,128]{2,1,0:T(8,128)S(1)} %get-tuple-element.26), channel_id=1, source_target_pairs={{256,0},{384,128},{512,256},{640,384},{768,512},{896,640},{257,1},... | collective-permute-start | bytes 73736 | tf_op jit(solution)/shard_map/ppermute | solution.py:463
  13.5 6.5 %collective-permute-done.3.from_high2 = f32[3,16,128]{2,1,0:T(8,128)S(1)} collective-permute-done((f32[3,16,128]{2,1,0:T(8,128)S(1)}, f32[3,16,128]{2,1,0:T(8,128)S(1)}, u32[]{:S(2)}, u32[]{:S(2)}) %collective-permute-start.3) | collective-permute-done | bytes 24608 | tf_op jit(solution)/shard_map/ppermute | solution.py:463
  20.1 0.0 copy-start.3
  20.1 0.0 copy-start.4
  20.1 0.0 copy-start.5
  20.1 0.0 copy-start.9
  20.1 0.1 shard_map.155
  20.3 0.0 copy-start
  20.3 3.2 %collective-permute-start.4 = (f32[64,128]{1,0:T(8,128)S(1)}, f32[64,128]{1,0:T(8,128)S(1)}, u32[]{:S(2)}, u32[]{:S(2)}) collective-permute-start(f32[64,128]{1,0:T(8,128)S(1)} %get-tuple-element.29), channel_id=1, source_target_pairs={{0,32},{32,64},{64,96},{1,33},{33,65},{65,97},{2,34},{34,66},{66,9... | collective-permute-start | bytes 98312 | tf_op jit(solution)/shard_map/ppermute | solution.py:463
  23.5 1.3 %collective-permute-start.5 = (f32[64,128]{1,0:T(8,128)S(1)}, f32[64,128]{1,0:T(8,128)S(1)}, u32[]{:S(2)}, u32[]{:S(2)}) collective-permute-start(f32[64,128]{1,0:T(8,128)S(1)} %get-tuple-element.30), channel_id=1, source_target_pairs={{32,0},{64,32},{96,64},{33,1},{65,33},{97,65},{34,2},{66,34},{98,6... | collective-permute-start | bytes 98312 | tf_op jit(solution)/shard_map/ppermute | solution.py:463
  24.8 3.3 %collective-permute-done.5.from_high = f32[64,128]{1,0:T(8,128)S(1)} collective-permute-done((f32[64,128]{1,0:T(8,128)S(1)}, f32[64,128]{1,0:T(8,128)S(1)}, u32[]{:S(2)}, u32[]{:S(2)}) %collective-permute-start.5) | collective-permute-done | bytes 32800 | tf_op jit(solution)/shard_map/ppermute | solution.py:463
  28.2 0.5 shard_map.156
  28.7 7.7 %collective-permute-start.7 = (f32[8,896]{1,0:T(8,128)S(1)}, f32[8,896]{1,0:T(8,128)S(1)}, u32[]{:S(2)}, u32[]{:S(2)}) collective-permute-start(f32[8,896]{1,0:T(8,128)S(1)} %get-tuple-element.33), channel_id=1, source_target_pairs={{1,0},{2,1},{3,2},{4,3},{5,4},{6,5},{7,6},{8,7},{9,8},{10,9},{11,1... | collective-permute-start | bytes 86024 | tf_op jit(solution)/shard_map/ppermute | solution.py:463
  36.4 1.9 %collective-permute-start.6 = (f32[8,896]{1,0:T(8,128)S(1)}, f32[8,896]{1,0:T(8,128)S(1)}, u32[]{:S(2)}, u32[]{:S(2)}) collective-permute-start(f32[8,896]{1,0:T(8,128)S(1)} %get-tuple-element.33), channel_id=1, source_target_pairs={{0,1},{1,2},{2,3},{3,4},{4,5},{5,6},{6,7},{7,8},{8,9},{9,10},{10,1... | collective-permute-start | bytes 86024 | tf_op jit(solution)/shard_map/ppermute | solution.py:463
  38.4 1.1 %collective-permute-done.6.from_low = f32[8,896]{1,0:T(8,128)S(1)} collective-permute-done((f32[8,896]{1,0:T(8,128)S(1)}, f32[8,896]{1,0:T(8,128)S(1)}, u32[]{:S(2)}, u32[]{:S(2)}) %collective-permute-start.6) | collective-permute-done | bytes 28704 | tf_op jit(solution)/shard_map/ppermute | solution.py:463
  39.6 1.4 %shard_map.157 = (f32[3,128,128]{2,1,0:T(8,128)S(1)}, f32[3,128,128]{2,1,0:T(8,128)S(1)}, f32[32,128]{1,0:T(8,128)S(1)}) custom-call(f32[3,256,128]{2,1,0:T(8,128)S(1)} %get-tuple-element.31.ext, f32[128,128]{1,0:T(8,128)S(1)} %get-tuple-element.32.drag, f32[8,16,128]{2,1,0:T(8,128)S(1)} %copy-done.1, f32[8,896]{1,0:T(8,128)S(1)} %collective-permute-done.6.from_low, ...), custom_call_target="tpu_custom_call" | custom-call | flops 1000000 | bytes 1921024 | tf_op jit(solution)/shard_map/pallas_call | solution.py:444
  41.0 31.8 %all_to_all.17 = f32[32,1,128]{2,1,0:T(1,128)S(1)} all-to-all(f32[32,1,128]{2,1,0:T(1,128)S(1)} %bitcast.6), channel_id=1, replica_groups=mesh['gx'=8,'gy'=4,'gz'=32] {'gz'}, dimensions={0} | all-to-all | bytes 32768 | tf_op jit(solution)/shard_map/all_to_all | solution.py:558
  72.8 0.1 reduce_sum.9
  72.9 16.1 %all_to_all.18 = f32[32,1,128]{2,1,0:T(1,128)S(1)} all-to-all(f32[32,1,128]{2,1,0:T(1,128)S(1)} %broadcast_in_dim.2), channel_id=1, replica_groups=mesh['gx'=8,'gy'=4,'gz'=32] {'gx','gy'}, dimensions={0} | all-to-all | bytes 32768 | tf_op jit(solution)/shard_map/all_to_all | solution.py:562
  89.0 0.8 shard_map.158
  (23 shorter events, 0.1 us)
Async XLA Ops:
  0.0 39.5 %copy-start.6 = (f32[128,128]{1,0:T(8,128)S(1)}, f32[128,128]{1,0:T(8,128)}, u32[]{:S(2)}) copy-start(f32[128,128]{1,0:T(8,128)} %constant.37.clone.plane_weight) | copy-start | bytes 196612
  0.0 39.5 %copy-start.7 = (f32[128,128]{1,0:T(8,128)S(1)}, f32[128,128]{1,0:T(8,128)}, u32[]{:S(2)}) copy-start(f32[128,128]{1,0:T(8,128)} %constant.36.clone.plane_weight_asm) | copy-start | bytes 196612
  0.0 39.5 %copy-start.8 = (f32[128,128]{1,0:T(8,128)S(1)}, f32[128,128]{1,0:T(8,128)}, u32[]{:S(2)}) copy-start(f32[128,128]{1,0:T(8,128)} %constant.27.clone.share) | copy-start | bytes 196612
  1.9 18.2 %collective-permute-start = (f32[7,16,128]{2,1,0:T(8,128)S(1)}, f32[7,16,128]{2,1,0:T(8,128)S(1)}, u32[]{:S(2)}, u32[]{:S(2)}) collective-permute-start(f32[7,16,128]{2,1,0:T(8,128)S(1)} %get-tuple-element.23), channel_id=1, source_target_pairs={{0,128},{128,256},{256,384},{384,512},{512,640},{640,768},{768,896... | collective-permute-start | bytes 172040 | tf_op jit(solution)/shard_map/ppermute | solution.py:463
  5.9 14.2 %collective-permute-start.1 = (f32[7,16,128]{2,1,0:T(8,128)S(1)}, f32[7,16,128]{2,1,0:T(8,128)S(1)}, u32[]{:S(2)}, u32[]{:S(2)}) collective-permute-start(f32[7,16,128]{2,1,0:T(8,128)S(1)} %get-tuple-element.24), channel_id=1, source_target_pairs={{128,0},{256,128},{384,256},{512,384},{640,512},{768,640},{896,768... | collective-permute-start | bytes 172040 | tf_op jit(solution)/shard_map/ppermute | solution.py:463
  7.2 6.3 %collective-permute-start.2 = (f32[3,16,128]{2,1,0:T(8,128)S(1)}, f32[3,16,128]{2,1,0:T(8,128)S(1)}, u32[]{:S(2)}, u32[]{:S(2)}) collective-permute-start(f32[3,16,128]{2,1,0:T(8,128)S(1)} %get-tuple-element.25), channel_id=1, source_target_pairs={{0,256},{128,384},{256,512},{384,640},{512,768},{640,896},{1,257},... | collective-permute-start | bytes 73736 | tf_op jit(solution)/shard_map/ppermute | solution.py:463
  12.2 7.9 %collective-permute-start.3 = (f32[3,16,128]{2,1,0:T(8,128)S(1)}, f32[3,16,128]{2,1,0:T(8,128)S(1)}, u32[]{:S(2)}, u32[]{:S(2)}) collective-permute-start(f32[3,16,128]{2,1,0:T(8,128)S(1)} %get-tuple-element.26), channel_id=1, source_target_pairs={{256,0},{384,128},{512,256},{640,384},{768,512},{896,640},{257,1},... | collective-permute-start | bytes 73736 | tf_op jit(solution)/shard_map/ppermute | solution.py:463
  20.1 8.1 %copy-start.10 = (f32[8,128]{1,0:T(8,128)S(1)}, f32[8,128]{1,0:T(8,128)}, u32[]{:S(2)}) copy-start(f32[8,128]{1,0:T(8,128)} %constant.30.clone.pick) | copy-start | bytes 12292
  20.1 19.5 %copy-start.3 = (bf16[256,256]{1,0:T(8,128)(2,1)S(1)}, bf16[256,256]{1,0:T(8,128)(2,1)}, u32[]{:S(2)}) copy-start(bf16[256,256]{1,0:T(8,128)(2,1)} %constant.35.clone.line_own) | copy-start | bytes 393220
  20.1 19.4 %copy-start.4 = (bf16[256,256]{1,0:T(8,128)(2,1)S(1)}, bf16[256,256]{1,0:T(8,128)(2,1)}, u32[]{:S(2)}) copy-start(bf16[256,256]{1,0:T(8,128)(2,1)} %constant.34.clone.plane_own) | copy-start | bytes 393220
  20.1 19.4 %copy-start.5 = (bf16[256,256]{1,0:T(8,128)(2,1)S(1)}, bf16[256,256]{1,0:T(8,128)(2,1)}, u32[]{:S(2)}) copy-start(bf16[256,256]{1,0:T(8,128)(2,1)} %constant.33.clone.line_asm) | copy-start | bytes 393220
  20.1 19.4 %copy-start.9 = (bf16[24,256]{1,0:T(8,128)(2,1)S(1)}, bf16[24,256]{1,0:T(8,128)(2,1)}, u32[]{:S(2)}) copy-start(bf16[24,256]{1,0:T(8,128)(2,1)} %constant.31.clone.place) | copy-start | bytes 36868
  20.3 19.3 %copy-start = (bf16[256,512]{1,0:T(8,128)(2,1)S(1)}, bf16[256,512]{1,0:T(8,128)(2,1)}, u32[]{:S(2)}) copy-start(bf16[256,512]{1,0:T(8,128)(2,1)} %constant.32.clone.plane_asm) | copy-start | bytes 786436
  20.3 4.6 %collective-permute-start.4 = (f32[64,128]{1,0:T(8,128)S(1)}, f32[64,128]{1,0:T(8,128)S(1)}, u32[]{:S(2)}, u32[]{:S(2)}) collective-permute-start(f32[64,128]{1,0:T(8,128)S(1)} %get-tuple-element.29), channel_id=1, source_target_pairs={{0,32},{32,64},{64,96},{1,33},{33,65},{65,97},{2,34},{34,66},{66,9... | collective-permute-start | bytes 98312 | tf_op jit(solution)/shard_map/ppermute | solution.py:463
  23.5 4.7 %collective-permute-start.5 = (f32[64,128]{1,0:T(8,128)S(1)}, f32[64,128]{1,0:T(8,128)S(1)}, u32[]{:S(2)}, u32[]{:S(2)}) collective-permute-start(f32[64,128]{1,0:T(8,128)S(1)} %get-tuple-element.30), channel_id=1, source_target_pairs={{32,0},{64,32},{96,64},{33,1},{65,33},{97,65},{34,2},{66,34},{98,6... | collective-permute-start | bytes 98312 | tf_op jit(solution)/shard_map/ppermute | solution.py:463
  28.2 11.4 %copy-start.1 = (f32[8,16,128]{2,1,0:T(8,128)S(1)}, f32[8,16,128]{2,1,0:T(8,128)}, u32[]{:S(2)}) copy-start(f32[8,16,128]{2,1,0:T(8,128)} %sponge.1) | copy-start | bytes 196612
  28.2 11.4 %copy-start.2 = (f32[128,128]{1,0:T(8,128)S(1)}, f32[128,128]{1,0:T(8,128)}, u32[]{:S(2)}) copy-start(f32[128,128]{1,0:T(8,128)} %constant.26.clone.mass_hbm.mass) | copy-start | bytes 196612
  28.7 9.7 %collective-permute-start.7 = (f32[8,896]{1,0:T(8,128)S(1)}, f32[8,896]{1,0:T(8,128)S(1)}, u32[]{:S(2)}, u32[]{:S(2)}) collective-permute-start(f32[8,896]{1,0:T(8,128)S(1)} %get-tuple-element.33), channel_id=1, source_target_pairs={{1,0},{2,1},{3,2},{4,3},{5,4},{6,5},{7,6},{8,7},{9,8},{10,9},{11,1... | collective-permute-start | bytes 86024 | tf_op jit(solution)/shard_map/ppermute | solution.py:463
  36.4 3.1 %collective-permute-start.6 = (f32[8,896]{1,0:T(8,128)S(1)}, f32[8,896]{1,0:T(8,128)S(1)}, u32[]{:S(2)}, u32[]{:S(2)}) collective-permute-start(f32[8,896]{1,0:T(8,128)S(1)} %get-tuple-element.33), channel_id=1, source_target_pairs={{0,1},{1,2},{2,3},{3,4},{4,5},{5,6},{6,7},{7,8},{8,9},{9,10},{10,1... | collective-permute-start | bytes 86024 | tf_op jit(solution)/shard_map/ppermute | solution.py:463

commit v4 on v3

--- a/solution.py
+++ b/solution.py
@@ -155,8 +155,6 @@
     drag,
     right,
     left,
-    right2,
-    left2,
     adj,
     flow,
     grads,
@@ -183,18 +181,22 @@
     for copy in copies:
         copy.start()
     ix = lax.axis_index("gx")
-    for copy in copies:
-        copy.wait()
+    copies[0].wait()
     a = adj[...]
     _, sx, sy, sz = a.shape
     rows = sx * sy
+    copies[1].wait()
+    grad_z = mul_right(a.reshape(3 * rows, sz), dz[...]).reshape(3, rows, sz)
+    copies[2].wait()
+    copies[3].wait()
     m = mass[...]
-    grad_z = mul_right(a.reshape(3 * rows, sz), dz[...]).reshape(3, rows, sz)
     s_local = m * (inverse_step + sponge[...].reshape(rows, sz))
     s_asm = twin_z(twin_y(s_local.reshape(sx, sy, sz)).reshape(rows, sz))
     drag[...] = s_asm
     right[6] = s_asm[(sx - 1) * sy :]
     left[6] = s_asm[:sy]
+    for copy in copies[4:]:
+        copy.wait()
     fl = [flow[j].astype(F32).reshape(rows, sz) for j in range(3)]
     flat = a.reshape(3, rows, sz)
     low_edge = jnp.where(ix == 0, 0.0, float(K1[7, 0])).astype(F32)
@@ -227,8 +229,6 @@
         right[3 + c] = up
         left[c] = plane[0]
         left[3 + c] = down
-        right2[c] = plane[sx - 1]
-        left2[c] = plane[0]
 
 
 def x_stage_kernel(
@@ -487,16 +487,16 @@
     )
     dy = jnp.asarray(left_operand(block_diag(D1, rows // NODES)))
     dz = jnp.asarray(right_operand(block_diag(D1, sz // NODES).T))
-    field, drag, right, left, right2, left2 = call(
+    field, drag, right, left = call(
         functools.partial(forcing_kernel, counts["gx"]),
         (adjoint_state, base_flow, base_grads, sponge, mass, dy, dz),
-        [(3, rows, sz), (rows, sz)] + [(7, sy, sz)] * 2 + [(3, sy, sz)] * 2,
+        [(3, rows, sz), (rows, sz)] + [(7, sy, sz)] * 2,
         fetch=True,
     )
-    x_low2 = shift(right2, "gx", 2)
-    x_high2 = shift(left2, "gx", -2)
     x_low = shift(right, "gx", 1)
+    x_low2 = shift(right, "gx", 2)
     x_high = shift(left, "gx", -1)
+    x_high2 = shift(left, "gx", -2)
     message_rows = 7 * sx + 8
     ext, drag, up, down = call(
         x_stage_kernel,

time: 90.2 us -> 89.5 us (level)
  waiting for transfers between devices: 11.1 us -> 9.17 us
  starting transfers between devices: 25.8 us -> 27.3 us
    all_to_all x1, blocking collectives: 31.8 us -> 29.2 us  [body(): sums = lax.all_to_all(sums, 'gz', 0, 0, tiled=True)]
    all_to_all x1, blocking collectives: 16.1 us -> 18.3 us  [body(): sums = lax.all_to_all(sums, ('gx', 'gy'), 0, 0, tiled=True)]
    ppermute x8, waiting for transfers between devices: 11.1 us -> 9.17 us  [shift(): return lax.ppermute(x, axis, pairs)]
    ppermute x8, starting transfers between devices: 25.8 us -> 27.3 us  [shift(): return lax.ppermute(x, axis, pairs)]
  transfers between devices with their start and end apart: 8 -> 8, of which waited for: 3 -> 4; matrix products, arithmetic and copies ran while one was open for 0% -> 0% of each run, Pallas kernels for 0% -> 0%
where the time goes in v4:
time: 89.5 us; the launch traced here: 89.1 us
  blocking collectives  47.5 us (53%)
  starting transfers between devices  27.3 us (31%)
  waiting for transfers between devices  9.17 us (10%)
  Pallas kernels  4.82 us (5%)
    all_to_all x1, blocking collectives, body(): sums = lax.all_to_all(sums, 'gz', 0, 0, tiled=True)  29.2 us
    ppermute x8, starting transfers between devices, shift(): return lax.ppermute(x, axis, pairs)  27.3 us
    all_to_all x1, blocking collectives, body(): sums = lax.all_to_all(sums, ('gx', 'gy'), 0, 0, tiled=True)  18.3 us
    ppermute x8, waiting for transfers between devices, shift(): return lax.ppermute(x, axis, pairs)  9.17 us
    pallas_call x5, Pallas kernels, call(): pl.pallas_call(kernel, out_shape=shapes, in_specs=[HBM if fetch else VMEM...  4.82 us
  transfers between devices with their start and end apart: 8, of which 4 were waited for; matrix products, arithmetic and copies ran while one was open for 0% of the time, Pallas kernels for 0%

profile of v4, /device:TPU:1, one launch (start us, length us, event | category | flops | bytes accessed | tf_op | source)
XLA Modules:
  0.0 89.1 jit_solution(12660955301202349380)
XLA Ops:
  0.0 1.9 %shard_map.154 = (f32[3,128,128]{2,1,0:T(8,128)S(1)}, f32[128,128]{1,0:T(8,128)S(1)}, f32[7,16,128]{2,1,0:T(8,128)S(1)}, f32[7,16,128]{2,1,0:T(8,128)S(1)}) custom-call(f32[3,8,16,128]{3,2,1,0:T(8,128)} %adj_hbm.1, bf16[3,8,16,128]{3,2,1,0:T(8,128)(2,1)} %flow_hbm.1, bf16[9,8,16,128]{3,2,1,0:T(8,128)(2,1)} %grads_hbm.1, f32[8,16,128]{2,1,0:T(8,128)} %sponge.1, ...), custom_call_target="tpu_custom_call" | custom-call | flops 1000000 | bytes 1359872 | tf_op jit(solution)/shard_map/pallas_call | solution.py:444
  1.9 5.0 %collective-permute-start.2 = (f32[7,16,128]{2,1,0:T(8,128)S(1)}, f32[7,16,128]{2,1,0:T(8,128)S(1)}, u32[]{:S(2)}, u32[]{:S(2)}) collective-permute-start(f32[7,16,128]{2,1,0:T(8,128)S(1)} %get-tuple-element.21), channel_id=1, source_target_pairs={{0,256},{128,384},{256,512},{384,640},{512,768},{640,896},{1,257},... | collective-permute-start | bytes 172040 | tf_op jit(solution)/shard_map/ppermute | solution.py:463
  7.0 3.2 %collective-permute-start = (f32[7,16,128]{2,1,0:T(8,128)S(1)}, f32[7,16,128]{2,1,0:T(8,128)S(1)}, u32[]{:S(2)}, u32[]{:S(2)}) collective-permute-start(f32[7,16,128]{2,1,0:T(8,128)S(1)} %get-tuple-element.21), channel_id=1, source_target_pairs={{0,128},{128,256},{256,384},{384,512},{512,640},{640,768},{768,896... | collective-permute-start | bytes 172040 | tf_op jit(solution)/shard_map/ppermute | solution.py:463
  10.2 1.3 %collective-permute-start.3 = (f32[7,16,128]{2,1,0:T(8,128)S(1)}, f32[7,16,128]{2,1,0:T(8,128)S(1)}, u32[]{:S(2)}, u32[]{:S(2)}) collective-permute-start(f32[7,16,128]{2,1,0:T(8,128)S(1)} %get-tuple-element.22), channel_id=1, source_target_pairs={{256,0},{384,128},{512,256},{640,384},{768,512},{896,640},{257,1},... | collective-permute-start | bytes 172040 | tf_op jit(solution)/shard_map/ppermute | solution.py:463
  11.5 1.3 %collective-permute-start.1 = (f32[7,16,128]{2,1,0:T(8,128)S(1)}, f32[7,16,128]{2,1,0:T(8,128)S(1)}, u32[]{:S(2)}, u32[]{:S(2)}) collective-permute-start(f32[7,16,128]{2,1,0:T(8,128)S(1)} %get-tuple-element.22), channel_id=1, source_target_pairs={{128,0},{256,128},{384,256},{512,384},{640,512},{768,640},{896,768... | collective-permute-start | bytes 172040 | tf_op jit(solution)/shard_map/ppermute | solution.py:463
  12.8 0.0 collective-permute-done.2.from_low2
  12.8 3.5 %collective-permute-done.3.from_high2 = f32[7,16,128]{2,1,0:T(8,128)S(1)} collective-permute-done((f32[7,16,128]{2,1,0:T(8,128)S(1)}, f32[7,16,128]{2,1,0:T(8,128)S(1)}, u32[]{:S(2)}, u32[]{:S(2)}) %collective-permute-start.3) | collective-permute-done | bytes 57376 | tf_op jit(solution)/shard_map/ppermute | solution.py:463
  16.3 1.2 %collective-permute-done.1.from_high = f32[7,16,128]{2,1,0:T(8,128)S(1)} collective-permute-done((f32[7,16,128]{2,1,0:T(8,128)S(1)}, f32[7,16,128]{2,1,0:T(8,128)S(1)}, u32[]{:S(2)}, u32[]{:S(2)}) %collective-permute-start.1) | collective-permute-done | bytes 57376 | tf_op jit(solution)/shard_map/ppermute | solution.py:463
  17.5 0.0 copy-start.6
  17.5 0.0 copy-start.9
  17.5 0.1 shard_map.155
  17.6 0.0 copy-start
  17.6 3.9 %collective-permute-start.4 = (f32[64,128]{1,0:T(8,128)S(1)}, f32[64,128]{1,0:T(8,128)S(1)}, u32[]{:S(2)}, u32[]{:S(2)}) collective-permute-start(f32[64,128]{1,0:T(8,128)S(1)} %get-tuple-element.25), channel_id=1, source_target_pairs={{0,32},{32,64},{64,96},{1,33},{33,65},{65,97},{2,34},{34,66},{66,9... | collective-permute-start | bytes 98312 | tf_op jit(solution)/shard_map/ppermute | solution.py:463
  21.5 1.3 %collective-permute-start.5 = (f32[64,128]{1,0:T(8,128)S(1)}, f32[64,128]{1,0:T(8,128)S(1)}, u32[]{:S(2)}, u32[]{:S(2)}) collective-permute-start(f32[64,128]{1,0:T(8,128)S(1)} %get-tuple-element.26), channel_id=1, source_target_pairs={{32,0},{64,32},{96,64},{33,1},{65,33},{97,65},{34,2},{66,34},{98,6... | collective-permute-start | bytes 98312 | tf_op jit(solution)/shard_map/ppermute | solution.py:463
  22.8 3.3 %collective-permute-done.5.from_high = f32[64,128]{1,0:T(8,128)S(1)} collective-permute-done((f32[64,128]{1,0:T(8,128)S(1)}, f32[64,128]{1,0:T(8,128)S(1)}, u32[]{:S(2)}, u32[]{:S(2)}) %collective-permute-start.5) | collective-permute-done | bytes 32800 | tf_op jit(solution)/shard_map/ppermute | solution.py:463
  26.2 0.5 shard_map.156
  26.7 9.4 %collective-permute-start.7 = (f32[8,896]{1,0:T(8,128)S(1)}, f32[8,896]{1,0:T(8,128)S(1)}, u32[]{:S(2)}, u32[]{:S(2)}) collective-permute-start(f32[8,896]{1,0:T(8,128)S(1)} %get-tuple-element.29), channel_id=1, source_target_pairs={{1,0},{2,1},{3,2},{4,3},{5,4},{6,5},{7,6},{8,7},{9,8},{10,9},{11,1... | collective-permute-start | bytes 86024 | tf_op jit(solution)/shard_map/ppermute | solution.py:463
  36.1 1.9 %collective-permute-start.6 = (f32[8,896]{1,0:T(8,128)S(1)}, f32[8,896]{1,0:T(8,128)S(1)}, u32[]{:S(2)}, u32[]{:S(2)}) collective-permute-start(f32[8,896]{1,0:T(8,128)S(1)} %get-tuple-element.29), channel_id=1, source_target_pairs={{0,1},{1,2},{2,3},{3,4},{4,5},{5,6},{6,7},{7,8},{8,9},{9,10},{10,1... | collective-permute-start | bytes 86024 | tf_op jit(solution)/shard_map/ppermute | solution.py:463
  38.1 1.2 %collective-permute-done.6.from_low = f32[8,896]{1,0:T(8,128)S(1)} collective-permute-done((f32[8,896]{1,0:T(8,128)S(1)}, f32[8,896]{1,0:T(8,128)S(1)}, u32[]{:S(2)}, u32[]{:S(2)}) %collective-permute-start.6) | collective-permute-done | bytes 28704 | tf_op jit(solution)/shard_map/ppermute | solution.py:463
  39.3 1.4 %shard_map.157 = (f32[3,128,128]{2,1,0:T(8,128)S(1)}, f32[3,128,128]{2,1,0:T(8,128)S(1)}, f32[32,128]{1,0:T(8,128)S(1)}) custom-call(f32[3,256,128]{2,1,0:T(8,128)S(1)} %get-tuple-element.27.ext, f32[128,128]{1,0:T(8,128)S(1)} %get-tuple-element.28.drag, f32[8,16,128]{2,1,0:T(8,128)S(1)} %copy-done.1, f32[8,896]{1,0:T(8,128)S(1)} %collective-permute-done.6.from_low, ...), custom_call_target="tpu_custom_call" | custom-call | flops 1000000 | bytes 1921024 | tf_op jit(solution)/shard_map/pallas_call | solution.py:444
  40.7 29.2 %all_to_all.17 = f32[32,1,128]{2,1,0:T(1,128)S(1)} all-to-all(f32[32,1,128]{2,1,0:T(1,128)S(1)} %bitcast.6), channel_id=1, replica_groups=mesh['gx'=8,'gy'=4,'gz'=32] {'gz'}, dimensions={0} | all-to-all | bytes 32768 | tf_op jit(solution)/shard_map/all_to_all | solution.py:558
  69.9 0.1 reduce_sum.9
  70.0 18.3 %all_to_all.18 = f32[32,1,128]{2,1,0:T(1,128)S(1)} all-to-all(f32[32,1,128]{2,1,0:T(1,128)S(1)} %broadcast_in_dim.2), channel_id=1, replica_groups=mesh['gx'=8,'gy'=4,'gz'=32] {'gx','gy'}, dimensions={0} | all-to-all | bytes 32768 | tf_op jit(solution)/shard_map/all_to_all | solution.py:562
  88.3 0.8 shard_map.158
  (23 shorter events, 0.1 us)
Async XLA Ops:
  0.0 39.2 %copy-start.7 = (f32[128,128]{1,0:T(8,128)S(1)}, f32[128,128]{1,0:T(8,128)}, u32[]{:S(2)}) copy-start(f32[128,128]{1,0:T(8,128)} %constant.36.clone.plane_weight_asm) | copy-start | bytes 196612
  0.0 39.2 %copy-start.8 = (f32[128,128]{1,0:T(8,128)S(1)}, f32[128,128]{1,0:T(8,128)}, u32[]{:S(2)}) copy-start(f32[128,128]{1,0:T(8,128)} %constant.27.clone.share) | copy-start | bytes 196612
  1.9 10.9 %collective-permute-start.2 = (f32[7,16,128]{2,1,0:T(8,128)S(1)}, f32[7,16,128]{2,1,0:T(8,128)S(1)}, u32[]{:S(2)}, u32[]{:S(2)}) collective-permute-start(f32[7,16,128]{2,1,0:T(8,128)S(1)} %get-tuple-element.21), channel_id=1, source_target_pairs={{0,256},{128,384},{256,512},{384,640},{512,768},{640,896},{1,257},... | collective-permute-start | bytes 172040 | tf_op jit(solution)/shard_map/ppermute | solution.py:463
  7.0 5.8 %collective-permute-start = (f32[7,16,128]{2,1,0:T(8,128)S(1)}, f32[7,16,128]{2,1,0:T(8,128)S(1)}, u32[]{:S(2)}, u32[]{:S(2)}) collective-permute-start(f32[7,16,128]{2,1,0:T(8,128)S(1)} %get-tuple-element.21), channel_id=1, source_target_pairs={{0,128},{128,256},{256,384},{384,512},{512,640},{640,768},{768,896... | collective-permute-start | bytes 172040 | tf_op jit(solution)/shard_map/ppermute | solution.py:463
  10.2 6.1 %collective-permute-start.3 = (f32[7,16,128]{2,1,0:T(8,128)S(1)}, f32[7,16,128]{2,1,0:T(8,128)S(1)}, u32[]{:S(2)}, u32[]{:S(2)}) collective-permute-start(f32[7,16,128]{2,1,0:T(8,128)S(1)} %get-tuple-element.22), channel_id=1, source_target_pairs={{256,0},{384,128},{512,256},{640,384},{768,512},{896,640},{257,1},... | collective-permute-start | bytes 172040 | tf_op jit(solution)/shard_map/ppermute | solution.py:463
  11.5 6.0 %collective-permute-start.1 = (f32[7,16,128]{2,1,0:T(8,128)S(1)}, f32[7,16,128]{2,1,0:T(8,128)S(1)}, u32[]{:S(2)}, u32[]{:S(2)}) collective-permute-start(f32[7,16,128]{2,1,0:T(8,128)S(1)} %get-tuple-element.22), channel_id=1, source_target_pairs={{128,0},{256,128},{384,256},{512,384},{640,512},{768,640},{896,768... | collective-permute-start | bytes 172040 | tf_op jit(solution)/shard_map/ppermute | solution.py:463
  17.5 8.7 %copy-start.10 = (f32[8,128]{1,0:T(8,128)S(1)}, f32[8,128]{1,0:T(8,128)}, u32[]{:S(2)}) copy-start(f32[8,128]{1,0:T(8,128)} %constant.30.clone.pick) | copy-start | bytes 12292
  17.5 21.8 %copy-start.3 = (bf16[256,256]{1,0:T(8,128)(2,1)S(1)}, bf16[256,256]{1,0:T(8,128)(2,1)}, u32[]{:S(2)}) copy-start(bf16[256,256]{1,0:T(8,128)(2,1)} %constant.35.clone.line_own) | copy-start | bytes 393220
  17.5 21.8 %copy-start.4 = (bf16[256,256]{1,0:T(8,128)(2,1)S(1)}, bf16[256,256]{1,0:T(8,128)(2,1)}, u32[]{:S(2)}) copy-start(bf16[256,256]{1,0:T(8,128)(2,1)} %constant.34.clone.plane_own) | copy-start | bytes 393220
  17.5 21.8 %copy-start.5 = (bf16[256,256]{1,0:T(8,128)(2,1)S(1)}, bf16[256,256]{1,0:T(8,128)(2,1)}, u32[]{:S(2)}) copy-start(bf16[256,256]{1,0:T(8,128)(2,1)} %constant.33.clone.line_asm) | copy-start | bytes 393220
  17.5 21.8 %copy-start.6 = (f32[128,128]{1,0:T(8,128)S(1)}, f32[128,128]{1,0:T(8,128)}, u32[]{:S(2)}) copy-start(f32[128,128]{1,0:T(8,128)} %constant.37.clone.plane_weight) | copy-start | bytes 196612
  17.5 21.8 %copy-start.9 = (bf16[24,256]{1,0:T(8,128)(2,1)S(1)}, bf16[24,256]{1,0:T(8,128)(2,1)}, u32[]{:S(2)}) copy-start(bf16[24,256]{1,0:T(8,128)(2,1)} %constant.31.clone.place) | copy-start | bytes 36868
  17.6 21.7 %copy-start = (bf16[256,512]{1,0:T(8,128)(2,1)S(1)}, bf16[256,512]{1,0:T(8,128)(2,1)}, u32[]{:S(2)}) copy-start(bf16[256,512]{1,0:T(8,128)(2,1)} %constant.32.clone.plane_asm) | copy-start | bytes 786436
  17.6 5.2 %collective-permute-start.4 = (f32[64,128]{1,0:T(8,128)S(1)}, f32[64,128]{1,0:T(8,128)S(1)}, u32[]{:S(2)}, u32[]{:S(2)}) collective-permute-start(f32[64,128]{1,0:T(8,128)S(1)} %get-tuple-element.25), channel_id=1, source_target_pairs={{0,32},{32,64},{64,96},{1,33},{33,65},{65,97},{2,34},{34,66},{66,9... | collective-permute-start | bytes 98312 | tf_op jit(solution)/shard_map/ppermute | solution.py:463
  21.5 4.7 %collective-permute-start.5 = (f32[64,128]{1,0:T(8,128)S(1)}, f32[64,128]{1,0:T(8,128)S(1)}, u32[]{:S(2)}, u32[]{:S(2)}) collective-permute-start(f32[64,128]{1,0:T(8,128)S(1)} %get-tuple-element.26), channel_id=1, source_target_pairs={{32,0},{64,32},{96,64},{33,1},{65,33},{97,65},{34,2},{66,34},{98,6... | collective-permute-start | bytes 98312 | tf_op jit(solution)/shard_map/ppermute | solution.py:463
  26.2 13.1 %copy-start.1 = (f32[8,16,128]{2,1,0:T(8,128)S(1)}, f32[8,16,128]{2,1,0:T(8,128)}, u32[]{:S(2)}) copy-start(f32[8,16,128]{2,1,0:T(8,128)} %sponge.1) | copy-start | bytes 196612
  26.2 13.1 %copy-start.2 = (f32[128,128]{1,0:T(8,128)S(1)}, f32[128,128]{1,0:T(8,128)}, u32[]{:S(2)}) copy-start(f32[128,128]{1,0:T(8,128)} %constant.26.clone.mass_hbm.mass) | copy-start | bytes 196612
  26.7 11.4 %collective-permute-start.7 = (f32[8,896]{1,0:T(8,128)S(1)}, f32[8,896]{1,0:T(8,128)S(1)}, u32[]{:S(2)}, u32[]{:S(2)}) collective-permute-start(f32[8,896]{1,0:T(8,128)S(1)} %get-tuple-element.29), channel_id=1, source_target_pairs={{1,0},{2,1},{3,2},{4,3},{5,4},{6,5},{7,6},{8,7},{9,8},{10,9},{11,1... | collective-permute-start | bytes 86024 | tf_op jit(solution)/shard_map/ppermute | solution.py:463
  36.1 3.1 %collective-permute-start.6 = (f32[8,896]{1,0:T(8,128)S(1)}, f32[8,896]{1,0:T(8,128)S(1)}, u32[]{:S(2)}, u32[]{:S(2)}) collective-permute-start(f32[8,896]{1,0:T(8,128)S(1)} %get-tuple-element.29), channel_id=1, source_target_pairs={{0,1},{1,2},{2,3},{3,4},{4,5},{5,6},{6,7},{7,8},{8,9},{9,10},{10,1... | collective-permute-start | bytes 86024 | tf_op jit(solution)/shard_map/ppermute | solution.py:463

commit v5 on v4

--- a/solution.py
+++ b/solution.py
@@ -142,8 +142,81 @@
     return jnp.concatenate([one, two], 1)
 
 
+def member(axis):
+    return (lax.axis_index(axis) & 1) == 0
+
+
+def has_neighbour(axis, high, count):
+    here = lax.axis_index(axis)
+    return jnp.where(high, here < count - 1, here > 0)
+
+
+def slot_of(x, z):
+    return 2 * x + z
+
+
+def as_number(flag):
+    return jnp.where(flag, 1, 0)
+
+
+def turned(pick, tile):
+    return lax.dot_general(
+        pick,
+        tile,
+        (((1,), (1,)), ((), ())),
+        precision=lax.Precision.HIGHEST,
+        preferred_element_type=F32,
+    )
+
+
+def spread(tiles, place):
+    both = jnp.concatenate(tiles, 1)
+    high = both.astype(BF16)
+    rest = both - high.astype(F32)
+    mid = rest.astype(BF16)
+    low = (rest - mid.astype(F32)).astype(BF16)
+    parts = jnp.concatenate([high, mid, low], 0)
+    return lax.dot_general(
+        parts, place, (((0,), (0,)), ((), ())), preferred_element_type=F32
+    )
+
+
+def picked(tile, high, ok):
+    row = lax.broadcasted_iota(jnp.int32, tile.shape, 0)
+    start = jnp.where(high, 2, 0)
+    use = (row >= start) & (row < start + 2) & ok
+    return jnp.where(use, tile, 0.0)
+
+
+def face_of(x, high, size):
+    return jnp.where(high, x[-size:], x[:size])
+
+
+def facing(face, high, rows):
+    gap = jnp.zeros((rows - face.shape[0], face.shape[1]), F32)
+    return jnp.where(
+        high, jnp.concatenate([face, gap], 0), jnp.concatenate([gap, face], 0)
+    )
+
+
+def contraction(x, high, size, nx):
+    ix = lax.axis_index("gx")
+    count = x.shape[0] // size
+    total = None
+    for i in range(count):
+        upper = 0.0 if i == count - 1 else float(K1[7, i])
+        lower = 0.0 if i == 0 else float(K1[0, i])
+        scale = jnp.where(high, upper, lower).astype(F32)
+        if i == 0:
+            scale = jnp.where(ix == 0, 0.0, scale)
+        if i == count - 1:
+            scale = jnp.where(ix == nx - 1, 0.0, scale)
+        term = scale * x[i * size : (i + 1) * size]
+        total = term if total is None else total + term
+    return total
+
+
 def forcing_kernel(
-    nx,
     adj_hbm,
     flow_hbm,
     grads_hbm,
@@ -151,10 +224,10 @@
     mass_hbm,
     dy_hbm,
     dz_hbm,
+    pick_hbm,
     field,
     drag,
-    right,
-    left,
+    slots,
     adj,
     flow,
     grads,
@@ -162,6 +235,7 @@
     mass,
     dy,
     dz,
+    pick,
     sems,
 ):
     copies = [
@@ -175,32 +249,28 @@
                 (dy_hbm, dy),
                 (flow_hbm, flow),
                 (grads_hbm, grads),
+                (pick_hbm, pick),
             )
         )
     ]
     for copy in copies:
         copy.start()
-    ix = lax.axis_index("gx")
+    slots[...] = jnp.zeros(slots.shape, F32)
     copies[0].wait()
     a = adj[...]
     _, sx, sy, sz = a.shape
     rows = sx * sy
     copies[1].wait()
     grad_z = mul_right(a.reshape(3 * rows, sz), dz[...]).reshape(3, rows, sz)
-    copies[2].wait()
-    copies[3].wait()
+    for copy in copies[2:]:
+        copy.wait()
     m = mass[...]
     s_local = m * (inverse_step + sponge[...].reshape(rows, sz))
     s_asm = twin_z(twin_y(s_local.reshape(sx, sy, sz)).reshape(rows, sz))
     drag[...] = s_asm
-    right[6] = s_asm[(sx - 1) * sy :]
-    left[6] = s_asm[:sy]
-    for copy in copies[4:]:
-        copy.wait()
     fl = [flow[j].astype(F32).reshape(rows, sz) for j in range(3)]
     flat = a.reshape(3, rows, sz)
-    low_edge = jnp.where(ix == 0, 0.0, float(K1[7, 0])).astype(F32)
-    high_edge = jnp.where(ix == nx - 1, 0.0, float(K1[0, 7])).astype(F32)
+    blocks = []
     for c in range(3):
         grad_y = mul_left(dy[...], flat[c])
         planes = [a[c, i] for i in range(sx)]
@@ -218,115 +288,143 @@
         local = m * local
         out = twin_z(twin_y(local.reshape(sx, sy, sz)).reshape(rows, sz))
         field[c] = out
-        plane = [out[i * sy : (i + 1) * sy] for i in range(sx)]
-        up = low_edge * plane[0]
-        for i in range(1, sx - 1):
-            up = up + float(K1[7, i]) * plane[i]
-        down = high_edge * plane[sx - 1]
-        for i in range(1, sx - 1):
-            down = down + float(K1[0, i]) * plane[i]
-        right[c] = plane[sx - 1]
-        right[3 + c] = up
-        left[c] = plane[0]
-        left[3 + c] = down
-
-
-def x_stage_kernel(
-    field, drag, from_low, from_high, from_low2, from_high2, ext, drag_out, up, down
+        blocks.append(out)
+    blocks.append(s_asm)
+    x_high, z_high = member("gx"), member("gz")
+    mx, mz = 1 - as_number(x_high), 1 - as_number(z_high)
+    for c, block in enumerate(blocks):
+        face = face_of(block, x_high, sy)
+        slots[slot_of(1 - mx, mz), c * sy : (c + 1) * sy] = face
+        slots[slot_of(mx, 1 - mz), c * 8 : (c + 1) * 8] = turned(pick[...], block)
+        slots[slot_of(1 - mx, 1 - mz), c * 8 : (c + 1) * 8] = turned(
+            pick[...], facing(face, x_high, rows)
+        )
+
+
+def join(blocks, got, place, x_high, z_high, x_ok, z_ok, sy):
+    mx, mz = 1 - as_number(x_high), 1 - as_number(z_high)
+    rows = blocks[0].shape[0]
+    sz = blocks[0].shape[1]
+    count = len(blocks)
+    tiles = []
+    for c in range(count):
+        tile = picked(got[slot_of(mx, 1 - mz), c * 8 : (c + 1) * 8], z_high, z_ok)
+        corner = picked(
+            got[slot_of(1 - mx, 1 - mz), c * 8 : (c + 1) * 8], z_high, z_ok & x_ok
+        )
+        tiles.append(tile + corner)
+    add = spread(tiles, place)
+    out, cross = [], []
+    for c in range(count):
+        face = got[slot_of(1 - mx, mz), c * sy : (c + 1) * sy]
+        face = jnp.where(x_ok, face, 0.0)
+        part = add[c * rows : (c + 1) * rows]
+        out.append(
+            blocks[c] + facing(face, jnp.logical_not(x_high), rows) + part[:, :sz]
+        )
+        cross.append(part[:, sz:])
+    return out, cross
+
+
+def second_kernel(
+    nx, field, drag, got, pick, place, field_out, drag_out, cross_out, slots
 ):
-    sy, sz = from_low.shape[1:]
-    rows = field.shape[1]
-    sx = rows // sy
-    drag_out[...] = drag[...]
-    drag_out[:sy] = drag[:sy] + from_low[6]
-    drag_out[rows - sy :] = drag[rows - sy :] + from_high[6]
-    count = 2 * sx
+    rows = drag.shape[0]
+    sy = rows // NODES
+    x_high, z_high = member("gx"), member("gz")
+    blocks = [field[0], field[1], field[2], drag[...]]
+    blocks, cross = join(blocks, got, place[...], x_high, z_high, True, True, sy)
+    slots[...] = jnp.zeros(slots.shape, F32)
+    x_high, z_high = jnp.logical_not(x_high), jnp.logical_not(z_high)
+    mx, mz = 1 - as_number(x_high), 1 - as_number(z_high)
+    bends = []
+    for c, block in enumerate(blocks):
+        face = face_of(block, x_high, sy)
+        slots[slot_of(1 - mx, mz), c * sy : (c + 1) * sy] = face
+        slots[slot_of(mx, 1 - mz), c * 8 : (c + 1) * 8] = turned(pick[...], block)
+        slots[slot_of(1 - mx, 1 - mz), c * 8 : (c + 1) * 8] = turned(
+            pick[...], facing(face, x_high, rows)
+        )
+        if c < 3:
+            field_out[c] = block
+            cross_out[c] = cross[c]
+            bend = contraction(block, x_high, sy, nx) + face_of(cross[c], x_high, sy)
+            slots[slot_of(1 - mx, mz), (4 + c) * sy : (5 + c) * sy] = bend
+            bends.append(bend)
+        else:
+            drag_out[...] = block
+    bends.append(jnp.zeros((rows - 3 * sy, drag.shape[1]), F32))
+    slots[slot_of(1 - mx, 1 - mz), 32:40] = turned(
+        pick[...], jnp.concatenate(bends, 0)
+    )
+
+
+def third_kernel(
+    nx,
+    ny,
+    nz,
+    field,
+    drag,
+    cross,
+    got,
+    place,
+    field_out,
+    drag_out,
+    cross_out,
+    bend_out,
+    slots,
+):
+    rows, sz = drag.shape
+    sx = NODES
+    sy = rows // sx
+    x_high, z_high = jnp.logical_not(member("gx")), jnp.logical_not(member("gz"))
+    x_ok = has_neighbour("gx", x_high, nx)
+    z_ok = has_neighbour("gz", z_high, nz)
+    mx, mz = 1 - as_number(x_high), 1 - as_number(z_high)
+    blocks = [field[0], field[1], field[2], drag[...]]
+    blocks, add = join(blocks, got, place[...], x_high, z_high, x_ok, z_ok, sy)
+    tile = picked(got[slot_of(1 - mx, 1 - mz), 32:40], z_high, z_ok & x_ok)
+    bend_add = spread([tile], place[...])
+    partner = slot_of(1 - mx, mz)
+    drag_out[...] = blocks[3]
+    slots[...] = jnp.zeros(slots.shape, F32)
+    x_high = jnp.logical_not(x_high)
+    mx = 1 - as_number(x_high)
+    j = lax.axis_index("gy")
+    above = mx * ny + jnp.minimum(j + 1, ny - 1)
+    below = mx * ny + jnp.maximum(j - 1, 0)
+    beside = (1 - mx) * ny + j
+    beside_above = (1 - mx) * ny + jnp.minimum(j + 1, ny - 1)
+    beside_below = (1 - mx) * ny + jnp.maximum(j - 1, 0)
+    top, bottom = sy - 1, 0
     for c in range(3):
-        ext[c, :rows] = field[c]
-        ext[c, :sy] = field[c, :sy] + from_low[c]
-        ext[c, rows - sy : rows] = field[c, rows - sy :] + from_high[c]
-        ext[c, rows : rows + sy] = from_low[3 + c] + float(K1[7, 0]) * from_low2[c]
-        ext[c, rows + sy : rows + 2 * sy] = (
-            from_high[3 + c] + float(K1[0, 7]) * from_high2[c]
-        )
-
-        def row(y):
-            return ext[c, pl.ds(y, sx, stride=sy), :]
-
-        up[c * count : c * count + sx] = row(sy - 1)
-        total = float(K1[7, 0]) * row(sy - 8)
-        for k in range(1, 7):
-            total = total + float(K1[7, k]) * row(sy - 8 + k)
-        up[c * count + sx : (c + 1) * count] = total
-        down[c * count : c * count + sx] = row(0)
-        total = float(K1[0, 7]) * row(7)
-        for k in range(1, 7):
-            total = total + float(K1[0, k]) * row(k)
-        down[c * count + sx : (c + 1) * count] = total
-    base = 3 * count
-    up[base : base + sx] = drag_out[pl.ds(sy - 1, sx, stride=sy), :]
-    down[base : base + sx] = drag_out[pl.ds(0, sx, stride=sy), :]
-    base += sx
-    up[base : base + 8] = jnp.zeros((8, sz), F32)
-    down[base : base + 8] = jnp.zeros((8, sz), F32)
-    for c in range(3):
-        for side in range(2):
-            spot = rows + side * sy
-            at = base + 2 * c + side
-            up[at : at + 1] = ext[c, spot + sy - 1 : spot + sy]
-            down[at : at + 1] = ext[c, spot : spot + 1]
-
-
-def y_stage_kernel(ext, drag, from_low, from_high, pick, ext_out, drag_out, message):
-    rows, sz = drag.shape
-    sy = (ext.shape[1] - rows) // 2
-    sx = rows // sy
-    count = 2 * sx
-    base = 3 * count
-    drag_out[...] = drag[...]
-    drag_out[pl.ds(0, sx, stride=sy), :] = (
-        drag[pl.ds(0, sx, stride=sy), :] + from_low[base : base + sx]
-    )
-    drag_out[pl.ds(sy - 1, sx, stride=sy), :] = (
-        drag[pl.ds(sy - 1, sx, stride=sy), :] + from_high[base : base + sx]
-    )
-    base += sx
-    used = rows + 2 * sy
-    size = ext_out.shape[1]
-    for c in range(3):
-        ext_out[c, :used] = ext[c]
-        ext_out[c, pl.ds(0, sx, stride=sy), :] = (
-            ext[c, pl.ds(0, sx, stride=sy), :] + from_low[c * count : c * count + sx]
-        )
-        ext_out[c, pl.ds(sy - 1, sx, stride=sy), :] = (
-            ext[c, pl.ds(sy - 1, sx, stride=sy), :]
-            + from_high[c * count : c * count + sx]
-        )
-        for side in range(2):
-            spot = rows + side * sy
-            at = base + 2 * c + side
-            ext_out[c, spot : spot + 1] = ext[c, spot : spot + 1] + from_low[at : at + 1]
-            ext_out[c, spot + sy - 1 : spot + sy] = (
-                ext[c, spot + sy - 1 : spot + sy] + from_high[at : at + 1]
-            )
-        ext_out[c, used : used + sx] = from_low[c * count + sx : (c + 1) * count]
-        ext_out[c, used + sx : used + 2 * sx] = from_high[c * count + sx : (c + 1) * count]
-        ext_out[c, used + 2 * sx :] = jnp.zeros((size - used - 2 * sx, sz), F32)
-    for c in range(3):
-        message[:, c * size : (c + 1) * size] = lax.dot_general(
-            pick[...],
-            ext_out[c],
-            (((1,), (1,)), ((), ())),
-            precision=lax.Precision.HIGHEST,
-            preferred_element_type=F32,
-        )
-    message[:, 3 * size :] = lax.dot_general(
-        pick[...],
-        drag_out[...],
-        (((1,), (1,)), ((), ())),
-        precision=lax.Precision.HIGHEST,
-        preferred_element_type=F32,
-    )
+        field_out[c] = blocks[c]
+        cross_out[c] = cross[c] + add[c]
+        bend = jnp.where(x_ok, got[partner, (4 + c) * sy : (5 + c) * sy], 0.0)
+        bend = bend + bend_add[c * sy : (c + 1) * sy, :sz]
+        bend_out[c] = bend
+        own = contraction(blocks[c], x_high, sy, nx)
+        slots[beside, c * sy : (c + 1) * sy] = own
+        slots[beside_above, 48 + c : 49 + c] = own[top:]
+        slots[beside_below, 48 + c : 49 + c] = own[:1]
+
+        def row(ref, y):
+            return ref[c, pl.ds(y, sx, stride=sy), :]
+
+        up = row(cross_out, top)
+        for k in range(7):
+            up = up + float(K1[7, k]) * row(field_out, sy - 8 + k)
+        down = row(cross_out, bottom)
+        for k in range(1, 8):
+            down = down + float(K1[0, k]) * row(field_out, k)
+        slots[above, c * 16 : c * 16 + 8] = row(field_out, top)
+        slots[above, c * 16 + 8 : c * 16 + 16] = up
+        slots[above, 56 + c : 57 + c] = bend[top:]
+        slots[below, c * 16 : c * 16 + 8] = row(field_out, bottom)
+        slots[below, c * 16 + 8 : c * 16 + 16] = down
+        slots[below, 56 + c : 57 + c] = bend[:1]
+    slots[above, 48:56] = drag_out[pl.ds(top, sx, stride=sy), :]
+    slots[below, 48:56] = drag_out[pl.ds(bottom, sx, stride=sy), :]
 
 
 def keep_mask(shape, sy, counts):
@@ -355,12 +453,12 @@
 def moments_kernel(
     counts,
     sy,
-    ext,
-    drag,
+    field,
+    drag_in,
+    cross,
+    bend_odd,
     sponge,
-    from_low,
-    from_high,
-    place,
+    got,
     plane_asm,
     line_asm,
     plane_own,
@@ -372,30 +470,55 @@
     base,
     image,
     sums,
+    ext,
+    drag,
 ):
     rows, sz = drag.shape
-    size = ext.shape[1]
+    sx = rows // sy
+    ny = counts["gy"]
     keep = keep_mask((rows, sz), sy, counts)
-    lane = lax.broadcasted_iota(jnp.int32, from_low.shape, 0)
-    both = jnp.where(lane < 2, from_low[...], from_high[...])
-    high = both.astype(BF16)
-    rest = both - high.astype(F32)
-    mid = rest.astype(BF16)
-    low = (rest - mid.astype(F32)).astype(BF16)
-    parts = jnp.concatenate([high, mid, low], 0)
-    add = lax.dot_general(
-        parts, place[...], (((0,), (0,)), ((), ())), preferred_element_type=F32
-    )
-    s_asm = drag[...] + add[3 * size :, :sz]
+    x_high = member("gx")
+    mx = 1 - as_number(x_high)
+    j = lax.axis_index("gy")
+    low_ok, high_ok = j > 0, j < ny - 1
+    below = jnp.maximum(j - 1, 0)
+    above = jnp.minimum(j + 1, ny - 1)
+    low = jnp.where(low_ok, got[mx * ny + below], 0.0)
+    high = jnp.where(high_ok, got[mx * ny + above], 0.0)
+    beside_low = jnp.where(low_ok, got[(1 - mx) * ny + below, 48:56], 0.0)
+    beside_high = jnp.where(high_ok, got[(1 - mx) * ny + above, 48:56], 0.0)
+    bottom, top = pl.ds(0, sx, stride=sy), pl.ds(sy - 1, sx, stride=sy)
+    drag[...] = drag_in[...]
+    drag[bottom, :] = drag_in[bottom, :] + low[48:56]
+    drag[top, :] = drag_in[top, :] + high[48:56]
+    used = rows + 2 * sy
+    gap = jnp.zeros((sy - 2, sz), F32)
+    for c in range(3):
+        at = 16 * c
+        ext[c, :rows] = field[c]
+        ext[c, bottom, :] = field[c, bottom, :] + low[at : at + 8]
+        ext[c, top, :] = field[c, top, :] + high[at : at + 8]
+        odd = bend_odd[c] + jnp.concatenate(
+            [low[56 + c : 57 + c], gap, high[56 + c : 57 + c]], 0
+        )
+        even = got[(1 - mx) * ny + j, c * sy : (c + 1) * sy] + jnp.concatenate(
+            [beside_low[c : c + 1], gap, beside_high[c : c + 1]], 0
+        )
+        ext[c, rows : rows + sy] = jnp.where(x_high, odd, even)
+        ext[c, rows + sy : used] = jnp.where(x_high, even, odd)
+        ext[c, used : used + 8] = low[at + 8 : at + 16]
+        ext[c, used + 8 : used + 16] = high[at + 8 : at + 16]
+        ext[c, used + 16 :] = jnp.zeros((rows - 2 * sy - 16, sz), F32)
+    s_asm = drag[...]
     s_own = mass[...] * (inverse_step + sponge[...].reshape(rows, sz))
     line_weight = line_pattern(W1, (1, sz))
     line_weight_asm = line_pattern(assembled_weights(NODES), (1, sz))
     total = [jnp.zeros((1, sz), F32) for _ in range(4)]
     for c in range(3):
-        whole = ext[c] + add[c * size : (c + 1) * size, :sz]
+        whole = ext[c]
         v = jnp.where(keep, whole[:rows], 0.0)
         plane = mul_left(plane_asm[...], jnp.concatenate([v, whole[rows:]], 0))
-        line = mul_right(v, line_asm[...]) + add[c * size : c * size + rows, sz:]
+        line = mul_right(v, line_asm[...]) + cross[c]
         stiff = plane * line_weight_asm + line * plane_weight_asm[...]
         u = jnp.where(keep, s_asm * v + viscosity * stiff, 0.0)
         stiff = (
@@ -434,7 +557,7 @@
 HBM = pl.BlockSpec(memory_space=pltpu.HBM)
 
 
-def call(kernel, operands, outs, fetch=False):
+def call(kernel, operands, outs, fetch=False, scratch=()):
     shapes = [jax.ShapeDtypeStruct(s, F32) for s in outs]
     size = sum(4 * int(np.prod(s)) for s in outs) + sum(
         o.dtype.itemsize * o.size for o in operands
@@ -449,7 +572,7 @@
         scratch_shapes=[pltpu.VMEM(o.shape, o.dtype) for o in operands]
         + [pltpu.SemaphoreType.DMA((len(operands),))]
         if fetch
-        else [],
+        else [pltpu.VMEM(s, F32) for s in scratch],
         compiler_params=pltpu.CompilerParams(vmem_limit_bytes=16 * 1024 * 1024),
         cost_estimate=pl.CostEstimate(
             flops=1_000_000, bytes_accessed=size, transcendentals=0
@@ -457,10 +580,12 @@
     )(*operands)
 
 
-def shift(x, axis, step):
-    count = lax.axis_size(axis)
-    pairs = [(i, i + step) for i in range(count) if 0 <= i + step < count]
-    return lax.ppermute(x, axis, pairs)
+def pairs_of(count, start):
+    return [((start + 2 * m) % count, (start + 2 * m + 1) % count) for m in range(count // 2)]
+
+
+def groups_of(x_pairs, z_pairs, width):
+    return [[x * width + z for x in xs for z in zs] for xs in x_pairs for zs in z_pairs]
 
 
 def body(adjoint_state, base_flow, base_grads, sponge):
@@ -487,40 +612,52 @@
     )
     dy = jnp.asarray(left_operand(block_diag(D1, rows // NODES)))
     dz = jnp.asarray(right_operand(block_diag(D1, sz // NODES).T))
-    field, drag, right, left = call(
-        functools.partial(forcing_kernel, counts["gx"]),
-        (adjoint_state, base_flow, base_grads, sponge, mass, dy, dz),
-        [(3, rows, sz), (rows, sz)] + [(7, sy, sz)] * 2,
-        fetch=True,
-    )
-    x_low = shift(right, "gx", 1)
-    x_low2 = shift(right, "gx", 2)
-    x_high = shift(left, "gx", -1)
-    x_high2 = shift(left, "gx", -2)
-    message_rows = 7 * sx + 8
-    ext, drag, up, down = call(
-        x_stage_kernel,
-        (field, drag, x_low, x_high, x_low2, x_high2),
-        [(3, used, sz), (rows, sz), (message_rows, sz), (message_rows, sz)],
-    )
-    y_low = shift(up, "gy", 1)
-    y_high = shift(down, "gy", -1)
     pick = np.zeros((8, sz))
     pick[0, sz - 1] = 1.0
     pick[1, sz - 8 : sz - 1] = K1[7, :7]
     pick[2, 0] = 1.0
     pick[3, 1:8] = K1[0, 1:]
-    ext, drag, message = call(
-        y_stage_kernel,
-        (ext, drag, y_low, y_high, f32(pick)),
-        [(3, size, sz), (rows, sz), (8, 3 * size + rows)],
-    )
-    z_low = shift(message, "gz", 1)
-    z_high = shift(message, "gz", -1)
-
+    pick = f32(pick)
     place = np.zeros((8, 2 * sz))
     place[0, 0] = place[1, sz] = place[2, sz - 1] = place[3, 2 * sz - 1] = 1.0
     place = jnp.asarray(np.tile(place, (3, 1)).astype(np.float32).astype(BF16))
+    nx, ny, nz = counts["gx"], counts["gy"], counts["gz"]
+
+    def exchange(slots, start):
+        groups = groups_of(pairs_of(nx, start), pairs_of(nz, start), nz)
+        return lax.all_to_all(
+            slots, ("gx", "gz"), 0, 0, tiled=True, axis_index_groups=groups
+        )
+
+    block, plane = (3, rows, sz), (rows, sz)
+    field, drag, slots = call(
+        forcing_kernel,
+        (adjoint_state, base_flow, base_grads, sponge, mass, dy, dz, pick),
+        [block, plane, (4, 64, sz)],
+        fetch=True,
+    )
+    got = exchange(slots, 0)
+    field, drag, cross, slots = call(
+        functools.partial(second_kernel, nx),
+        (field, drag, got, pick, place),
+        [block, plane, block, (4, 7 * sy, sz)],
+    )
+    got = exchange(slots, 1)
+    field, drag, cross, bend, slots = call(
+        functools.partial(third_kernel, nx, ny, nz),
+        (field, drag, cross, got, place),
+        [block, plane, block, (3, sy, sz), (2 * ny, 64, sz)],
+    )
+    every = [tuple(range(ny))]
+    got = lax.all_to_all(
+        slots,
+        ("gx", "gy"),
+        0,
+        0,
+        tiled=True,
+        axis_index_groups=groups_of(pairs_of(nx, 0), every, ny),
+    )
+
     plane_asm = np.zeros((rows, size))
     plane_asm[:, :rows] = np.kron(assembled_stiffness(sx), np.diag(ay)) + np.kron(
         np.diag(ax), assembled_stiffness(sy)
@@ -538,12 +675,12 @@
     base, image, sums = call(
         functools.partial(moments_kernel, counts, sy),
         (
-            ext,
+            field,
             drag,
+            cross,
+            bend,
             sponge,
-            z_low,
-            z_high,
-            place,
+            got,
             jnp.asarray(left_operand(plane_asm)),
             jnp.asarray(right_operand(assembled_stiffness(sz).T)),
             jnp.asarray(left_operand(plane_own)),
@@ -553,7 +690,8 @@
             over_plane(ax, ay),
             over_plane(wx, wy),
         ),
-        [(3, rows, sz), (3, rows, sz), (slots, sz)],
+        [block, block, (slots, sz)],
+        scratch=[(3, size, sz), plane],
     )
     sums = lax.all_to_all(sums, "gz", 0, 0, tiled=True)
     sums = jnp.sum(sums, axis=0, keepdims=True)

time: 89.5 us -> 83.7 us (0.935)
  blocking collectives: 47.5 us -> 77 us
  starting transfers between devices: 27.3 us -> 0 us
  waiting for transfers between devices: 9.17 us -> 0 us
  Pallas kernels: 4.82 us -> 6.1 us
    all_to_all x0 -> x3, blocking collectives: none -> 36.7 us  [the longest x2 28 us: exchange(): lax.all_to_all(slots, ('gx', 'gz'), 0, 0, tiled=True, axis_index_groups=g...]
    ppermute x8 -> x0, starting transfers between devices: 27.3 us -> none  [shift(): return lax.ppermute(x, axis, pairs)]
    ppermute x8 -> x0, waiting for transfers between devices: 9.17 us -> none  [shift(): return lax.ppermute(x, axis, pairs)]
    all_to_all x1, blocking collectives: 29.2 us -> 24.9 us  [body(): sums = lax.all_to_all(sums, 'gz', 0, 0, tiled=True)]
    all_to_all x1, blocking collectives: 18.3 us -> 15.5 us  [body(): sums = lax.all_to_all(sums, ('gx', 'gy'), 0, 0, tiled=True)]
    pallas_call x5, Pallas kernels: 4.82 us -> 6.1 us  [call(): pl.pallas_call(kernel, out_shape=shapes, in_specs=[HBM if fetch else VMEM...]
  transfers between devices with their start and end apart: 8 -> 0, of which waited for: 4 -> 0; matrix products, arithmetic and copies ran while one was open for 0% -> 0% of each run, Pallas kernels for 0% -> 0%
where the time goes in v5:
time: 83.7 us; the launch traced here: 83.4 us
  blocking collectives  77 us (92%)
  Pallas kernels  6.1 us (7%)
    all_to_all x2, blocking collectives, exchange(): lax.all_to_all(slots, ('gx', 'gz'), 0, 0, tiled=True, axis_index_groups=g...  28 us
    all_to_all x1, blocking collectives, body(): sums = lax.all_to_all(sums, 'gz', 0, 0, tiled=True)  24.9 us
    all_to_all x1, blocking collectives, body(): sums = lax.all_to_all(sums, ('gx', 'gy'), 0, 0, tiled=True)  15.5 us
    all_to_all x1, blocking collectives, body(): lax.all_to_all(slots, ('gx', 'gy'), 0, 0, tiled=True, axis_index_groups=g...  8.62 us
    pallas_call x5, Pallas kernels, call(): pl.pallas_call(kernel, out_shape=shapes, in_specs=[HBM if fetch else VMEM...  6.1 us

profile of v5, /device:TPU:1, one launch (start us, length us, event | category | flops | bytes accessed | tf_op | source)
XLA Modules:
  0.0 83.4 jit_solution(4964248825360310783)
XLA Ops:
  0.0 2.6 %shard_map.154 = (f32[3,128,128]{2,1,0:T(8,128)S(1)}, f32[128,128]{1,0:T(8,128)S(1)}, f32[4,64,128]{2,1,0:T(8,128)S(1)}) custom-call(f32[3,8,16,128]{3,2,1,0:T(8,128)} %adj_hbm.1, bf16[3,8,16,128]{3,2,1,0:T(8,128)(2,1)} %flow_hbm.1, bf16[9,8,16,128]{3,2,1,0:T(8,128)(2,1)} %grads_hbm.1, f32[8,16,128]{2,1,0:T(8,128)} %sponge.1, ...), custom_call_target="tpu_custom_call" | custom-call | flops 1000000 | bytes 1380352 | tf_op jit(solution)/shard_map/pallas_call | solution.py:567
  2.6 0.0 copy-start.9
  2.6 0.0 copy-start.10
  2.6 20.1 %all_to_all.32.got = f32[4,64,128]{2,1,0:T(8,128)S(1)} all-to-all(f32[4,64,128]{2,1,0:T(8,128)S(1)} %get-tuple-element.22), channel_id=1, replica_groups={{0,1,128,129},{2,3,130,131},{4,5,132,133},{6,7,134,135},{8,9,136,137},{..., dimensions={0} | all-to-all | bytes 262144 | tf_op jit(solution)/shard_map/all_to_all | solution.py:628
  22.8 0.0 copy-done.9
  22.8 0.0 copy-done.10
  22.8 1.2 %shard_map.155 = (f32[3,128,128]{2,1,0:T(8,128)S(1)}, f32[128,128]{1,0:T(8,128)S(1)}, f32[3,128,128]{2,1,0:T(8,128)S(1)}, f32[4,112,128]{2,1,0:T(8,128)S(1)}) custom-call(f32[3,128,128]{2,1,0:T(8,128)S(1)} %get-tuple-element.20.field, f32[128,128]{1,0:T(8,128)S(1)} %get-tuple-element.21.drag, f32[4,64,128]{2,1,0:T(8,128)S(1)} %all_to_all.32.got, ...), custom_call_target="tpu_custom_call" | custom-call | flops 1000000 | bytes 1097728 | tf_op jit(solution)/shard_map/pallas_call | solution.py:567
  23.9 7.9 %all_to_all.33.got = f32[4,112,128]{2,1,0:T(8,128)S(1)} all-to-all(f32[4,112,128]{2,1,0:T(8,128)S(1)} %get-tuple-element.26), channel_id=1, replica_groups={{129,130,257,258},{131,132,259,260},{133,134,261,262},{135,136,263,264}..., dimensions={0} | all-to-all | bytes 458752 | tf_op jit(solution)/shard_map/all_to_all | solution.py:628
  31.9 0.0 copy-start.8
  31.9 0.3 shard_map.156
  32.2 0.0 copy-start
  32.2 0.0 copy-start.1
  32.3 0.0 copy-start.2
  32.3 0.0 copy-start.3
  32.3 8.6 %all_to_all.34.got = f32[8,64,128]{2,1,0:T(8,128)S(1)} all-to-all(f32[8,64,128]{2,1,0:T(8,128)S(1)} %get-tuple-element.31), channel_id=1, replica_groups={{0,32,64,96,128,160,192,224},{256,288,320,352,384,416,448,480},{512,544..., dimensions={0} | all-to-all | bytes 524288 | tf_op jit(solution)/shard_map/all_to_all | solution.py:652
  40.9 0.0 copy-done.4
  40.9 0.0 copy-done.5
  40.9 0.0 copy-done.6
  40.9 0.0 copy-done.7
  41.0 1.1 %shard_map.157 = (f32[3,128,128]{2,1,0:T(8,128)S(1)}, f32[3,128,128]{2,1,0:T(8,128)S(1)}, f32[32,128]{1,0:T(8,128)S(1)}) custom-call(f32[3,128,128]{2,1,0:T(8,128)S(1)} %get-tuple-element.27.field, f32[128,128]{1,0:T(8,128)S(1)} %get-tuple-element.28.drag_in, f32[3,128,128]{2,1,0:T(8,128)S(1)} %get-tuple-element.29.cross, ...), custom_call_target="tpu_custom_call" | custom-call | flops 1000000 | bytes 2138112 | tf_op jit(solution)/shard_map/pallas_call | solution.py:567
  42.1 24.9 %all_to_all.35 = f32[32,1,128]{2,1,0:T(1,128)S(1)} all-to-all(f32[32,1,128]{2,1,0:T(1,128)S(1)} %bitcast.6), channel_id=1, replica_groups=mesh['gx'=8,'gy'=4,'gz'=32] {'gz'}, dimensions={0} | all-to-all | bytes 32768 | tf_op jit(solution)/shard_map/all_to_all | solution.py:696
  67.0 0.1 reduce_sum.9
  67.0 15.5 %all_to_all.36 = f32[32,1,128]{2,1,0:T(1,128)S(1)} all-to-all(f32[32,1,128]{2,1,0:T(1,128)S(1)} %broadcast_in_dim.2), channel_id=1, replica_groups=mesh['gx'=8,'gy'=4,'gz'=32] {'gx','gy'}, dimensions={0} | all-to-all | bytes 32768 | tf_op jit(solution)/shard_map/all_to_all | solution.py:700
  82.5 0.8 %shard_map.158 = f32[3,128,128]{2,1,0:T(8,128)} custom-call(f32[3,128,128]{2,1,0:T(8,128)S(1)} %get-tuple-element.32.base, f32[3,128,128]{2,1,0:T(8,128)S(1)} %get-tuple-element.33.image, f32[32,128]{1,0:T(8,128)S(1)} %bitcast.5), custom_call_target="tpu_custom_call" | custom-call | flops 1000000 | bytes 606208 | tf_op jit(solution)/shard_map/pallas_call | solution.py:567
  (10 shorter events, 0.0 us)
Async XLA Ops:
  2.6 20.2 %copy-start.9 = (bf16[24,256]{1,0:T(8,128)(2,1)S(1)}, bf16[24,256]{1,0:T(8,128)(2,1)}, u32[]{:S(2)}) copy-start(bf16[24,256]{1,0:T(8,128)(2,1)} %constant.31.clone.place) | copy-start | bytes 36868
  2.6 20.2 %copy-start.10 = (f32[8,128]{1,0:T(8,128)S(1)}, f32[8,128]{1,0:T(8,128)}, u32[]{:S(2)}) copy-start(f32[8,128]{1,0:T(8,128)} %constant.30.clone.pick_hbm.pick) | copy-start | bytes 12292
  31.9 9.0 %copy-start.4 = (bf16[256,256]{1,0:T(8,128)(2,1)S(1)}, bf16[256,256]{1,0:T(8,128)(2,1)}, u32[]{:S(2)}) copy-start(bf16[256,256]{1,0:T(8,128)(2,1)} %constant.34.clone.plane_own) | copy-start | bytes 393220
  31.9 9.0 %copy-start.5 = (bf16[256,256]{1,0:T(8,128)(2,1)S(1)}, bf16[256,256]{1,0:T(8,128)(2,1)}, u32[]{:S(2)}) copy-start(bf16[256,256]{1,0:T(8,128)(2,1)} %constant.33.clone.line_asm) | copy-start | bytes 393220
  31.9 9.0 %copy-start.6 = (f32[128,128]{1,0:T(8,128)S(1)}, f32[128,128]{1,0:T(8,128)}, u32[]{:S(2)}) copy-start(f32[128,128]{1,0:T(8,128)} %constant.37.clone.plane_weight) | copy-start | bytes 196612
  31.9 9.1 %copy-start.7 = (f32[128,128]{1,0:T(8,128)S(1)}, f32[128,128]{1,0:T(8,128)}, u32[]{:S(2)}) copy-start(f32[128,128]{1,0:T(8,128)} %constant.36.clone.plane_weight_asm) | copy-start | bytes 196612
  31.9 9.1 %copy-start.8 = (f32[128,128]{1,0:T(8,128)S(1)}, f32[128,128]{1,0:T(8,128)}, u32[]{:S(2)}) copy-start(f32[128,128]{1,0:T(8,128)} %constant.27.clone.share) | copy-start | bytes 196612
  32.2 8.7 %copy-start = (bf16[256,512]{1,0:T(8,128)(2,1)S(1)}, bf16[256,512]{1,0:T(8,128)(2,1)}, u32[]{:S(2)}) copy-start(bf16[256,512]{1,0:T(8,128)(2,1)} %constant.32.clone.plane_asm) | copy-start | bytes 786436
  32.2 8.7 %copy-start.1 = (f32[8,16,128]{2,1,0:T(8,128)S(1)}, f32[8,16,128]{2,1,0:T(8,128)}, u32[]{:S(2)}) copy-start(f32[8,16,128]{2,1,0:T(8,128)} %sponge.1) | copy-start | bytes 196612
  32.3 8.7 %copy-start.2 = (f32[128,128]{1,0:T(8,128)S(1)}, f32[128,128]{1,0:T(8,128)}, u32[]{:S(2)}) copy-start(f32[128,128]{1,0:T(8,128)} %constant.26.clone.mass_hbm.mass) | copy-start | bytes 196612
  32.3 8.7 %copy-start.3 = (bf16[256,256]{1,0:T(8,128)(2,1)S(1)}, bf16[256,256]{1,0:T(8,128)(2,1)}, u32[]{:S(2)}) copy-start(bf16[256,256]{1,0:T(8,128)(2,1)} %constant.35.clone.line_own) | copy-start | bytes 393220

commit v6 on v5

--- a/solution.py
+++ b/solution.py
@@ -160,13 +160,14 @@
 
 
 def turned(pick, tile):
-    return lax.dot_general(
+    count = pick.shape[0] // 2
+    out = lax.dot_general(
         pick,
-        tile,
+        jnp.concatenate(split(tile), 1),
         (((1,), (1,)), ((), ())),
-        precision=lax.Precision.HIGHEST,
         preferred_element_type=F32,
     )
+    return out[:count] + out[count:]
 
 
 def spread(tiles, place):
@@ -190,6 +191,13 @@
 
 def face_of(x, high, size):
     return jnp.where(high, x[-size:], x[:size])
+
+
+def corner_at(packed, c, x_high, size, rows):
+    start = jnp.where(x_high, rows - size, 0)
+    moved = pltpu.roll(packed, lax.rem(start + rows - c * size, rows), 1)
+    lane = lax.broadcasted_iota(jnp.int32, packed.shape, 1)
+    return jnp.where((lane >= start) & (lane < start + size), moved, 0.0)
 
 
 def facing(face, high, rows):
@@ -292,27 +300,28 @@
     blocks.append(s_asm)
     x_high, z_high = member("gx"), member("gz")
     mx, mz = 1 - as_number(x_high), 1 - as_number(z_high)
+    faces = []
     for c, block in enumerate(blocks):
         face = face_of(block, x_high, sy)
         slots[slot_of(1 - mx, mz), c * sy : (c + 1) * sy] = face
         slots[slot_of(mx, 1 - mz), c * 8 : (c + 1) * 8] = turned(pick[...], block)
-        slots[slot_of(1 - mx, 1 - mz), c * 8 : (c + 1) * 8] = turned(
-            pick[...], facing(face, x_high, rows)
-        )
-
-
-def join(blocks, got, place, x_high, z_high, x_ok, z_ok, sy):
+        faces.append(face)
+    faces.append(jnp.zeros((rows - 4 * sy, sz), F32))
+    slots[slot_of(1 - mx, 1 - mz), 0:8] = turned(pick[...], jnp.concatenate(faces, 0))
+
+
+def join(blocks, got, place, x_high, z_high, x_ok, z_ok, sy, bends=False):
     mx, mz = 1 - as_number(x_high), 1 - as_number(z_high)
     rows = blocks[0].shape[0]
     sz = blocks[0].shape[1]
     count = len(blocks)
     tiles = []
+    packed = picked(got[slot_of(1 - mx, 1 - mz), 0:8], z_high, z_ok & x_ok)
     for c in range(count):
         tile = picked(got[slot_of(mx, 1 - mz), c * 8 : (c + 1) * 8], z_high, z_ok)
-        corner = picked(
-            got[slot_of(1 - mx, 1 - mz), c * 8 : (c + 1) * 8], z_high, z_ok & x_ok
-        )
-        tiles.append(tile + corner)
+        tiles.append(tile + corner_at(packed, c, x_high, sy, rows))
+    if bends:
+        tiles.append(pltpu.roll(packed, rows - count * sy, 1))
     add = spread(tiles, place)
     out, cross = [], []
     for c in range(count):
@@ -323,7 +332,7 @@
             blocks[c] + facing(face, jnp.logical_not(x_high), rows) + part[:, :sz]
         )
         cross.append(part[:, sz:])
-    return out, cross
+    return out, cross, add[count * rows :, :sz]
 
 
 def second_kernel(
@@ -333,18 +342,16 @@
     sy = rows // NODES
     x_high, z_high = member("gx"), member("gz")
     blocks = [field[0], field[1], field[2], drag[...]]
-    blocks, cross = join(blocks, got, place[...], x_high, z_high, True, True, sy)
+    blocks, cross, _ = join(blocks, got, place[...], x_high, z_high, True, True, sy)
     slots[...] = jnp.zeros(slots.shape, F32)
     x_high, z_high = jnp.logical_not(x_high), jnp.logical_not(z_high)
     mx, mz = 1 - as_number(x_high), 1 - as_number(z_high)
-    bends = []
+    faces, bends = [], []
     for c, block in enumerate(blocks):
         face = face_of(block, x_high, sy)
         slots[slot_of(1 - mx, mz), c * sy : (c + 1) * sy] = face
         slots[slot_of(mx, 1 - mz), c * 8 : (c + 1) * 8] = turned(pick[...], block)
-        slots[slot_of(1 - mx, 1 - mz), c * 8 : (c + 1) * 8] = turned(
-            pick[...], facing(face, x_high, rows)
-        )
+        faces.append(face)
         if c < 3:
             field_out[c] = block
             cross_out[c] = cross[c]
@@ -353,9 +360,9 @@
             bends.append(bend)
         else:
             drag_out[...] = block
-    bends.append(jnp.zeros((rows - 3 * sy, drag.shape[1]), F32))
-    slots[slot_of(1 - mx, 1 - mz), 32:40] = turned(
-        pick[...], jnp.concatenate(bends, 0)
+    gap = jnp.zeros((rows - 7 * sy, drag.shape[1]), F32)
+    slots[slot_of(1 - mx, 1 - mz), 0:8] = turned(
+        pick[...], jnp.concatenate(faces + bends + [gap], 0)
     )
 
 
@@ -382,9 +389,9 @@
     z_ok = has_neighbour("gz", z_high, nz)
     mx, mz = 1 - as_number(x_high), 1 - as_number(z_high)
     blocks = [field[0], field[1], field[2], drag[...]]
-    blocks, add = join(blocks, got, place[...], x_high, z_high, x_ok, z_ok, sy)
-    tile = picked(got[slot_of(1 - mx, 1 - mz), 32:40], z_high, z_ok & x_ok)
-    bend_add = spread([tile], place[...])
+    blocks, add, bend_add = join(
+        blocks, got, place[...], x_high, z_high, x_ok, z_ok, sy, bends=True
+    )
     partner = slot_of(1 - mx, mz)
     drag_out[...] = blocks[3]
     slots[...] = jnp.zeros(slots.shape, F32)
@@ -401,7 +408,7 @@
         field_out[c] = blocks[c]
         cross_out[c] = cross[c] + add[c]
         bend = jnp.where(x_ok, got[partner, (4 + c) * sy : (5 + c) * sy], 0.0)
-        bend = bend + bend_add[c * sy : (c + 1) * sy, :sz]
+        bend = bend + bend_add[c * sy : (c + 1) * sy]
         bend_out[c] = bend
         own = contraction(blocks[c], x_high, sy, nx)
         slots[beside, c * sy : (c + 1) * sy] = own
@@ -617,7 +624,7 @@
     pick[1, sz - 8 : sz - 1] = K1[7, :7]
     pick[2, 0] = 1.0
     pick[3, 1:8] = K1[0, 1:]
-    pick = f32(pick)
+    pick = jnp.asarray(left_operand(pick))
     place = np.zeros((8, 2 * sz))
     place[0, 0] = place[1, sz] = place[2, sz - 1] = place[3, 2 * sz - 1] = 1.0
     place = jnp.asarray(np.tile(place, (3, 1)).astype(np.float32).astype(BF16))

time: 83.7 us -> 82.5 us (0.986)
  Pallas kernels: 6.1 us -> 4.86 us
    pallas_call x5, Pallas kernels: 6.1 us -> 4.86 us  [call(): pl.pallas_call(kernel, out_shape=shapes, in_specs=[HBM if fetch else VMEM...]
where the time goes in v6:
time: 82.5 us; the launch traced here: 82.1 us
  blocking collectives  77 us (93%)
  Pallas kernels  4.86 us (6%)
    all_to_all x2, blocking collectives, exchange(): lax.all_to_all(slots, ('gx', 'gz'), 0, 0, tiled=True, axis_index_groups=g...  28 us
    all_to_all x1, blocking collectives, body(): sums = lax.all_to_all(sums, 'gz', 0, 0, tiled=True)  24.9 us
    all_to_all x1, blocking collectives, body(): sums = lax.all_to_all(sums, ('gx', 'gy'), 0, 0, tiled=True)  15.5 us
    all_to_all x1, blocking collectives, body(): lax.all_to_all(slots, ('gx', 'gy'), 0, 0, tiled=True, axis_index_groups=g...  8.62 us
    pallas_call x5, Pallas kernels, call(): pl.pallas_call(kernel, out_shape=shapes, in_specs=[HBM if fetch else VMEM...  4.86 us

profile of v6, /device:TPU:1, one launch (start us, length us, event | category | flops | bytes accessed | tf_op | source)
XLA Modules:
  0.0 82.1 jit_solution(4543661459662461626)
XLA Ops:
  0.0 2.0 %shard_map.154 = (f32[3,128,128]{2,1,0:T(8,128)S(1)}, f32[128,128]{1,0:T(8,128)S(1)}, f32[4,64,128]{2,1,0:T(8,128)S(1)}) custom-call(f32[3,8,16,128]{3,2,1,0:T(8,128)} %adj_hbm.1, bf16[3,8,16,128]{3,2,1,0:T(8,128)(2,1)} %flow_hbm.1, bf16[9,8,16,128]{3,2,1,0:T(8,128)(2,1)} %grads_hbm.1, f32[8,16,128]{2,1,0:T(8,128)} %sponge.1, ...), custom_call_target="tpu_custom_call" | custom-call | flops 1000000 | bytes 1384448 | tf_op jit(solution)/shard_map/pallas_call | solution.py:574
  2.0 0.0 copy-start.9
  2.0 0.0 copy-start.10
  2.0 20.1 %all_to_all.32.got = f32[4,64,128]{2,1,0:T(8,128)S(1)} all-to-all(f32[4,64,128]{2,1,0:T(8,128)S(1)} %get-tuple-element.22), channel_id=1, replica_groups={{0,1,128,129},{2,3,130,131},{4,5,132,133},{6,7,134,135},{8,9,136,137},{..., dimensions={0} | all-to-all | bytes 262144 | tf_op jit(solution)/shard_map/all_to_all | solution.py:635
  22.1 0.5 shard_map.155
  22.6 7.9 %all_to_all.33.got = f32[4,112,128]{2,1,0:T(8,128)S(1)} all-to-all(f32[4,112,128]{2,1,0:T(8,128)S(1)} %get-tuple-element.26), channel_id=1, replica_groups={{129,130,257,258},{131,132,259,260},{133,134,261,262},{135,136,263,264}..., dimensions={0} | all-to-all | bytes 458752 | tf_op jit(solution)/shard_map/all_to_all | solution.py:635
  30.6 0.0 copy-start.8
  30.6 0.4 shard_map.156
  31.0 0.0 copy-start
  31.0 0.0 copy-start.1
  31.0 0.0 copy-start.2
  31.0 0.0 copy-start.3
  31.0 8.6 %all_to_all.34.got = f32[8,64,128]{2,1,0:T(8,128)S(1)} all-to-all(f32[8,64,128]{2,1,0:T(8,128)S(1)} %get-tuple-element.31), channel_id=1, replica_groups={{0,32,64,96,128,160,192,224},{256,288,320,352,384,416,448,480},{512,544..., dimensions={0} | all-to-all | bytes 524288 | tf_op jit(solution)/shard_map/all_to_all | solution.py:659
  39.7 0.0 copy-done.7
  39.7 0.0 copy-done.8
  39.7 0.0 copy-done
  39.7 0.0 copy-done.1
  39.7 0.0 copy-done.2
  39.7 0.0 copy-done.3
  39.7 1.1 %shard_map.157 = (f32[3,128,128]{2,1,0:T(8,128)S(1)}, f32[3,128,128]{2,1,0:T(8,128)S(1)}, f32[32,128]{1,0:T(8,128)S(1)}) custom-call(f32[3,128,128]{2,1,0:T(8,128)S(1)} %get-tuple-element.27.field, f32[128,128]{1,0:T(8,128)S(1)} %get-tuple-element.28.drag_in, f32[3,128,128]{2,1,0:T(8,128)S(1)} %get-tuple-element.29.cross, ...), custom_call_target="tpu_custom_call" | custom-call | flops 1000000 | bytes 2138112 | tf_op jit(solution)/shard_map/pallas_call | solution.py:574
  40.9 24.9 %all_to_all.35 = f32[32,1,128]{2,1,0:T(1,128)S(1)} all-to-all(f32[32,1,128]{2,1,0:T(1,128)S(1)} %bitcast.6), channel_id=1, replica_groups=mesh['gx'=8,'gy'=4,'gz'=32] {'gz'}, dimensions={0} | all-to-all | bytes 32768 | tf_op jit(solution)/shard_map/all_to_all | solution.py:703
  65.7 0.1 reduce_sum.9
  65.8 15.5 %all_to_all.36 = f32[32,1,128]{2,1,0:T(1,128)S(1)} all-to-all(f32[32,1,128]{2,1,0:T(1,128)S(1)} %broadcast_in_dim.2), channel_id=1, replica_groups=mesh['gx'=8,'gy'=4,'gz'=32] {'gx','gy'}, dimensions={0} | all-to-all | bytes 32768 | tf_op jit(solution)/shard_map/all_to_all | solution.py:707
  81.3 0.8 %shard_map.158 = f32[3,128,128]{2,1,0:T(8,128)} custom-call(f32[3,128,128]{2,1,0:T(8,128)S(1)} %get-tuple-element.32.base, f32[3,128,128]{2,1,0:T(8,128)S(1)} %get-tuple-element.33.image, f32[32,128]{1,0:T(8,128)S(1)} %bitcast.5), custom_call_target="tpu_custom_call" | custom-call | flops 1000000 | bytes 606208 | tf_op jit(solution)/shard_map/pallas_call | solution.py:574
  (10 shorter events, 0.0 us)
Async XLA Ops:
  2.0 20.2 %copy-start.9 = (bf16[24,256]{1,0:T(8,128)(2,1)S(1)}, bf16[24,256]{1,0:T(8,128)(2,1)}, u32[]{:S(2)}) copy-start(bf16[24,256]{1,0:T(8,128)(2,1)} %constant.31.clone.place) | copy-start | bytes 36868
  2.0 20.2 %copy-start.10 = (bf16[16,256]{1,0:T(8,128)(2,1)S(1)}, bf16[16,256]{1,0:T(8,128)(2,1)}, u32[]{:S(2)}) copy-start(bf16[16,256]{1,0:T(8,128)(2,1)} %constant.30.clone.pick_hbm.pick) | copy-start | bytes 24580
  30.5 9.1 %copy-start.4 = (bf16[256,256]{1,0:T(8,128)(2,1)S(1)}, bf16[256,256]{1,0:T(8,128)(2,1)}, u32[]{:S(2)}) copy-start(bf16[256,256]{1,0:T(8,128)(2,1)} %constant.34.clone.plane_own) | copy-start | bytes 393220
  30.6 9.1 %copy-start.5 = (bf16[256,256]{1,0:T(8,128)(2,1)S(1)}, bf16[256,256]{1,0:T(8,128)(2,1)}, u32[]{:S(2)}) copy-start(bf16[256,256]{1,0:T(8,128)(2,1)} %constant.33.clone.line_asm) | copy-start | bytes 393220
  30.6 9.1 %copy-start.6 = (f32[128,128]{1,0:T(8,128)S(1)}, f32[128,128]{1,0:T(8,128)}, u32[]{:S(2)}) copy-start(f32[128,128]{1,0:T(8,128)} %constant.37.clone.plane_weight) | copy-start | bytes 196612
  30.6 9.1 %copy-start.7 = (f32[128,128]{1,0:T(8,128)S(1)}, f32[128,128]{1,0:T(8,128)}, u32[]{:S(2)}) copy-start(f32[128,128]{1,0:T(8,128)} %constant.36.clone.plane_weight_asm) | copy-start | bytes 196612
  30.6 9.1 %copy-start.8 = (f32[128,128]{1,0:T(8,128)S(1)}, f32[128,128]{1,0:T(8,128)}, u32[]{:S(2)}) copy-start(f32[128,128]{1,0:T(8,128)} %constant.27.clone.share) | copy-start | bytes 196612
  31.0 8.7 %copy-start = (bf16[256,512]{1,0:T(8,128)(2,1)S(1)}, bf16[256,512]{1,0:T(8,128)(2,1)}, u32[]{:S(2)}) copy-start(bf16[256,512]{1,0:T(8,128)(2,1)} %constant.32.clone.plane_asm) | copy-start | bytes 786436
  31.0 8.7 %copy-start.1 = (f32[8,16,128]{2,1,0:T(8,128)S(1)}, f32[8,16,128]{2,1,0:T(8,128)}, u32[]{:S(2)}) copy-start(f32[8,16,128]{2,1,0:T(8,128)} %sponge.1) | copy-start | bytes 196612
  31.0 8.7 %copy-start.2 = (f32[128,128]{1,0:T(8,128)S(1)}, f32[128,128]{1,0:T(8,128)}, u32[]{:S(2)}) copy-start(f32[128,128]{1,0:T(8,128)} %constant.26.clone.mass_hbm.mass) | copy-start | bytes 196612
  31.0 8.7 %copy-start.3 = (bf16[256,256]{1,0:T(8,128)(2,1)S(1)}, bf16[256,256]{1,0:T(8,128)(2,1)}, u32[]{:S(2)}) copy-start(bf16[256,256]{1,0:T(8,128)(2,1)} %constant.35.clone.line_own) | copy-start | bytes 393220

commit v7 on v6

--- a/solution.py
+++ b/solution.py
@@ -678,7 +678,11 @@
     plane_own = np.kron(K1, np.diag(wy)) + np.kron(
         np.diag(wx), block_diag(K1, sy // NODES)
     )
-    slots = counts["gz"]
+    near = min(4, nz)
+    runs = [tuple(range(k, k + near)) for k in range(0, nz, near)]
+    first = groups_of(every, runs, nz)
+    strides = [tuple(range(k, nz, near)) for k in range(near)]
+    second = groups_of([tuple(range(nx))], strides, nz)
     base, image, sums = call(
         functools.partial(moments_kernel, counts, sy),
         (
@@ -697,14 +701,17 @@
             over_plane(ax, ay),
             over_plane(wx, wy),
         ),
-        [block, block, (slots, sz)],
+        [block, block, (len(first[0]), sz)],
         scratch=[(3, size, sz), plane],
     )
-    sums = lax.all_to_all(sums, "gz", 0, 0, tiled=True)
+    sums = lax.all_to_all(
+        sums, ("gy", "gz"), 0, 0, tiled=True, axis_index_groups=first
+    )
     sums = jnp.sum(sums, axis=0, keepdims=True)
-    slots = counts["gx"] * counts["gy"]
-    sums = jnp.broadcast_to(sums, (slots, sz))
-    sums = lax.all_to_all(sums, ("gx", "gy"), 0, 0, tiled=True)
+    sums = jnp.broadcast_to(sums, (len(second[0]), sz))
+    sums = lax.all_to_all(
+        sums, ("gx", "gz"), 0, 0, tiled=True, axis_index_groups=second
+    )
     (out,) = call(combine_kernel, (base, image, sums), [(3, rows, sz)])
     return out.reshape(3, sx, sy, sz)
 

time: 82.5 us -> 84.6 us (1.025)
  blocking collectives: 77 us -> 79.1 us
    all_to_all x2, blocking collectives: 40.3 us -> 42.4 us  [the longest x1 27.2 us: body(): lax.all_to_all(sums, ('gx', 'gz'), 0, 0, tiled=True, axis_index_groups=se...]
where the time goes in v7:
time: 84.6 us; the launch traced here: 84.2 us
  blocking collectives  79.1 us (93%)
  Pallas kernels  4.86 us (6%)
    all_to_all x2, blocking collectives, exchange(): lax.all_to_all(slots, ('gx', 'gz'), 0, 0, tiled=True, axis_index_groups=g...  28 us
    all_to_all x1, blocking collectives, body(): lax.all_to_all(sums, ('gx', 'gz'), 0, 0, tiled=True, axis_index_groups=se...  27.2 us
    all_to_all x1, blocking collectives, body(): lax.all_to_all(sums, ('gy', 'gz'), 0, 0, tiled=True, axis_index_groups=fi...  15.2 us
    all_to_all x1, blocking collectives, body(): lax.all_to_all(slots, ('gx', 'gy'), 0, 0, tiled=True, axis_index_groups=g...  8.62 us
    pallas_call x5, Pallas kernels, call(): pl.pallas_call(kernel, out_shape=shapes, in_specs=[HBM if fetch else VMEM...  4.86 us

profile of v7, /device:TPU:1, one launch (start us, length us, event | category | flops | bytes accessed | tf_op | source)
XLA Modules:
  0.0 84.2 jit_solution(1063076715040346649)
XLA Ops:
  0.0 2.0 %shard_map.154 = (f32[3,128,128]{2,1,0:T(8,128)S(1)}, f32[128,128]{1,0:T(8,128)S(1)}, f32[4,64,128]{2,1,0:T(8,128)S(1)}) custom-call(f32[3,8,16,128]{3,2,1,0:T(8,128)} %adj_hbm.1, bf16[3,8,16,128]{3,2,1,0:T(8,128)(2,1)} %flow_hbm.1, bf16[9,8,16,128]{3,2,1,0:T(8,128)(2,1)} %grads_hbm.1, f32[8,16,128]{2,1,0:T(8,128)} %sponge.1, ...), custom_call_target="tpu_custom_call" | custom-call | flops 1000000 | bytes 1384448 | tf_op jit(solution)/shard_map/pallas_call | solution.py:574
  2.0 0.0 copy-start.9
  2.0 0.0 copy-start.10
  2.0 20.1 %all_to_all.32.got = f32[4,64,128]{2,1,0:T(8,128)S(1)} all-to-all(f32[4,64,128]{2,1,0:T(8,128)S(1)} %get-tuple-element.22), channel_id=1, replica_groups={{0,1,128,129},{2,3,130,131},{4,5,132,133},{6,7,134,135},{8,9,136,137},{..., dimensions={0} | all-to-all | bytes 262144 | tf_op jit(solution)/shard_map/all_to_all | solution.py:635
  22.1 0.0 copy-done.9
  22.1 0.5 shard_map.155
  22.6 7.9 %all_to_all.33.got = f32[4,112,128]{2,1,0:T(8,128)S(1)} all-to-all(f32[4,112,128]{2,1,0:T(8,128)S(1)} %get-tuple-element.26), channel_id=1, replica_groups={{129,130,257,258},{131,132,259,260},{133,134,261,262},{135,136,263,264}..., dimensions={0} | all-to-all | bytes 458752 | tf_op jit(solution)/shard_map/all_to_all | solution.py:635
  30.6 0.0 copy-start.8
  30.6 0.4 shard_map.156
  31.0 0.0 copy-start
  31.0 0.0 copy-start.1
  31.0 0.0 copy-start.2
  31.0 0.0 copy-start.3
  31.0 8.6 %all_to_all.34.got = f32[8,64,128]{2,1,0:T(8,128)S(1)} all-to-all(f32[8,64,128]{2,1,0:T(8,128)S(1)} %get-tuple-element.31), channel_id=1, replica_groups={{0,32,64,96,128,160,192,224},{256,288,320,352,384,416,448,480},{512,544..., dimensions={0} | all-to-all | bytes 524288 | tf_op jit(solution)/shard_map/all_to_all | solution.py:659
  39.7 0.0 copy-done.7
  39.7 0.0 copy-done.8
  39.7 0.0 copy-done
  39.7 0.0 copy-done.1
  39.7 0.0 copy-done.2
  39.7 0.0 copy-done.3
  39.7 1.1 %shard_map.157 = (f32[3,128,128]{2,1,0:T(8,128)S(1)}, f32[3,128,128]{2,1,0:T(8,128)S(1)}, f32[16,128]{1,0:T(8,128)S(1)}) custom-call(f32[3,128,128]{2,1,0:T(8,128)S(1)} %get-tuple-element.27.field, f32[128,128]{1,0:T(8,128)S(1)} %get-tuple-element.28.drag_in, f32[3,128,128]{2,1,0:T(8,128)S(1)} %get-tuple-element.29.cross, ...), custom_call_target="tpu_custom_call" | custom-call | flops 1000000 | bytes 2129920 | tf_op jit(solution)/shard_map/pallas_call | solution.py:574
  40.9 15.2 %all_to_all.35 = f32[16,1,128]{2,1,0:T(1,128)S(1)} all-to-all(f32[16,1,128]{2,1,0:T(1,128)S(1)} %bitcast.6), channel_id=1, replica_groups={{0,1,2,3,32,33,34,35,64,65,66,67,96,97,98,99},{4,5,6,7,36,37,38,39,68,6..., dimensions={0} | all-to-all | bytes 16384 | tf_op jit(solution)/shard_map/all_to_all | solution.py:707
  56.1 27.2 %all_to_all.36 = f32[64,1,128]{2,1,0:T(1,128)S(1)} all-to-all(f32[64,1,128]{2,1,0:T(1,128)S(1)} %broadcast_in_dim.2), channel_id=1, replica_groups={{0,4,8,12,16,20,24,28,128,132,136,140,144,148,152,156,256,260,264,268,2..., dimensions={0} | all-to-all | bytes 65536 | tf_op jit(solution)/shard_map/all_to_all | solution.py:712
  83.4 0.8 %shard_map.158 = f32[3,128,128]{2,1,0:T(8,128)} custom-call(f32[3,128,128]{2,1,0:T(8,128)S(1)} %get-tuple-element.32.base, f32[3,128,128]{2,1,0:T(8,128)S(1)} %get-tuple-element.33.image, f32[64,128]{1,0:T(8,128)S(1)} %bitcast.5), custom_call_target="tpu_custom_call" | custom-call | flops 1000000 | bytes 622592 | tf_op jit(solution)/shard_map/pallas_call | solution.py:574
  (10 shorter events, 0.1 us)
Async XLA Ops:
  2.0 20.2 %copy-start.9 = (bf16[24,256]{1,0:T(8,128)(2,1)S(1)}, bf16[24,256]{1,0:T(8,128)(2,1)}, u32[]{:S(2)}) copy-start(bf16[24,256]{1,0:T(8,128)(2,1)} %constant.31.clone.place) | copy-start | bytes 36868
  2.0 20.2 %copy-start.10 = (bf16[16,256]{1,0:T(8,128)(2,1)S(1)}, bf16[16,256]{1,0:T(8,128)(2,1)}, u32[]{:S(2)}) copy-start(bf16[16,256]{1,0:T(8,128)(2,1)} %constant.30.clone.pick_hbm.pick) | copy-start | bytes 24580
  30.5 9.1 %copy-start.4 = (bf16[256,256]{1,0:T(8,128)(2,1)S(1)}, bf16[256,256]{1,0:T(8,128)(2,1)}, u32[]{:S(2)}) copy-start(bf16[256,256]{1,0:T(8,128)(2,1)} %constant.34.clone.plane_own) | copy-start | bytes 393220
  30.6 9.1 %copy-start.5 = (bf16[256,256]{1,0:T(8,128)(2,1)S(1)}, bf16[256,256]{1,0:T(8,128)(2,1)}, u32[]{:S(2)}) copy-start(bf16[256,256]{1,0:T(8,128)(2,1)} %constant.33.clone.line_asm) | copy-start | bytes 393220
  30.6 9.1 %copy-start.6 = (f32[128,128]{1,0:T(8,128)S(1)}, f32[128,128]{1,0:T(8,128)}, u32[]{:S(2)}) copy-start(f32[128,128]{1,0:T(8,128)} %constant.37.clone.plane_weight) | copy-start | bytes 196612
  30.6 9.1 %copy-start.7 = (f32[128,128]{1,0:T(8,128)S(1)}, f32[128,128]{1,0:T(8,128)}, u32[]{:S(2)}) copy-start(f32[128,128]{1,0:T(8,128)} %constant.36.clone.plane_weight_asm) | copy-start | bytes 196612
  30.6 9.1 %copy-start.8 = (f32[128,128]{1,0:T(8,128)S(1)}, f32[128,128]{1,0:T(8,128)}, u32[]{:S(2)}) copy-start(f32[128,128]{1,0:T(8,128)} %constant.27.clone.share) | copy-start | bytes 196612
  31.0 8.7 %copy-start = (bf16[256,512]{1,0:T(8,128)(2,1)S(1)}, bf16[256,512]{1,0:T(8,128)(2,1)}, u32[]{:S(2)}) copy-start(bf16[256,512]{1,0:T(8,128)(2,1)} %constant.32.clone.plane_asm) | copy-start | bytes 786436
  31.0 8.7 %copy-start.1 = (f32[8,16,128]{2,1,0:T(8,128)S(1)}, f32[8,16,128]{2,1,0:T(8,128)}, u32[]{:S(2)}) copy-start(f32[8,16,128]{2,1,0:T(8,128)} %sponge.1) | copy-start | bytes 196612
  31.0 8.7 %copy-start.2 = (f32[128,128]{1,0:T(8,128)S(1)}, f32[128,128]{1,0:T(8,128)}, u32[]{:S(2)}) copy-start(f32[128,128]{1,0:T(8,128)} %constant.26.clone.mass_hbm.mass) | copy-start | bytes 196612
  31.0 8.7 %copy-start.3 = (bf16[256,256]{1,0:T(8,128)(2,1)S(1)}, bf16[256,256]{1,0:T(8,128)(2,1)}, u32[]{:S(2)}) copy-start(bf16[256,256]{1,0:T(8,128)(2,1)} %constant.35.clone.line_own) | copy-start | bytes 393220

commit v8 on v6

--- a/solution.py
+++ b/solution.py
@@ -252,11 +252,11 @@
             (
                 (adj_hbm, adj),
                 (dz_hbm, dz),
+                (grads_hbm, grads),
+                (flow_hbm, flow),
+                (dy_hbm, dy),
+                (sponge_hbm, sponge),
                 (mass_hbm, mass),
-                (sponge_hbm, sponge),
-                (dy_hbm, dy),
-                (flow_hbm, flow),
-                (grads_hbm, grads),
                 (pick_hbm, pick),
             )
         )
@@ -521,15 +521,24 @@
     line_weight = line_pattern(W1, (1, sz))
     line_weight_asm = line_pattern(assembled_weights(NODES), (1, sz))
     total = [jnp.zeros((1, sz), F32) for _ in range(4)]
+    vs = [jnp.where(keep, ext[c, :rows], 0.0) for c in range(3)]
+    wide = jnp.concatenate(
+        [jnp.concatenate([vs[c], ext[c, rows:]], 0) for c in range(3)], 1
+    )
+    planes = mul_left(plane_asm[...], wide)
+    us = []
     for c in range(3):
-        whole = ext[c]
-        v = jnp.where(keep, whole[:rows], 0.0)
-        plane = mul_left(plane_asm[...], jnp.concatenate([v, whole[rows:]], 0))
+        v = vs[c]
         line = mul_right(v, line_asm[...]) + cross[c]
-        stiff = plane * line_weight_asm + line * plane_weight_asm[...]
+        stiff = planes[:, c * sz : (c + 1) * sz] * line_weight_asm
+        stiff = stiff + line * plane_weight_asm[...]
         u = jnp.where(keep, s_asm * v + viscosity * stiff, 0.0)
+        us.append(u)
+    planes = mul_left(plane_own[...], jnp.concatenate(us, 1))
+    for c in range(3):
+        v, u = vs[c], us[c]
         stiff = (
-            mul_left(plane_own[...], u) * line_weight
+            planes[:, c * sz : (c + 1) * sz] * line_weight
             + mul_right(u, line_own[...]) * plane_weight[...]
         )
         own = s_own * u + viscosity * stiff

time: 82.5 us -> 82.1 us (level)
  no operation moved by 1% of the time
where the time goes in v8:
time: 82.1 us; the launch traced here: 81.8 us
  blocking collectives  77 us (94%)
  Pallas kernels  4.53 us (6%)
    all_to_all x2, blocking collectives, exchange(): lax.all_to_all(slots, ('gx', 'gz'), 0, 0, tiled=True, axis_index_groups=g...  28 us
    all_to_all x1, blocking collectives, body(): sums = lax.all_to_all(sums, 'gz', 0, 0, tiled=True)  24.9 us
    all_to_all x1, blocking collectives, body(): sums = lax.all_to_all(sums, ('gx', 'gy'), 0, 0, tiled=True)  15.5 us
    all_to_all x1, blocking collectives, body(): lax.all_to_all(slots, ('gx', 'gy'), 0, 0, tiled=True, axis_index_groups=g...  8.62 us
    pallas_call x5, Pallas kernels, call(): pl.pallas_call(kernel, out_shape=shapes, in_specs=[HBM if fetch else VMEM...  4.53 us

profile of v8, /device:TPU:1, one launch (start us, length us, event | category | flops | bytes accessed | tf_op | source)
XLA Modules:
  0.0 81.8 jit_solution(17372427717789174868)
XLA Ops:
  0.0 1.9 %shard_map.154 = (f32[3,128,128]{2,1,0:T(8,128)S(1)}, f32[128,128]{1,0:T(8,128)S(1)}, f32[4,64,128]{2,1,0:T(8,128)S(1)}) custom-call(f32[3,8,16,128]{3,2,1,0:T(8,128)} %adj_hbm.1, bf16[3,8,16,128]{3,2,1,0:T(8,128)(2,1)} %flow_hbm.1, bf16[9,8,16,128]{3,2,1,0:T(8,128)(2,1)} %grads_hbm.1, f32[8,16,128]{2,1,0:T(8,128)} %sponge.1, ...), custom_call_target="tpu_custom_call" | custom-call | flops 1000000 | bytes 1384448 | tf_op jit(solution)/shard_map/pallas_call | solution.py:583
  1.9 0.0 copy-start.9
  2.0 0.0 copy-start.10
  2.0 20.1 %all_to_all.32.got = f32[4,64,128]{2,1,0:T(8,128)S(1)} all-to-all(f32[4,64,128]{2,1,0:T(8,128)S(1)} %get-tuple-element.22), channel_id=1, replica_groups={{0,1,128,129},{2,3,130,131},{4,5,132,133},{6,7,134,135},{8,9,136,137},{..., dimensions={0} | all-to-all | bytes 262144 | tf_op jit(solution)/shard_map/all_to_all | solution.py:644
  22.1 0.0 copy-done.9
  22.1 0.0 copy-done.10
  22.1 0.5 shard_map.155
  22.6 7.9 %all_to_all.33.got = f32[4,112,128]{2,1,0:T(8,128)S(1)} all-to-all(f32[4,112,128]{2,1,0:T(8,128)S(1)} %get-tuple-element.26), channel_id=1, replica_groups={{129,130,257,258},{131,132,259,260},{133,134,261,262},{135,136,263,264}..., dimensions={0} | all-to-all | bytes 458752 | tf_op jit(solution)/shard_map/all_to_all | solution.py:644
  30.5 0.0 copy-start.8
  30.5 0.4 shard_map.156
  31.0 0.0 copy-start
  31.0 0.0 copy-start.1
  31.0 0.0 copy-start.2
  31.0 0.0 copy-start.3
  31.0 8.6 %all_to_all.34.got = f32[8,64,128]{2,1,0:T(8,128)S(1)} all-to-all(f32[8,64,128]{2,1,0:T(8,128)S(1)} %get-tuple-element.31), channel_id=1, replica_groups={{0,32,64,96,128,160,192,224},{256,288,320,352,384,416,448,480},{512,544..., dimensions={0} | all-to-all | bytes 524288 | tf_op jit(solution)/shard_map/all_to_all | solution.py:668
  39.6 0.0 copy-done.4
  39.6 0.0 copy-done.5
  39.6 0.0 copy-done.6
  39.6 0.0 copy-done.7
  39.7 0.8 %shard_map.157 = (f32[3,128,128]{2,1,0:T(8,128)S(1)}, f32[3,128,128]{2,1,0:T(8,128)S(1)}, f32[32,128]{1,0:T(8,128)S(1)}) custom-call(f32[3,128,128]{2,1,0:T(8,128)S(1)} %get-tuple-element.27.field, f32[128,128]{1,0:T(8,128)S(1)} %get-tuple-element.28.drag_in, f32[3,128,128]{2,1,0:T(8,128)S(1)} %get-tuple-element.29.cross, ...), custom_call_target="tpu_custom_call" | custom-call | flops 1000000 | bytes 2138112 | tf_op jit(solution)/shard_map/pallas_call | solution.py:583
  40.5 24.9 %all_to_all.35 = f32[32,1,128]{2,1,0:T(1,128)S(1)} all-to-all(f32[32,1,128]{2,1,0:T(1,128)S(1)} %bitcast.6), channel_id=1, replica_groups=mesh['gx'=8,'gy'=4,'gz'=32] {'gz'}, dimensions={0} | all-to-all | bytes 32768 | tf_op jit(solution)/shard_map/all_to_all | solution.py:712
  65.4 0.1 reduce_sum.9
  65.5 15.5 %all_to_all.36 = f32[32,1,128]{2,1,0:T(1,128)S(1)} all-to-all(f32[32,1,128]{2,1,0:T(1,128)S(1)} %broadcast_in_dim.2), channel_id=1, replica_groups=mesh['gx'=8,'gy'=4,'gz'=32] {'gx','gy'}, dimensions={0} | all-to-all | bytes 32768 | tf_op jit(solution)/shard_map/all_to_all | solution.py:716
  80.9 0.8 %shard_map.158 = f32[3,128,128]{2,1,0:T(8,128)} custom-call(f32[3,128,128]{2,1,0:T(8,128)S(1)} %get-tuple-element.32.base, f32[3,128,128]{2,1,0:T(8,128)S(1)} %get-tuple-element.33.image, f32[32,128]{1,0:T(8,128)S(1)} %bitcast.5), custom_call_target="tpu_custom_call" | custom-call | flops 1000000 | bytes 606208 | tf_op jit(solution)/shard_map/pallas_call | solution.py:583
  (10 shorter events, 0.0 us)
Async XLA Ops:
  1.9 20.2 %copy-start.9 = (bf16[24,256]{1,0:T(8,128)(2,1)S(1)}, bf16[24,256]{1,0:T(8,128)(2,1)}, u32[]{:S(2)}) copy-start(bf16[24,256]{1,0:T(8,128)(2,1)} %constant.31.clone.place) | copy-start | bytes 36868
  2.0 20.2 %copy-start.10 = (bf16[16,256]{1,0:T(8,128)(2,1)S(1)}, bf16[16,256]{1,0:T(8,128)(2,1)}, u32[]{:S(2)}) copy-start(bf16[16,256]{1,0:T(8,128)(2,1)} %constant.30.clone.pick_hbm.pick) | copy-start | bytes 24580
  30.5 9.1 %copy-start.4 = (bf16[256,256]{1,0:T(8,128)(2,1)S(1)}, bf16[256,256]{1,0:T(8,128)(2,1)}, u32[]{:S(2)}) copy-start(bf16[256,256]{1,0:T(8,128)(2,1)} %constant.34.clone.plane_own) | copy-start | bytes 393220
  30.5 9.1 %copy-start.5 = (bf16[256,256]{1,0:T(8,128)(2,1)S(1)}, bf16[256,256]{1,0:T(8,128)(2,1)}, u32[]{:S(2)}) copy-start(bf16[256,256]{1,0:T(8,128)(2,1)} %constant.33.clone.line_asm) | copy-start | bytes 393220
  30.5 9.1 %copy-start.6 = (f32[128,128]{1,0:T(8,128)S(1)}, f32[128,128]{1,0:T(8,128)}, u32[]{:S(2)}) copy-start(f32[128,128]{1,0:T(8,128)} %constant.37.clone.plane_weight) | copy-start | bytes 196612
  30.5 9.1 %copy-start.7 = (f32[128,128]{1,0:T(8,128)S(1)}, f32[128,128]{1,0:T(8,128)}, u32[]{:S(2)}) copy-start(f32[128,128]{1,0:T(8,128)} %constant.36.clone.plane_weight_asm) | copy-start | bytes 196612
  30.5 9.1 %copy-start.8 = (f32[128,128]{1,0:T(8,128)S(1)}, f32[128,128]{1,0:T(8,128)}, u32[]{:S(2)}) copy-start(f32[128,128]{1,0:T(8,128)} %constant.27.clone.share) | copy-start | bytes 196612
  31.0 8.7 %copy-start = (bf16[256,512]{1,0:T(8,128)(2,1)S(1)}, bf16[256,512]{1,0:T(8,128)(2,1)}, u32[]{:S(2)}) copy-start(bf16[256,512]{1,0:T(8,128)(2,1)} %constant.32.clone.plane_asm) | copy-start | bytes 786436
  31.0 8.7 %copy-start.1 = (f32[8,16,128]{2,1,0:T(8,128)S(1)}, f32[8,16,128]{2,1,0:T(8,128)}, u32[]{:S(2)}) copy-start(f32[8,16,128]{2,1,0:T(8,128)} %sponge.1) | copy-start | bytes 196612
  31.0 8.7 %copy-start.2 = (f32[128,128]{1,0:T(8,128)S(1)}, f32[128,128]{1,0:T(8,128)}, u32[]{:S(2)}) copy-start(f32[128,128]{1,0:T(8,128)} %constant.26.clone.mass_hbm.mass) | copy-start | bytes 196612
  31.0 8.7 %copy-start.3 = (bf16[256,256]{1,0:T(8,128)(2,1)S(1)}, bf16[256,256]{1,0:T(8,128)(2,1)}, u32[]{:S(2)}) copy-start(bf16[256,256]{1,0:T(8,128)(2,1)} %constant.35.clone.line_own) | copy-start | bytes 393220

commit v9 on v8

--- a/solution.py
+++ b/solution.py
@@ -687,7 +687,7 @@
     plane_own = np.kron(K1, np.diag(wy)) + np.kron(
         np.diag(wx), block_diag(K1, sy // NODES)
     )
-    slots = counts["gz"]
+    slots = nx * ny
     base, image, sums = call(
         functools.partial(moments_kernel, counts, sy),
         (
@@ -709,11 +709,10 @@
         [block, block, (slots, sz)],
         scratch=[(3, size, sz), plane],
     )
+    sums = lax.all_to_all(sums, ("gx", "gy"), 0, 0, tiled=True)
+    sums = jnp.sum(sums, axis=0, keepdims=True)
+    sums = jnp.broadcast_to(sums, (nz, sz))
     sums = lax.all_to_all(sums, "gz", 0, 0, tiled=True)
-    sums = jnp.sum(sums, axis=0, keepdims=True)
-    slots = counts["gx"] * counts["gy"]
-    sums = jnp.broadcast_to(sums, (slots, sz))
-    sums = lax.all_to_all(sums, ("gx", "gy"), 0, 0, tiled=True)
     (out,) = call(combine_kernel, (base, image, sums), [(3, rows, sz)])
     return out.reshape(3, sx, sy, sz)
 

time: 82.1 us -> 83.6 us (1.018)
  blocking collectives: 77 us -> 78.4 us
    all_to_all x1, blocking collectives: 24.9 us -> 29.4 us  [body(): sums = lax.all_to_all(sums, 'gz', 0, 0, tiled=True)]
    all_to_all x1, blocking collectives: 15.5 us -> 12.4 us  [body(): sums = lax.all_to_all(sums, ('gx', 'gy'), 0, 0, tiled=True)]
where the time goes in v9:
time: 83.6 us; the launch traced here: 83.2 us
  blocking collectives  78.4 us (94%)
  Pallas kernels  4.53 us (5%)
    all_to_all x1, blocking collectives, body(): sums = lax.all_to_all(sums, 'gz', 0, 0, tiled=True)  29.4 us
    all_to_all x2, blocking collectives, exchange(): lax.all_to_all(slots, ('gx', 'gz'), 0, 0, tiled=True, axis_index_groups=g...  28 us
    all_to_all x1, blocking collectives, body(): sums = lax.all_to_all(sums, ('gx', 'gy'), 0, 0, tiled=True)  12.4 us
    all_to_all x1, blocking collectives, body(): lax.all_to_all(slots, ('gx', 'gy'), 0, 0, tiled=True, axis_index_groups=g...  8.62 us
    pallas_call x5, Pallas kernels, call(): pl.pallas_call(kernel, out_shape=shapes, in_specs=[HBM if fetch else VMEM...  4.53 us

profile of v9, /device:TPU:1, one launch (start us, length us, event | category | flops | bytes accessed | tf_op | source)
XLA Modules:
  0.0 83.2 jit_solution(4233792810979586022)
XLA Ops:
  0.0 1.9 %shard_map.154 = (f32[3,128,128]{2,1,0:T(8,128)S(1)}, f32[128,128]{1,0:T(8,128)S(1)}, f32[4,64,128]{2,1,0:T(8,128)S(1)}) custom-call(f32[3,8,16,128]{3,2,1,0:T(8,128)} %adj_hbm.1, bf16[3,8,16,128]{3,2,1,0:T(8,128)(2,1)} %flow_hbm.1, bf16[9,8,16,128]{3,2,1,0:T(8,128)(2,1)} %grads_hbm.1, f32[8,16,128]{2,1,0:T(8,128)} %sponge.1, ...), custom_call_target="tpu_custom_call" | custom-call | flops 1000000 | bytes 1384448 | tf_op jit(solution)/shard_map/pallas_call | solution.py:583
  1.9 0.0 copy-start.9
  2.0 0.0 copy-start.10
  2.0 20.1 %all_to_all.32.got = f32[4,64,128]{2,1,0:T(8,128)S(1)} all-to-all(f32[4,64,128]{2,1,0:T(8,128)S(1)} %get-tuple-element.22), channel_id=1, replica_groups={{0,1,128,129},{2,3,130,131},{4,5,132,133},{6,7,134,135},{8,9,136,137},{..., dimensions={0} | all-to-all | bytes 262144 | tf_op jit(solution)/shard_map/all_to_all | solution.py:644
  22.1 0.0 copy-done.9
  22.1 0.0 copy-done.10
  22.1 0.5 shard_map.155
  22.6 7.9 %all_to_all.33.got = f32[4,112,128]{2,1,0:T(8,128)S(1)} all-to-all(f32[4,112,128]{2,1,0:T(8,128)S(1)} %get-tuple-element.26), channel_id=1, replica_groups={{129,130,257,258},{131,132,259,260},{133,134,261,262},{135,136,263,264}..., dimensions={0} | all-to-all | bytes 458752 | tf_op jit(solution)/shard_map/all_to_all | solution.py:644
  30.5 0.0 copy-start.8
  30.5 0.4 shard_map.156
  31.0 0.0 copy-start
  31.0 0.0 copy-start.1
  31.0 0.0 copy-start.2
  31.0 0.0 copy-start.3
  31.0 8.6 %all_to_all.34.got = f32[8,64,128]{2,1,0:T(8,128)S(1)} all-to-all(f32[8,64,128]{2,1,0:T(8,128)S(1)} %get-tuple-element.31), channel_id=1, replica_groups={{0,32,64,96,128,160,192,224},{256,288,320,352,384,416,448,480},{512,544..., dimensions={0} | all-to-all | bytes 524288 | tf_op jit(solution)/shard_map/all_to_all | solution.py:668
  39.6 0.0 copy-done.4
  39.6 0.0 copy-done.5
  39.6 0.0 copy-done.6
  39.6 0.0 copy-done.7
  39.7 0.8 %shard_map.157 = (f32[3,128,128]{2,1,0:T(8,128)S(1)}, f32[3,128,128]{2,1,0:T(8,128)S(1)}, f32[32,128]{1,0:T(8,128)S(1)}) custom-call(f32[3,128,128]{2,1,0:T(8,128)S(1)} %get-tuple-element.27.field, f32[128,128]{1,0:T(8,128)S(1)} %get-tuple-element.28.drag_in, f32[3,128,128]{2,1,0:T(8,128)S(1)} %get-tuple-element.29.cross, ...), custom_call_target="tpu_custom_call" | custom-call | flops 1000000 | bytes 2138112 | tf_op jit(solution)/shard_map/pallas_call | solution.py:583
  40.5 12.4 %all_to_all.35 = f32[32,1,128]{2,1,0:T(1,128)S(1)} all-to-all(f32[32,1,128]{2,1,0:T(1,128)S(1)} %bitcast.6), channel_id=1, replica_groups=mesh['gx'=8,'gy'=4,'gz'=32] {'gx','gy'}, dimensions={0} | all-to-all | bytes 32768 | tf_op jit(solution)/shard_map/all_to_all | solution.py:712
  52.9 0.1 reduce_sum.9
  53.0 29.4 %all_to_all.36 = f32[32,1,128]{2,1,0:T(1,128)S(1)} all-to-all(f32[32,1,128]{2,1,0:T(1,128)S(1)} %broadcast_in_dim.2), channel_id=1, replica_groups=mesh['gx'=8,'gy'=4,'gz'=32] {'gz'}, dimensions={0} | all-to-all | bytes 32768 | tf_op jit(solution)/shard_map/all_to_all | solution.py:715
  82.4 0.8 %shard_map.158 = f32[3,128,128]{2,1,0:T(8,128)} custom-call(f32[3,128,128]{2,1,0:T(8,128)S(1)} %get-tuple-element.32.base, f32[3,128,128]{2,1,0:T(8,128)S(1)} %get-tuple-element.33.image, f32[32,128]{1,0:T(8,128)S(1)} %bitcast.5), custom_call_target="tpu_custom_call" | custom-call | flops 1000000 | bytes 606208 | tf_op jit(solution)/shard_map/pallas_call | solution.py:583
  (10 shorter events, 0.0 us)
Async XLA Ops:
  1.9 20.2 %copy-start.9 = (bf16[24,256]{1,0:T(8,128)(2,1)S(1)}, bf16[24,256]{1,0:T(8,128)(2,1)}, u32[]{:S(2)}) copy-start(bf16[24,256]{1,0:T(8,128)(2,1)} %constant.31.clone.place) | copy-start | bytes 36868
  2.0 20.2 %copy-start.10 = (bf16[16,256]{1,0:T(8,128)(2,1)S(1)}, bf16[16,256]{1,0:T(8,128)(2,1)}, u32[]{:S(2)}) copy-start(bf16[16,256]{1,0:T(8,128)(2,1)} %constant.30.clone.pick_hbm.pick) | copy-start | bytes 24580
  30.5 9.1 %copy-start.4 = (bf16[256,256]{1,0:T(8,128)(2,1)S(1)}, bf16[256,256]{1,0:T(8,128)(2,1)}, u32[]{:S(2)}) copy-start(bf16[256,256]{1,0:T(8,128)(2,1)} %constant.34.clone.plane_own) | copy-start | bytes 393220
  30.5 9.1 %copy-start.5 = (bf16[256,256]{1,0:T(8,128)(2,1)S(1)}, bf16[256,256]{1,0:T(8,128)(2,1)}, u32[]{:S(2)}) copy-start(bf16[256,256]{1,0:T(8,128)(2,1)} %constant.33.clone.line_asm) | copy-start | bytes 393220
  30.5 9.1 %copy-start.6 = (f32[128,128]{1,0:T(8,128)S(1)}, f32[128,128]{1,0:T(8,128)}, u32[]{:S(2)}) copy-start(f32[128,128]{1,0:T(8,128)} %constant.37.clone.plane_weight) | copy-start | bytes 196612
  30.5 9.1 %copy-start.7 = (f32[128,128]{1,0:T(8,128)S(1)}, f32[128,128]{1,0:T(8,128)}, u32[]{:S(2)}) copy-start(f32[128,128]{1,0:T(8,128)} %constant.36.clone.plane_weight_asm) | copy-start | bytes 196612
  30.5 9.1 %copy-start.8 = (f32[128,128]{1,0:T(8,128)S(1)}, f32[128,128]{1,0:T(8,128)}, u32[]{:S(2)}) copy-start(f32[128,128]{1,0:T(8,128)} %constant.27.clone.share) | copy-start | bytes 196612
  31.0 8.7 %copy-start = (bf16[256,512]{1,0:T(8,128)(2,1)S(1)}, bf16[256,512]{1,0:T(8,128)(2,1)}, u32[]{:S(2)}) copy-start(bf16[256,512]{1,0:T(8,128)(2,1)} %constant.32.clone.plane_asm) | copy-start | bytes 786436
  31.0 8.7 %copy-start.1 = (f32[8,16,128]{2,1,0:T(8,128)S(1)}, f32[8,16,128]{2,1,0:T(8,128)}, u32[]{:S(2)}) copy-start(f32[8,16,128]{2,1,0:T(8,128)} %sponge.1) | copy-start | bytes 196612
  31.0 8.7 %copy-start.2 = (f32[128,128]{1,0:T(8,128)S(1)}, f32[128,128]{1,0:T(8,128)}, u32[]{:S(2)}) copy-start(f32[128,128]{1,0:T(8,128)} %constant.26.clone.mass_hbm.mass) | copy-start | bytes 196612
  31.0 8.7 %copy-start.3 = (bf16[256,256]{1,0:T(8,128)(2,1)S(1)}, bf16[256,256]{1,0:T(8,128)(2,1)}, u32[]{:S(2)}) copy-start(bf16[256,256]{1,0:T(8,128)(2,1)} %constant.35.clone.line_own) | copy-start | bytes 393220

commit v10 on v8

--- a/solution.py
+++ b/solution.py
@@ -404,6 +404,7 @@
     beside_above = (1 - mx) * ny + jnp.minimum(j + 1, ny - 1)
     beside_below = (1 - mx) * ny + jnp.maximum(j - 1, 0)
     top, bottom = sy - 1, 0
+    side = lax.broadcasted_iota(jnp.int32, (sx, sz), 0) == jnp.where(x_high, 0, sx - 1)
     for c in range(3):
         field_out[c] = blocks[c]
         cross_out[c] = cross[c] + add[c]
@@ -424,12 +425,12 @@
         down = row(cross_out, bottom)
         for k in range(1, 8):
             down = down + float(K1[0, k]) * row(field_out, k)
+        up = up + jnp.where(side, bend[top:], 0.0)
+        down = down + jnp.where(side, bend[:1], 0.0)
         slots[above, c * 16 : c * 16 + 8] = row(field_out, top)
         slots[above, c * 16 + 8 : c * 16 + 16] = up
-        slots[above, 56 + c : 57 + c] = bend[top:]
         slots[below, c * 16 : c * 16 + 8] = row(field_out, bottom)
         slots[below, c * 16 + 8 : c * 16 + 16] = down
-        slots[below, 56 + c : 57 + c] = bend[:1]
     slots[above, 48:56] = drag_out[pl.ds(top, sx, stride=sy), :]
     slots[below, 48:56] = drag_out[pl.ds(bottom, sx, stride=sy), :]
 
@@ -505,9 +506,7 @@
         ext[c, :rows] = field[c]
         ext[c, bottom, :] = field[c, bottom, :] + low[at : at + 8]
         ext[c, top, :] = field[c, top, :] + high[at : at + 8]
-        odd = bend_odd[c] + jnp.concatenate(
-            [low[56 + c : 57 + c], gap, high[56 + c : 57 + c]], 0
-        )
+        odd = bend_odd[c]
         even = got[(1 - mx) * ny + j, c * sy : (c + 1) * sy] + jnp.concatenate(
             [beside_low[c : c + 1], gap, beside_high[c : c + 1]], 0
         )
@@ -662,7 +661,7 @@
     field, drag, cross, bend, slots = call(
         functools.partial(third_kernel, nx, ny, nz),
         (field, drag, cross, got, place),
-        [block, plane, block, (3, sy, sz), (2 * ny, 64, sz)],
+        [block, plane, block, (3, sy, sz), (2 * ny, 56, sz)],
     )
     every = [tuple(range(ny))]
     got = lax.all_to_all(

time: 82.1 us -> 82 us (level)
  no operation moved by 1% of the time
where the time goes in v10:
time: 82 us; the launch traced here: 81.6 us
  blocking collectives  76.8 us (94%)
  Pallas kernels  4.55 us (6%)
    all_to_all x2, blocking collectives, exchange(): lax.all_to_all(slots, ('gx', 'gz'), 0, 0, tiled=True, axis_index_groups=g...  28 us
    all_to_all x1, blocking collectives, body(): sums = lax.all_to_all(sums, 'gz', 0, 0, tiled=True)  24.9 us
    all_to_all x1, blocking collectives, body(): sums = lax.all_to_all(sums, ('gx', 'gy'), 0, 0, tiled=True)  15.4 us
    all_to_all x1, blocking collectives, body(): lax.all_to_all(slots, ('gx', 'gy'), 0, 0, tiled=True, axis_index_groups=g...  8.48 us
    pallas_call x5, Pallas kernels, call(): pl.pallas_call(kernel, out_shape=shapes, in_specs=[HBM if fetch else VMEM...  4.55 us

profile of v10, /device:TPU:1, one launch (start us, length us, event | category | flops | bytes accessed | tf_op | source)
XLA Modules:
  0.0 81.6 jit_solution(2926823465107060334)
XLA Ops:
  0.0 1.9 %shard_map.154 = (f32[3,128,128]{2,1,0:T(8,128)S(1)}, f32[128,128]{1,0:T(8,128)S(1)}, f32[4,64,128]{2,1,0:T(8,128)S(1)}) custom-call(f32[3,8,16,128]{3,2,1,0:T(8,128)} %adj_hbm.1, bf16[3,8,16,128]{3,2,1,0:T(8,128)(2,1)} %flow_hbm.1, bf16[9,8,16,128]{3,2,1,0:T(8,128)(2,1)} %grads_hbm.1, f32[8,16,128]{2,1,0:T(8,128)} %sponge.1, ...), custom_call_target="tpu_custom_call" | custom-call | flops 1000000 | bytes 1384448 | tf_op jit(solution)/shard_map/pallas_call | solution.py:582
  1.9 0.0 copy-start.9
  2.0 0.0 copy-start.10
  2.0 20.1 %all_to_all.32.got = f32[4,64,128]{2,1,0:T(8,128)S(1)} all-to-all(f32[4,64,128]{2,1,0:T(8,128)S(1)} %get-tuple-element.22), channel_id=1, replica_groups={{0,1,128,129},{2,3,130,131},{4,5,132,133},{6,7,134,135},{8,9,136,137},{..., dimensions={0} | all-to-all | bytes 262144 | tf_op jit(solution)/shard_map/all_to_all | solution.py:643
  22.1 0.0 copy-done.9
  22.1 0.0 copy-done.10
  22.1 0.5 shard_map.155
  22.6 7.9 %all_to_all.33.got = f32[4,112,128]{2,1,0:T(8,128)S(1)} all-to-all(f32[4,112,128]{2,1,0:T(8,128)S(1)} %get-tuple-element.26), channel_id=1, replica_groups={{129,130,257,258},{131,132,259,260},{133,134,261,262},{135,136,263,264}..., dimensions={0} | all-to-all | bytes 458752 | tf_op jit(solution)/shard_map/all_to_all | solution.py:643
  30.5 0.0 copy-start.8
  30.5 0.4 shard_map.156
  31.0 0.0 copy-start
  31.0 0.0 copy-start.1
  31.0 0.0 copy-start.2
  31.0 0.0 copy-start.6
  31.0 8.5 %all_to_all.34.got = f32[8,56,128]{2,1,0:T(8,128)S(1)} all-to-all(f32[8,56,128]{2,1,0:T(8,128)S(1)} %get-tuple-element.31), channel_id=1, replica_groups={{0,32,64,96,128,160,192,224},{256,288,320,352,384,416,448,480},{512,544..., dimensions={0} | all-to-all | bytes 458752 | tf_op jit(solution)/shard_map/all_to_all | solution.py:667
  39.5 0.0 copy-done.3
  39.5 0.0 copy-done.4
  39.5 0.0 copy-done.5
  39.5 0.0 copy-done.7
  39.6 0.8 %shard_map.157 = (f32[3,128,128]{2,1,0:T(8,128)S(1)}, f32[3,128,128]{2,1,0:T(8,128)S(1)}, f32[32,128]{1,0:T(8,128)S(1)}) custom-call(f32[3,128,128]{2,1,0:T(8,128)S(1)} %get-tuple-element.27.field, f32[128,128]{1,0:T(8,128)S(1)} %get-tuple-element.28.drag_in, f32[3,128,128]{2,1,0:T(8,128)S(1)} %get-tuple-element.29.cross, ...), custom_call_target="tpu_custom_call" | custom-call | flops 1000000 | bytes 2105344 | tf_op jit(solution)/shard_map/pallas_call | solution.py:582
  40.4 24.9 %all_to_all.35 = f32[32,1,128]{2,1,0:T(1,128)S(1)} all-to-all(f32[32,1,128]{2,1,0:T(1,128)S(1)} %bitcast.6), channel_id=1, replica_groups=mesh['gx'=8,'gy'=4,'gz'=32] {'gz'}, dimensions={0} | all-to-all | bytes 32768 | tf_op jit(solution)/shard_map/all_to_all | solution.py:711
  65.3 0.1 reduce_sum.9
  65.4 15.4 %all_to_all.36 = f32[32,1,128]{2,1,0:T(1,128)S(1)} all-to-all(f32[32,1,128]{2,1,0:T(1,128)S(1)} %broadcast_in_dim.2), channel_id=1, replica_groups=mesh['gx'=8,'gy'=4,'gz'=32] {'gx','gy'}, dimensions={0} | all-to-all | bytes 32768 | tf_op jit(solution)/shard_map/all_to_all | solution.py:715
  80.8 0.8 %shard_map.158 = f32[3,128,128]{2,1,0:T(8,128)} custom-call(f32[3,128,128]{2,1,0:T(8,128)S(1)} %get-tuple-element.32.base, f32[3,128,128]{2,1,0:T(8,128)S(1)} %get-tuple-element.33.image, f32[32,128]{1,0:T(8,128)S(1)} %bitcast.5), custom_call_target="tpu_custom_call" | custom-call | flops 1000000 | bytes 606208 | tf_op jit(solution)/shard_map/pallas_call | solution.py:582
  (10 shorter events, 0.0 us)
Async XLA Ops:
  1.9 20.2 %copy-start.9 = (bf16[24,256]{1,0:T(8,128)(2,1)S(1)}, bf16[24,256]{1,0:T(8,128)(2,1)}, u32[]{:S(2)}) copy-start(bf16[24,256]{1,0:T(8,128)(2,1)} %constant.31.clone.place) | copy-start | bytes 36868
  2.0 20.2 %copy-start.10 = (bf16[16,256]{1,0:T(8,128)(2,1)S(1)}, bf16[16,256]{1,0:T(8,128)(2,1)}, u32[]{:S(2)}) copy-start(bf16[16,256]{1,0:T(8,128)(2,1)} %constant.30.clone.pick_hbm.pick) | copy-start | bytes 24580
  30.5 9.0 %copy-start.3 = (bf16[256,256]{1,0:T(8,128)(2,1)S(1)}, bf16[256,256]{1,0:T(8,128)(2,1)}, u32[]{:S(2)}) copy-start(bf16[256,256]{1,0:T(8,128)(2,1)} %constant.35.clone.line_own) | copy-start | bytes 393220
  30.5 9.0 %copy-start.4 = (bf16[256,256]{1,0:T(8,128)(2,1)S(1)}, bf16[256,256]{1,0:T(8,128)(2,1)}, u32[]{:S(2)}) copy-start(bf16[256,256]{1,0:T(8,128)(2,1)} %constant.34.clone.plane_own) | copy-start | bytes 393220
  30.5 9.0 %copy-start.5 = (bf16[256,256]{1,0:T(8,128)(2,1)S(1)}, bf16[256,256]{1,0:T(8,128)(2,1)}, u32[]{:S(2)}) copy-start(bf16[256,256]{1,0:T(8,128)(2,1)} %constant.33.clone.line_asm) | copy-start | bytes 393220
  30.5 9.0 %copy-start.7 = (f32[128,128]{1,0:T(8,128)S(1)}, f32[128,128]{1,0:T(8,128)}, u32[]{:S(2)}) copy-start(f32[128,128]{1,0:T(8,128)} %constant.36.clone.plane_weight_asm) | copy-start | bytes 196612
  30.5 9.0 %copy-start.8 = (f32[128,128]{1,0:T(8,128)S(1)}, f32[128,128]{1,0:T(8,128)}, u32[]{:S(2)}) copy-start(f32[128,128]{1,0:T(8,128)} %constant.27.clone.share) | copy-start | bytes 196612
  31.0 8.6 %copy-start = (bf16[256,512]{1,0:T(8,128)(2,1)S(1)}, bf16[256,512]{1,0:T(8,128)(2,1)}, u32[]{:S(2)}) copy-start(bf16[256,512]{1,0:T(8,128)(2,1)} %constant.32.clone.plane_asm) | copy-start | bytes 786436
  31.0 8.6 %copy-start.1 = (f32[8,16,128]{2,1,0:T(8,128)S(1)}, f32[8,16,128]{2,1,0:T(8,128)}, u32[]{:S(2)}) copy-start(f32[8,16,128]{2,1,0:T(8,128)} %sponge.1) | copy-start | bytes 196612
  31.0 8.6 %copy-start.2 = (f32[128,128]{1,0:T(8,128)S(1)}, f32[128,128]{1,0:T(8,128)}, u32[]{:S(2)}) copy-start(f32[128,128]{1,0:T(8,128)} %constant.26.clone.mass_hbm.mass) | copy-start | bytes 196612
  31.0 8.6 %copy-start.6 = (f32[128,128]{1,0:T(8,128)S(1)}, f32[128,128]{1,0:T(8,128)}, u32[]{:S(2)}) copy-start(f32[128,128]{1,0:T(8,128)} %constant.37.clone.plane_weight) | copy-start | bytes 196612
